TPU v7x, 32 devices: a whole 2x2x4 slice. The times are simulated.
32 devices in a mesh: tm: 8 (over z, x), space: 4 (over y, core).
Axes of the slice: x: 2, y: 2, z: 4, core: 2. Of those that a mesh axis runs over, the one named last changes fastest.
Arguments:
- snapshots: float32 [4224, 4096], P('tm', 'space')
- starts: int32 [32], replicated, may hold values from 0 to 3968, as said below
- freq_lines: int32 [128], replicated, may hold values from 0 to 128, as said below
Outputs:
- power_density: float32 [128, 4096], P(None, ('space', 'tm'))
- gram_matrices: float32 [2, 128, 32, 32], P(None, 'tm')
Inputs may be any that keep to these rules, and one draw needn't show every extreme that they name: starts never fall, and block b starts at most 64 snapshots away from b * 128; the first block starts at 0 and the last at 3968. `freq_lines`: distinct line numbers in any order; 0 and 128 are among them.
All inputs are finite; a program needn't handle non-finite values.
Results may differ from a plain program's by a relative error of at most 0.0001.
Values sent between devices are 32-bit elements; how exact they have to be, the bound alone decides.
No kernel may reach another device: no remote copies, remote signals or barrier semaphores. Data moves between devices by JAX's collectives and lax.ppermute only.
A program may use at most 64 MiB of HBM per device.

v0:
```python
import math

import jax
import jax.numpy as jnp
from jax import lax
from jax.sharding import PartitionSpec as P

NFFT = 256
NF = 128
NB = 32


def spectral_table(freq_lines):
    moments = jnp.arange(NFFT, dtype=jnp.int32)
    cycle = freq_lines[:, None] * moments[None, :] % NFFT
    angles = 2.0 * math.pi / NFFT * cycle.astype(jnp.float32)
    window = 0.5 - 0.5 * jnp.cos(2.0 * math.pi / NFFT * moments.astype(jnp.float32))
    window = window / jnp.sqrt(jnp.sum(window * window))
    return jnp.concatenate(
        [window[None, :] * jnp.cos(angles), -window[None, :] * jnp.sin(angles)], axis=0
    )


def block_spectra(series, starts, table):
    offsets = starts[:, None] + jnp.arange(NFFT, dtype=jnp.int32)[None, :]
    blocks = series[offsets]
    return jnp.einsum("kt,btp->kbp", table, blocks, precision=lax.Precision.HIGHEST)


def local_terms(spectra, factor):
    highest = lax.Precision.HIGHEST
    real_part = spectra[:NF]
    imag_part = spectra[NF:]
    power = jnp.sum(real_part * real_part + imag_part * imag_part, axis=1) / NB
    gram_real = jnp.einsum("fbp,fcp->fbc", real_part, real_part, precision=highest) + jnp.einsum(
        "fbp,fcp->fbc", imag_part, imag_part, precision=highest
    )
    gram_imag = jnp.einsum("fbp,fcp->fbc", real_part, imag_part, precision=highest) - jnp.einsum(
        "fbp,fcp->fbc", imag_part, real_part, precision=highest
    )
    return (power, jnp.stack([gram_real, gram_imag]) * factor)


def body(snapshots, starts, freq_lines):
    groups = lax.axis_size("tm")
    columns = snapshots.shape[1] // groups
    table = spectral_table(freq_lines)
    arranged = snapshots.reshape(snapshots.shape[0], groups, columns)
    spectra = block_spectra(
        lax.all_to_all(arranged, "tm", split_axis=1, concat_axis=0, tiled=True)[:, 0, :],
        starts,
        table,
    )
    total_points = columns * groups * lax.axis_size("space")
    power_density, own_gram = local_terms(spectra, 1.0 / (NB * total_points))
    per_device = NF // groups
    summed = lax.psum(own_gram, ("tm", "space"))
    gram_matrices = lax.dynamic_slice_in_dim(
        summed, lax.axis_index("tm") * per_device, per_device, 1
    )
    return (power_density, gram_matrices)


def solution(mesh):
    placed = (P("tm", "space"), P(), P())
    return jax.shard_map(
        body,
        mesh=mesh,
        in_specs=placed,
        out_specs=(P(None, ("space", "tm")), P(None, "tm", None, None)),
        check_vma=False,
    )
```

profile of v0, /device:TPU:0, one launch (start us, length us, event | category | flops | bytes accessed | tf_op | source)
XLA Modules:
  0.0 276.6 jit_solution(2760193698736418181)
XLA Ops:
  7.2 0.0 copy-start
  7.2 1.6 copy-done
  8.8 1.5 copy_bitcast_fusion
  10.3 0.0 copy-start.2
  10.3 0.0 copy-start.3
  10.3 7.4 %all-to-all-start = ((f32[528,8,128]{2,0,1:T(8,128)}), f32[528,8,128]{2,0,1:T(8,128)}, u32[]{:S(2)}, u32[]{:S(2)}) async-start(f32[528,8,128]{2,0,1:T(8,128)} %copy_bitcast_fusion), calls=%async_computation | async-start | bytes 4325376 | tf_op jit(solution)/shard_map/all_to_all | solution.py:50
  17.7 0.0 all-reduce.2.cloned.1.call-start
  17.7 0.6 multiply_reduce_fusion
  19.1 0.0 copy-done.2
  19.1 0.1 fusion.25
  19.2 0.0 copy-done.3
  19.2 0.6 cosine_multiply_fusion
  19.9 47.6 %all-to-all-done = f32[528,8,128]{2,0,1:T(8,128)} async-done(((f32[528,8,128]{2,0,1:T(8,128)}), f32[528,8,128]{2,0,1:T(8,128)}, u32[]{:S(2)}, u32[]{:S(2)}) %all-to-all-start) | async-done | bytes 2162720 | tf_op jit(solution)/shard_map/all_to_all | solution.py:50
  67.4 29.4 %gather_fusion = f32[8192,128]{1,0:T(8,128)} fusion(f32[4224,128]{1,0:T(8,128)} %bitcast.3, s32[8192]{0:T(1024)S(1)} %broadcast_clamp_fusion), kind=kCustom, calls=%fused_computation | custom fusion | bytes 8421376 | tf_op jit(solution)/shard_map/gather | solution.py:26
  96.8 5.6 %fusion.16 = f32[256,32,128]{2,0,1:T(8,128)S(1)} fusion(f32[32,256,128]{2,1,0:T(8,128)} %bitcast.23, f32[128,256]{1,0:T(8,128)S(1)} %get-tuple-element.8, f32[128,256]{1,0:T(8,128)S(1)} %get-tuple-element.7), kind=kOutput, calls=%fused_computation.17 | convolution fusion | flops 3221291008 | bytes 8650752 | tf_op jit(solution)/shard_map/kt,btp->kbp/dot_general | solution.py:27
  102.4 0.7 fusion.29
  103.1 0.0 copy-start.1
  103.1 5.7 %fusion.4 = f32[128,32,32]{2,1,0:T(8,128)} fusion(f32[128,32,128]{2,0,1:T(8,128)S(1)} %get-tuple-element.6), kind=kOutput, calls=%fused_computation.9 | convolution fusion | flops 201326592 | bytes 2621440 | tf_op jit(solution)/shard_map/fbp,fcp->fbc/dot_general | solution.py:35
  108.8 5.7 %fusion = f32[128,32,32]{2,1,0:T(8,128)S(1)} fusion(f32[128,32,128]{2,0,1:T(8,128)S(1)} %get-tuple-element.6, f32[128,32,128]{2,0,1:T(8,128)S(1)} %get-tuple-element.4), kind=kOutput, calls=%fused_computation.5 | convolution fusion | flops 201326592 | bytes 4718592 | tf_op jit(solution)/shard_map/fbp,fcp->fbc/dot_general | solution.py:38
  114.5 0.0 copy-done.1
  114.5 7.2 %subtract_bitcast_fusion = f32[1,128,32,32]{3,2,1,0:T(8,128)} fusion(f32[128,32,32]{2,1,0:T(8,128)S(1)} %fusion, f32[128,32,128]{2,0,1:T(8,128)S(1)} %get-tuple-element.6, f32[128,32,128]{2,0,1:T(8,128)S(1)} %get-tuple-element.4), kind=kOutput, calls=%fused_computation.2 | convolution fusion | flops 201457664 | bytes 5242880 | tf_op jit(solution)/shard_map/fbp,fcp->fbc/dot_general | solution.py:38
  121.7 2.7 copy.33
  124.3 9.7 %add_bitcast_fusion = f32[1,128,32,32]{3,2,1,0:T(8,128)} fusion(f32[128,32,32]{2,1,0:T(8,128)} %fusion.4, f32[128,32,128]{2,0,1:T(8,128)} %copy-done.1), kind=kOutput, calls=%fused_computation.3 | convolution fusion | flops 201457664 | bytes 3145728 | tf_op jit(solution)/shard_map/fbp,fcp->fbc/dot_general | solution.py:35
  134.1 2.7 copy.32
  136.7 1.1 maximum_multiply_fusion
  137.8 0.0 all-reduce.2.cloned.1.call-update
  137.9 0.6 broadcast_multiply_fusion
  138.5 128.4 %all-reduce.2.cloned.1.call-done = f32[2,128,32,32]{1,3,2,0:T(8,128)} async-done(((f32[2,128,32,32]{1,3,2,0:T(8,128)}), f32[2,128,32,32]{1,3,2,0:T(8,128)}) %all-reduce.2.cloned.1.call-update) | async-done | bytes 1048592 | tf_op jit(solution)/shard_map/psum | solution.py:57
  266.9 1.6 constant_dynamic-slice_fusion
  268.5 1.2 copy.34
  (3 shorter events, 0.1 us)
Async XLA Ops:
  7.2 1.6 copy-start
  10.3 8.8 %copy-start.2 = (s32[32]{0:T(128)S(1)}, s32[32]{0:T(128)}, u32[]{:S(2)}) copy-start(s32[32]{0:T(128)} %param.4) | copy-start | bytes 388
  10.3 9.0 %copy-start.3 = (s32[128]{0:T(128)S(1)}, s32[128]{0:T(128)}, u32[]{:S(2)}) copy-start(s32[128]{0:T(128)} %param.5) | copy-start | bytes 1540
  10.3 57.1 %all-to-all-start = ((f32[528,8,128]{2,0,1:T(8,128)}), f32[528,8,128]{2,0,1:T(8,128)}, u32[]{:S(2)}, u32[]{:S(2)}) async-start(f32[528,8,128]{2,0,1:T(8,128)} %copy_bitcast_fusion), calls=%async_computation | async-start | bytes 4325376 | tf_op jit(solution)/shard_map/all_to_all | solution.py:50
  17.7 249.3 %all-reduce.2.cloned.1.call-start = ((), (), s32[]{:S(2)}) async-start(), calls=%async_computation.1 | async-start | bytes 2097152 | tf_op jit(solution)/shard_map/psum | solution.py:57
  103.1 11.4 %copy-start.1 = (f32[128,32,128]{2,0,1:T(8,128)}, f32[128,32,128]{2,0,1:T(8,128)S(1)}, u32[]{:S(2)}) copy-start(f32[128,32,128]{2,0,1:T(8,128)S(1)} %get-tuple-element.4) | copy-start | bytes 6291460
Sparse Core Ops, SparseCore 0:
  138.0 128.9 all-reduce.1
where the time goes:
time: 277 us
  waiting for transfers between devices  176 us (64%)
  local copies, waits for them, and re-layouts  40.6 us (15%)
  matrix products  33.9 us (12%)
  between operations  14.8 us (5%)
  starting transfers between devices  7.42 us (3%)
  other arithmetic  3.87 us (1%)
    psum x1, waiting for transfers between devices, body(): summed = lax.psum(own_gram, ('tm', 'space'))  128 us
    all_to_all x1, waiting for transfers between devices, body(): lax.all_to_all(arranged, 'tm', split_axis=1, concat_axis=0, tiled=True)  47.6 us
    gather x1, local copies, waits for them, and re-layouts, block_spectra(): blocks = series[offsets]  29.4 us
    dot_general x1, matrix products, local_terms(): jnp.einsum('fbp,fcp->fbc', real_part, real_part, precision=highest)  9.72 us
    all_to_all x1, starting transfers between devices, body(): lax.all_to_all(arranged, 'tm', split_axis=1, concat_axis=0, tiled=True)  7.38 us
    dot_general x1, matrix products, local_terms(): jnp.einsum('fbp,fcp->fbc', real_part, imag_part, precision=highest)  7.21 us
    dot_general x1, matrix products, local_terms(): jnp.einsum('fbp,fcp->fbc', imag_part, imag_part, precision=highest)  5.68 us
    dot_general x1, matrix products, local_terms(): jnp.einsum('fbp,fcp->fbc', imag_part, real_part, precision=highest)  5.67 us
  transfers between devices with their start and end apart: 2, of which 2 were waited for; matrix products, arithmetic and copies ran while one was open for 1% of the time, Pallas kernels for 0%

commit v1 on v0

v1 whole, which is shorter than its diff:
```python
import functools
import math

import jax
import jax.numpy as jnp
from jax import lax
from jax.experimental import pallas as pl
from jax.experimental.pallas import tpu as pltpu
from jax.sharding import PartitionSpec as P

NFFT = 256
NF = 128
NB = 32
LANES = 128
PACK = LANES // NB
F32 = jnp.float32
BF16 = jnp.bfloat16
VMEM = pltpu.VMEM
SMEM = pltpu.SMEM


def spectral_table(freq_lines):
    moments = jnp.arange(NFFT, dtype=jnp.int32)
    cycle = freq_lines[:, None] * moments[None, :] % NFFT
    angles = 2.0 * math.pi / NFFT * cycle.astype(jnp.float32)
    window = 0.5 - 0.5 * jnp.cos(2.0 * math.pi / NFFT * moments.astype(jnp.float32))
    window = window / jnp.sqrt(jnp.sum(window * window))
    return jnp.concatenate(
        [window[None, :] * jnp.cos(angles), -window[None, :] * jnp.sin(angles)], axis=0
    )


def split(x):
    high = x.astype(BF16)
    return high, (x - high.astype(F32)).astype(BF16)


def dft_kernel(starts_ref, table_ref, series_ref, spec_ref, power_ref, halves):
    high, low = split(table_ref[...])
    halves[:NFFT] = high
    halves[NFFT:] = low
    power_ref[...] = jnp.zeros_like(power_ref)

    def step(pair, carry):
        b = 2 * pair
        block = jnp.concatenate(
            [series_ref[pl.ds(starts_ref[b + i], NFFT), :] for i in range(2)], axis=1
        )
        x_high, x_low = split(block)
        both = jnp.dot(halves[...], x_high, preferred_element_type=F32)
        out = jnp.dot(halves[:NFFT], x_low, preferred_element_type=F32)
        out = out + both[:NFFT] + both[NFFT:]
        for i in range(2):
            part = out[:, i * LANES : (i + 1) * LANES]
            spec_ref[pl.ds(b + i, 2 * NF, stride=NB), :] = part
            square = part * part
            power_ref[...] += square[:NF] + square[NF:]
        return carry

    lax.fori_loop(0, NB // 2, step, 0, unroll=2)
    power_ref[...] = power_ref[...] * (1.0 / NB)


def block_spectra(starts, table, series):
    return pl.pallas_call(
        dft_kernel,
        name="dft",
        in_specs=[
            pl.BlockSpec(memory_space=SMEM),
            pl.BlockSpec(memory_space=VMEM),
            pl.BlockSpec(memory_space=VMEM),
        ],
        out_specs=[pl.BlockSpec(memory_space=VMEM)] * 2,
        out_shape=[
            jax.ShapeDtypeStruct((2 * NF * NB, LANES), F32),
            jax.ShapeDtypeStruct((NF, LANES), F32),
        ],
        scratch_shapes=[VMEM((2 * NFFT, NFFT), BF16)],
        compiler_params=pltpu.CompilerParams(vmem_limit_bytes=24 << 20),
        cost_estimate=pl.CostEstimate(
            flops=6 * 2 * NF * NFFT * NB * LANES, bytes_accessed=6 << 20, transcendentals=0
        ),
    )(starts, table, series)


def gram_kernel(count, first_ref, spec_ref, out_ref):
    rows = PACK * NB
    base = first_ref[0] * rows
    row = lax.broadcasted_iota(jnp.int32, (NB, LANES), 0)
    lane = lax.broadcasted_iota(jnp.int32, (NB, LANES), 1)
    upper = row <= lane % NB
    contract = (((1,), (1,)), ((), ()))
    for j in range(count):
        start = pl.multiple_of(base + j * rows, rows)
        spectra = jnp.concatenate(
            [spec_ref[pl.ds(start, rows), :], spec_ref[pl.ds(start + NF * NB, rows), :]], axis=1
        )
        high, low = split(spectra)
        turned = [
            jnp.concatenate([a, jnp.concatenate([a[:, LANES:], -a[:, :LANES]], axis=1)], axis=0)
            for a in (high, low)
        ]
        both = lax.dot_general(
            jnp.concatenate([high, low], axis=0), turned[0], contract, preferred_element_type=F32
        )
        full = lax.dot_general(high, turned[1], contract, preferred_element_type=F32)
        full = full + both[:rows] + both[rows:]
        packed = jnp.zeros((NB, LANES), F32)
        for i in range(PACK):
            mine = full[i * NB : (i + 1) * NB]
            chosen = jnp.where(upper, mine[:, :LANES], mine[:, LANES:])
            packed = jnp.where(lane // NB == i, chosen, packed)
        out_ref[j] = packed


def packed_grams(first, count, spec):
    return pl.pallas_call(
        functools.partial(gram_kernel, count),
        name="gram",
        in_specs=[pl.BlockSpec(memory_space=SMEM), pl.BlockSpec(memory_space=VMEM)],
        out_specs=pl.BlockSpec(memory_space=VMEM),
        out_shape=jax.ShapeDtypeStruct((count, NB, LANES), F32),
        compiler_params=pltpu.CompilerParams(vmem_limit_bytes=24 << 20),
        cost_estimate=pl.CostEstimate(
            flops=count * 6 * LANES * 4 * LANES * LANES * 2,
            bytes_accessed=count << 18,
            transcendentals=0,
        ),
    )(first.reshape(1), spec)


def unpack_kernel(count, factor, packed_ref, out_ref):
    row = lax.broadcasted_iota(jnp.int32, (NB, NB), 0)
    column = lax.broadcasted_iota(jnp.int32, (NB, NB), 1)
    for j in range(count):
        packed = packed_ref[j] * factor
        turned = packed.T
        for i in range(PACK):
            here = packed[:, i * NB : (i + 1) * NB]
            there = turned[i * NB : (i + 1) * NB, :]
            out_ref[0, j * PACK + i] = jnp.where(row <= column, here, there)
            out_ref[1, j * PACK + i] = jnp.where(
                row > column, here, jnp.where(row < column, -there, 0.0)
            )


def unpack(packed, factor):
    count = packed.shape[0]
    return pl.pallas_call(
        functools.partial(unpack_kernel, count, factor),
        name="unpack",
        in_specs=[pl.BlockSpec(memory_space=VMEM)],
        out_specs=pl.BlockSpec(memory_space=VMEM),
        out_shape=jax.ShapeDtypeStruct((2, count * PACK, NB, NB), F32),
    )(packed)


def summed_small(spec):
    tm = lax.axis_index("tm")
    core = lax.axis_index("space") % 2
    z, x = tm // 2, tm % 2
    groups = NF // PACK // 4

    def swap(value, axis, bits):
        size = lax.axis_size(axis)
        return lax.ppermute(value, axis, [(i, i ^ bits) for i in range(size)])

    terms = []
    for j in (2, 3, 1):
        part = packed_grams((z ^ j) * groups, groups, spec)
        terms.append(swap(part, "tm", 2 * j))
    total = packed_grams(z * groups, groups, spec)
    for term in terms:
        total = total + term
    total = total.reshape(2, 2, groups // 4, NB, LANES)
    kept = lax.dynamic_index_in_dim(total, core, 1, keepdims=False)
    sent = lax.dynamic_index_in_dim(total, 1 - core, 1, keepdims=False)
    kept = kept + swap(sent, "space", 1)
    mine = lax.dynamic_index_in_dim(kept, x, 0, keepdims=False)
    other = lax.dynamic_index_in_dim(kept, 1 - x, 0, keepdims=False)
    from_y = swap(mine, "space", 2)
    from_x = swap(other, "tm", 1)
    from_xy = lax.ppermute(
        other,
        ("tm", "space"),
        [(i * 4 + s, (i ^ 1) * 4 + (s ^ 2)) for i in range(8) for s in range(4)],
    )
    mine = mine + from_y + from_x + from_xy
    theirs = swap(mine, "space", 1)
    first = jnp.where(core == 0, mine, theirs)
    second = jnp.where(core == 0, theirs, mine)
    return jnp.concatenate([first, second], axis=0)


def summed_any(spec):
    packed = packed_grams(jnp.int32(0), NF // PACK, spec)
    own = lax.psum_scatter(packed, "tm", scatter_dimension=0, tiled=True)
    return lax.psum(own, "space")


def body(snapshots, starts, freq_lines):
    groups = lax.axis_size("tm")
    spaces = lax.axis_size("space")
    columns = snapshots.shape[1] // groups
    table = spectral_table(freq_lines)
    arranged = snapshots.reshape(snapshots.shape[0], groups, columns)
    series = lax.all_to_all(arranged, "tm", split_axis=1, concat_axis=0, tiled=True)[:, 0, :]
    spec, power_density = block_spectra(starts, table, series)
    if (groups, spaces) == (8, 4):
        own = summed_small(spec)
    else:
        own = summed_any(spec)
    factor = 1.0 / (NB * columns * groups * spaces)
    return power_density, unpack(own, factor)


def solution(mesh):
    placed = (P("tm", "space"), P(), P())
    return jax.shard_map(
        body,
        mesh=mesh,
        in_specs=placed,
        out_specs=(P(None, ("space", "tm")), P(None, "tm", None, None)),
        check_vma=False,
    )
```

time: 277 us -> 97.4 us (0.35)
  waiting for transfers between devices: 176 us -> 60.9 us
  local copies, waits for them, and re-layouts: 40.6 us -> 5.3 us
  matrix products: 33.9 us -> 0 us
  between operations: 14.8 us -> 1.51 us
  Pallas kernels: 0 us -> 12.6 us
  starting transfers between devices: 7.42 us -> 14.7 us
    psum x1 -> x0, waiting for transfers between devices: 128 us -> none  [body(): summed = lax.psum(own_gram, ('tm', 'space'))]
    dot_general x5 -> x0, matrix products: 33.9 us -> none  [the longest x1 9.72 us: local_terms(): jnp.einsum('fbp,fcp->fbc', real_part, real_part, precision=highest)]
    gather x1 -> x0, local copies, waits for them, and re-layouts: 29.4 us -> none  [block_spectra(): blocks = series[offsets]]
    ppermute x0 -> x8, waiting for transfers between devices: none -> 13.2 us  [the longest x7 11.6 us: swap(): return lax.ppermute(value, axis, [(i, i ^ bits) for i in range(size)])]
    pallas_call x0 -> x6, Pallas kernels: none -> 12.6 us  [the longest x1 7.68 us: block_spectra(): pl.pallas_call(dft_kernel, name='dft', in_specs=[pl.BlockSpec(memory_spac...]
    ppermute x0 -> x8, starting transfers between devices: none -> 7.34 us  [the longest x7 5.39 us: swap(): return lax.ppermute(value, axis, [(i, i ^ bits) for i in range(size)])]
    another operation x2 -> x0, local copies, waits for them, and re-layouts: 5.31 us -> none  [local_terms(): return (power, jnp.stack([gram_real, gram_imag]) * factor)]
  transfers between devices with their start and end apart: 2 -> 9, of which waited for: 2 -> 8; matrix products, arithmetic and copies ran while one was open for 1% -> 1% of each run, Pallas kernels for 0% -> 2%
where the time goes in v1:
time: 97.4 us; the launch traced here: 97 us
  waiting for transfers between devices  60.9 us (63%)
  starting transfers between devices  14.7 us (15%)
  Pallas kernels  12.6 us (13%)
  local copies, waits for them, and re-layouts  5.3 us (5%)
  other arithmetic  2.02 us (2%)
  between operations  1.51 us (2%)
    all_to_all x1, waiting for transfers between devices, body(): lax.all_to_all(arranged, 'tm', split_axis=1, concat_axis=0, tiled=True)  47.7 us
    ppermute x7, waiting for transfers between devices, swap(): return lax.ppermute(value, axis, [(i, i ^ bits) for i in range(size)])  11.6 us
    pallas_call x1, Pallas kernels, block_spectra(): pl.pallas_call(dft_kernel, name='dft', in_specs=[pl.BlockSpec(memory_spac...  7.68 us
    all_to_all x1, starting transfers between devices, body(): lax.all_to_all(arranged, 'tm', split_axis=1, concat_axis=0, tiled=True)  7.38 us
    ppermute x7, starting transfers between devices, swap(): return lax.ppermute(value, axis, [(i, i ^ bits) for i in range(size)])  5.39 us
    unnamed x10, local copies, waits for them, and re-layouts  3.81 us
    pallas_call x4, Pallas kernels, packed_grams(): pl.pallas_call(functools.partial(gram_kernel, count), name='gram', in_spe...  3.12 us
    ppermute x1, starting transfers between devices, summed_small(): lax.ppermute(other, ('tm', 'space'), [(i * 4 + s, (i ^ 1) * 4 + (s ^ 2))...  1.95 us
  transfers between devices with their start and end apart: 9, of which 8 were waited for; matrix products, arithmetic and copies ran while one was open for 1% of the time, Pallas kernels for 2%

profile of v1, /device:TPU:0, one launch (start us, length us, event | category | flops | bytes accessed | tf_op | source)
XLA Modules:
  0.0 97.0 jit_solution(4344081898146957788)
XLA Ops:
  0.6 0.0 copy-start
  0.6 1.6 %copy-done = f32[528,1024]{1,0:T(8,128)S(1)} copy-done((f32[528,1024]{1,0:T(8,128)S(1)}, f32[528,1024]{1,0:T(8,128)}, u32[]{:S(2)}) %copy-start) | copy-done | bytes 2162712
  2.2 1.5 %copy_bitcast_fusion = f32[528,8,128]{2,0,1:T(8,128)} fusion(f32[528,1024]{1,0:T(8,128)S(1)} %copy-done), kind=kLoop, calls=%fused_computation | loop fusion | bytes 4325376 | tf_op jit(solution)/shard_map/reshape | solution.py:206
  3.7 0.0 copy-start.4
  3.7 0.0 copy-start.3
  3.7 7.4 %all-to-all-start = ((f32[528,8,128]{2,0,1:T(8,128)}), f32[528,8,128]{2,0,1:T(8,128)}, u32[]{:S(2)}, u32[]{:S(2)}) async-start(f32[528,8,128]{2,0,1:T(8,128)} %copy_bitcast_fusion), calls=%async_computation | async-start | bytes 4325376 | tf_op jit(solution)/shard_map/all_to_all | solution.py:207
  11.1 0.6 multiply_reduce_fusion
  12.5 0.0 copy-done.4
  12.5 0.6 cosine_multiply_fusion
  13.2 47.7 %all-to-all-done = f32[528,8,128]{2,0,1:T(8,128)} async-done(((f32[528,8,128]{2,0,1:T(8,128)}), f32[528,8,128]{2,0,1:T(8,128)}, u32[]{:S(2)}, u32[]{:S(2)}) %all-to-all-start) | async-done | bytes 2162720 | tf_op jit(solution)/shard_map/all_to_all | solution.py:207
  60.8 0.0 copy-done.3
  60.8 7.7 %dft.1 = (f32[8192,128]{1,0:T(8,128)S(1)}, f32[128,128]{1,0:T(8,128)}) custom-call(s32[32]{0:T(128)S(1)} %copy-done.3, f32[256,256]{1,0:T(8,128)S(1)} %pad_maximum_fusion.table_ref, f32[4224,128]{1,0:T(8,128)} %bitcast.2.series_ref), custom_call_target="tpu_custom_call" | custom-call | flops 1610612736 | bytes 6291456 | tf_op jit(solution)/shard_map/dft/pallas_call | solution.py:65
  68.5 0.0 copy-start.1
  68.5 0.8 gram.7
  69.3 0.1 collective-permute-start.2
  69.4 0.8 gram.6
  70.2 2.3 %collective-permute-start.1 = (f32[8,32,128]{2,1,0:T(8,128)S(1)}, f32[8,32,128]{2,1,0:T(8,128)S(1)}, u32[]{:S(2)}, u32[]{:S(2)}) collective-permute-start(f32[8,32,128]{2,1,0:T(8,128)S(1)} %gram.6), channel_id=1, source_target_pairs={{0,24},{4,28},{8,16},{12,20},{16,8},{20,12},{24,0},{28,4},{1,25},{... | collective-permute-start | bytes 393224 | tf_op jit(solution)/shard_map/ppermute | solution.py:166
  72.5 0.0 copy-done.1
  72.5 0.8 gram.5
  73.3 1.2 %collective-permute-start = (f32[8,32,128]{2,1,0:T(8,128)S(1)}, f32[8,32,128]{2,1,0:T(8,128)S(1)}, u32[]{:S(2)}, u32[]{:S(2)}) collective-permute-start(f32[8,32,128]{2,1,0:T(8,128)S(1)} %gram.5), channel_id=1, source_target_pairs={{0,16},{4,20},{8,24},{12,28},{16,0},{20,4},{24,8},{28,12},{1,17},{... | collective-permute-start | bytes 393224 | tf_op jit(solution)/shard_map/ppermute | solution.py:166
  74.5 0.0 copy-start.2
  74.6 2.2 %copy-done.2 = f32[8192,128]{1,0:T(8,128)S(1)} copy-done((f32[8192,128]{1,0:T(8,128)S(1)}, f32[8192,128]{1,0:T(8,128)}, u32[]{:S(2)}) %copy-start.2) | copy-done | bytes 4194328
  76.7 0.8 gram.4
  77.5 0.0 collective-permute-done.2
  77.5 1.3 %collective-permute-done.1 = f32[8,32,128]{2,1,0:T(8,128)S(1)} collective-permute-done((f32[8,32,128]{2,1,0:T(8,128)S(1)}, f32[8,32,128]{2,1,0:T(8,128)S(1)}, u32[]{:S(2)}, u32[]{:S(2)}) %collective-permute-start.1) | collective-permute-done | bytes 131104 | tf_op jit(solution)/shard_map/ppermute | solution.py:166
  78.9 6.0 %collective-permute-done = f32[8,32,128]{2,1,0:T(8,128)S(1)} collective-permute-done((f32[8,32,128]{2,1,0:T(8,128)S(1)}, f32[8,32,128]{2,1,0:T(8,128)S(1)}, u32[]{:S(2)}, u32[]{:S(2)}) %collective-permute-start) | collective-permute-done | bytes 131104 | tf_op jit(solution)/shard_map/ppermute | solution.py:166
  84.9 0.1 collective-permute-start.3
  85.0 1.2 %collective-permute-done.3 = f32[2,2,32,128]{3,2,1,0:T(8,128)S(1)} collective-permute-done((f32[2,2,32,128]{3,2,1,0:T(8,128)S(1)}, f32[2,2,32,128]{3,2,1,0:T(8,128)S(1)}, u32[]{:S(2)}, u32[]{:S(2)}) %collective-permute-start.3) | collective-permute-done | bytes 65568 | tf_op jit(solution)/shard_map/ppermute | solution.py:166
  86.3 2.0 %collective-permute-start.6 = (f32[2,32,128]{2,1,0:T(8,128)S(1)}, f32[2,32,128]{2,1,0:T(8,128)S(1)}, u32[]{:S(2)}, u32[]{:S(2)}) collective-permute-start(f32[2,32,128]{2,1,0:T(8,128)S(1)} %get-tuple-element.9), channel_id=1, source_target_pairs={{0,6},{1,7},{2,4},{3,5},{4,2},{5,3},{6,0},{7,1},{8,14},{9,15},{10,... | collective-permute-start | bytes 98312 | tf_op jit(solution)/shard_map/ppermute | solution.py:183
  88.3 1.1 %collective-permute-start.5 = (f32[2,32,128]{2,1,0:T(8,128)S(1)}, f32[2,32,128]{2,1,0:T(8,128)S(1)}, u32[]{:S(2)}, u32[]{:S(2)}) collective-permute-start(f32[2,32,128]{2,1,0:T(8,128)S(1)} %get-tuple-element.9), channel_id=1, source_target_pairs={{0,4},{4,0},{8,12},{12,8},{16,20},{20,16},{24,28},{28,24},{1,5},{5... | collective-permute-start | bytes 98312 | tf_op jit(solution)/shard_map/ppermute | solution.py:166
  89.3 0.5 collective-permute-start.4
  89.9 1.5 %collective-permute-done.6 = f32[2,32,128]{2,1,0:T(8,128)S(1)} collective-permute-done((f32[2,32,128]{2,1,0:T(8,128)S(1)}, f32[2,32,128]{2,1,0:T(8,128)S(1)}, u32[]{:S(2)}, u32[]{:S(2)}) %collective-permute-start.6) | collective-permute-done | bytes 32800 | tf_op jit(solution)/shard_map/ppermute | solution.py:183
  91.4 0.8 collective-permute-done.5
  92.2 1.1 %collective-permute-done.4 = f32[2,32,128]{2,1,0:T(8,128)S(1)} collective-permute-done((f32[2,32,128]{2,1,0:T(8,128)S(1)}, f32[2,32,128]{2,1,0:T(8,128)S(1)}, u32[]{:S(2)}, u32[]{:S(2)}) %collective-permute-start.4) | collective-permute-done | bytes 32800 | tf_op jit(solution)/shard_map/ppermute | solution.py:166
  93.3 0.1 collective-permute-start.7
  93.4 1.2 %collective-permute-done.7 = f32[2,32,128]{2,1,0:T(8,128)S(1)} collective-permute-done((f32[2,32,128]{2,1,0:T(8,128)S(1)}, f32[2,32,128]{2,1,0:T(8,128)S(1)}, u32[]{:S(2)}, u32[]{:S(2)}) %collective-permute-start.7) | collective-permute-done | bytes 32800 | tf_op jit(solution)/shard_map/ppermute | solution.py:166
  94.6 0.6 pad_maximum_fusion.1.packed_ref
  95.2 1.8 %unpack.1 = f32[2,16,32,32]{3,2,1,0:T(8,128)} custom-call(f32[4,32,128]{2,1,0:T(8,128)} %pad_maximum_fusion.1.packed_ref), custom_call_target="tpu_custom_call" | custom-call | tf_op jit(solution)/shard_map/unpack/pallas_call | solution.py:149
  (8 shorter events, 0.2 us)
Async XLA Ops:
  0.6 1.6 %copy-start = (f32[528,1024]{1,0:T(8,128)S(1)}, f32[528,1024]{1,0:T(8,128)}, u32[]{:S(2)}) copy-start(f32[528,1024]{1,0:T(8,128)} %param.3) | copy-start | bytes 6488068
  3.7 8.8 %copy-start.4 = (s32[128]{0:T(128)S(1)}, s32[128]{0:T(128)}, u32[]{:S(2)}) copy-start(s32[128]{0:T(128)} %param.5) | copy-start | bytes 1540
  3.7 57.1 %copy-start.3 = (s32[32]{0:T(128)S(1)}, s32[32]{0:T(128)}, u32[]{:S(2)}) copy-start(s32[32]{0:T(128)} %starts_ref.1) | copy-start | bytes 388
  3.7 57.1 %all-to-all-start = ((f32[528,8,128]{2,0,1:T(8,128)}), f32[528,8,128]{2,0,1:T(8,128)}, u32[]{:S(2)}, u32[]{:S(2)}) async-start(f32[528,8,128]{2,0,1:T(8,128)} %copy_bitcast_fusion), calls=%async_computation | async-start | bytes 4325376 | tf_op jit(solution)/shard_map/all_to_all | solution.py:207
  68.5 4.0 %copy-start.1 = (f32[8192,128]{1,0:T(8,128)}, f32[8192,128]{1,0:T(8,128)S(1)}, u32[]{:S(2)}) copy-start(f32[8192,128]{1,0:T(8,128)S(1)} %get-tuple-element.5.spec_ref) | copy-start | bytes 12582916
  69.3 8.2 %collective-permute-start.2 = (f32[8,32,128]{2,1,0:T(8,128)S(1)}, f32[8,32,128]{2,1,0:T(8,128)S(1)}, u32[]{:S(2)}, u32[]{:S(2)}) collective-permute-start(f32[8,32,128]{2,1,0:T(8,128)S(1)} %gram.7), channel_id=1, source_target_pairs={{0,8},{4,12},{8,0},{12,4},{16,24},{20,28},{24,16},{28,20},{1,9},{5... | collective-permute-start | bytes 393224 | tf_op jit(solution)/shard_map/ppermute | solution.py:166
  70.2 8.7 %collective-permute-start.1 = (f32[8,32,128]{2,1,0:T(8,128)S(1)}, f32[8,32,128]{2,1,0:T(8,128)S(1)}, u32[]{:S(2)}, u32[]{:S(2)}) collective-permute-start(f32[8,32,128]{2,1,0:T(8,128)S(1)} %gram.6), channel_id=1, source_target_pairs={{0,24},{4,28},{8,16},{12,20},{16,8},{20,12},{24,0},{28,4},{1,25},{... | collective-permute-start | bytes 393224 | tf_op jit(solution)/shard_map/ppermute | solution.py:166
  73.3 11.6 %collective-permute-start = (f32[8,32,128]{2,1,0:T(8,128)S(1)}, f32[8,32,128]{2,1,0:T(8,128)S(1)}, u32[]{:S(2)}, u32[]{:S(2)}) collective-permute-start(f32[8,32,128]{2,1,0:T(8,128)S(1)} %gram.5), channel_id=1, source_target_pairs={{0,16},{4,20},{8,24},{12,28},{16,0},{20,4},{24,8},{28,12},{1,17},{... | collective-permute-start | bytes 393224 | tf_op jit(solution)/shard_map/ppermute | solution.py:166
  74.5 2.2 %copy-start.2 = (f32[8192,128]{1,0:T(8,128)S(1)}, f32[8192,128]{1,0:T(8,128)}, u32[]{:S(2)}) copy-start(f32[8192,128]{1,0:T(8,128)} %copy-done.1) | copy-start | bytes 12582916
  84.9 1.3 %collective-permute-start.3 = (f32[2,2,32,128]{3,2,1,0:T(8,128)S(1)}, f32[2,2,32,128]{3,2,1,0:T(8,128)S(1)}, u32[]{:S(2)}, u32[]{:S(2)}) collective-permute-start(f32[2,2,32,128]{3,2,1,0:T(8,128)S(1)} %dynamic-slice_bitcast_fusion), channel_id=1, source_target_pairs={{0,1},{1,0},{2,3},{3,2},{4,5},{5,4},{6,7},{7,6},{8,9},{9,8},{10,11... | collective-permute-start | bytes 196616 | tf_op jit(solution)/shard_map/ppermute | solution.py:166
  86.3 5.1 %collective-permute-start.6 = (f32[2,32,128]{2,1,0:T(8,128)S(1)}, f32[2,32,128]{2,1,0:T(8,128)S(1)}, u32[]{:S(2)}, u32[]{:S(2)}) collective-permute-start(f32[2,32,128]{2,1,0:T(8,128)S(1)} %get-tuple-element.9), channel_id=1, source_target_pairs={{0,6},{1,7},{2,4},{3,5},{4,2},{5,3},{6,0},{7,1},{8,14},{9,15},{10,... | collective-permute-start | bytes 98312 | tf_op jit(solution)/shard_map/ppermute | solution.py:183
  88.3 3.9 %collective-permute-start.5 = (f32[2,32,128]{2,1,0:T(8,128)S(1)}, f32[2,32,128]{2,1,0:T(8,128)S(1)}, u32[]{:S(2)}, u32[]{:S(2)}) collective-permute-start(f32[2,32,128]{2,1,0:T(8,128)S(1)} %get-tuple-element.9), channel_id=1, source_target_pairs={{0,4},{4,0},{8,12},{12,8},{16,20},{20,16},{24,28},{28,24},{1,5},{5... | collective-permute-start | bytes 98312 | tf_op jit(solution)/shard_map/ppermute | solution.py:166
  89.3 3.9 %collective-permute-start.4 = (f32[2,32,128]{2,1,0:T(8,128)S(1)}, f32[2,32,128]{2,1,0:T(8,128)S(1)}, u32[]{:S(2)}, u32[]{:S(2)}) collective-permute-start(f32[2,32,128]{2,1,0:T(8,128)S(1)} %get-tuple-element.8), channel_id=1, source_target_pairs={{0,2},{1,3},{2,0},{3,1},{4,6},{5,7},{6,4},{7,5},{8,10},{9,11},{10,... | collective-permute-start | bytes 98312 | tf_op jit(solution)/shard_map/ppermute | solution.py:166
  93.3 1.3 %collective-permute-start.7 = (f32[2,32,128]{2,1,0:T(8,128)S(1)}, f32[2,32,128]{2,1,0:T(8,128)S(1)}, u32[]{:S(2)}, u32[]{:S(2)}) collective-permute-start(f32[2,32,128]{2,1,0:T(8,128)S(1)} %add_add_fusion.1), channel_id=1, source_target_pairs={{0,1},{1,0},{2,3},{3,2},{4,5},{5,4},{6,7},{7,6},{8,9},{9,8},{10,11... | collective-permute-start | bytes 98312 | tf_op jit(solution)/shard_map/ppermute | solution.py:166

commit v2 on v1

v2 whole, which is shorter than its diff:
```python
import functools
import math

import jax
import jax.numpy as jnp
from jax import lax
from jax.experimental import pallas as pl
from jax.experimental.pallas import tpu as pltpu
from jax.sharding import PartitionSpec as P

NFFT = 256
NF = 128
NB = 32
LANES = 128
PACK = LANES // NB
PITCH = NB + 8
CORE_STEP = 2
F32 = jnp.float32
BF16 = jnp.bfloat16
VMEM = pltpu.VMEM
SMEM = pltpu.SMEM


def spectral_table(freq_lines):
    moments = jnp.arange(NFFT, dtype=jnp.int32)
    cycle = freq_lines[:, None] * moments[None, :] % NFFT
    angles = 2.0 * math.pi / NFFT * cycle.astype(jnp.float32)
    window = 0.5 - 0.5 * jnp.cos(2.0 * math.pi / NFFT * moments.astype(jnp.float32))
    window = window / jnp.sqrt(jnp.sum(window * window))
    return jnp.concatenate(
        [window[None, :] * jnp.cos(angles), -window[None, :] * jnp.sin(angles)], axis=0
    )


def split(x):
    high = x.astype(BF16)
    return high, (x - high.astype(F32)).astype(BF16)


def dft_kernel(count, rows, where_ref, starts_ref, table_ref, *refs):
    pieces, (spec_ref, power_ref, halves, series) = refs[:count], refs[count:]
    for k in range(count):
        start = pl.multiple_of(where_ref[k] * rows, 8)
        series[pl.ds(start, rows), :] = pieces[k][...]
    high, low = split(table_ref[...])
    halves[:NFFT] = high
    halves[NFFT:] = low
    power_ref[...] = jnp.zeros_like(power_ref)

    def step(pair, carry):
        b = 2 * pair
        block = jnp.concatenate(
            [series[pl.ds(starts_ref[b + i], NFFT), :] for i in range(2)], axis=1
        )
        x_high, x_low = split(block)
        both = jnp.dot(halves[...], x_high, preferred_element_type=F32)
        out = jnp.dot(halves[:NFFT], x_low, preferred_element_type=F32)
        out = out + both[:NFFT] + both[NFFT:]
        for i in range(2):
            part = out[:, i * LANES : (i + 1) * LANES]
            spec_ref[pl.ds(b + i, 2 * NF, stride=PITCH), :] = part
            square = part * part
            power_ref[...] += square[:NF] + square[NF:]
        return carry

    lax.fori_loop(0, NB // 2, step, 0, unroll=4)
    power_ref[...] = power_ref[...] * (1.0 / NB)


def block_spectra(starts, table, pieces, where):
    count, rows = len(pieces), pieces[0].shape[0]
    return pl.pallas_call(
        functools.partial(dft_kernel, count, rows),
        name="dft",
        in_specs=[pl.BlockSpec(memory_space=SMEM)] * 2
        + [pl.BlockSpec(memory_space=VMEM)] * (1 + count),
        out_specs=[pl.BlockSpec(memory_space=VMEM)] * 2,
        out_shape=[
            jax.ShapeDtypeStruct((2 * NF * PITCH, LANES), F32),
            jax.ShapeDtypeStruct((NF, LANES), F32),
        ],
        scratch_shapes=[VMEM((2 * NFFT, NFFT), BF16), VMEM((count * rows, LANES), F32)],
        compiler_params=pltpu.CompilerParams(vmem_limit_bytes=24 << 20),
        cost_estimate=pl.CostEstimate(
            flops=6 * 2 * NF * NFFT * NB * LANES, bytes_accessed=6 << 20, transcendentals=0
        ),
    )(where, starts, table, *pieces)


def gram_kernel(order, first_ref, core_ref, spec_ref, *out_refs):
    rows = PACK * NB
    row = lax.broadcasted_iota(jnp.int32, (NB, LANES), 0)
    lane = lax.broadcasted_iota(jnp.int32, (NB, LANES), 1)
    upper = row <= lane % NB
    contract = (((1,), (1,)), ((), ()))
    for j, place in order:
        for out_ref, group in zip(out_refs, (j + core_ref[0] * CORE_STEP, j + (1 - core_ref[0]) * CORE_STEP)):
            line = (first_ref[0] + group) * PACK
            starts = [pl.multiple_of((line + i) * PITCH, 8) for i in range(PACK)]
            spectra = jnp.concatenate(
                [
                    jnp.concatenate([spec_ref[pl.ds(s + part * NF * PITCH, NB), :] for s in starts], axis=0)
                    for part in range(2)
                ],
                axis=1,
            )
            high, low = split(spectra)
            turned = [
                jnp.concatenate([a, jnp.concatenate([a[:, LANES:], -a[:, :LANES]], axis=1)], axis=0)
                for a in (high, low)
            ]
            both = lax.dot_general(
                jnp.concatenate([high, low], axis=0), turned[0], contract, preferred_element_type=F32
            )
            full = lax.dot_general(high, turned[1], contract, preferred_element_type=F32)
            full = full + both[:rows] + both[rows:]
            packed = jnp.zeros((NB, LANES), F32)
            for i in range(PACK):
                mine = full[i * NB : (i + 1) * NB]
                chosen = jnp.where(upper, mine[:, :LANES], mine[:, LANES:])
                packed = jnp.where(lane // NB == i, chosen, packed)
            out_ref[place] = packed


def packed_grams(first, core, order, outputs, spec):
    count = len(order)
    return pl.pallas_call(
        functools.partial(gram_kernel, order),
        name="gram",
        in_specs=[pl.BlockSpec(memory_space=SMEM)] * 2 + [pl.BlockSpec(memory_space=VMEM)],
        out_specs=[pl.BlockSpec(memory_space=VMEM)] * outputs,
        out_shape=[jax.ShapeDtypeStruct((count, NB, LANES), F32)] * outputs,
        compiler_params=pltpu.CompilerParams(vmem_limit_bytes=24 << 20),
        cost_estimate=pl.CostEstimate(
            flops=outputs * count * 6 * LANES * 4 * LANES * LANES * 2,
            bytes_accessed=outputs * count << 18,
            transcendentals=0,
        ),
    )(first.reshape(1), core.reshape(1), spec)


def unpack_kernel(factor, order_ref, *refs):
    packed_refs, out_ref = refs[:-1], refs[-1]
    row = lax.broadcasted_iota(jnp.int32, (NB, NB), 0)
    column = lax.broadcasted_iota(jnp.int32, (NB, NB), 1)
    for n, packed_ref in enumerate(packed_refs):
        count = packed_ref.shape[0]
        for j in range(count):
            packed = packed_ref[j] * factor
            turned = packed.T
            line = (order_ref[n] * count + j) * PACK
            for i in range(PACK):
                here = packed[:, i * NB : (i + 1) * NB]
                there = turned[i * NB : (i + 1) * NB, :]
                out_ref[0, line + i] = jnp.where(row <= column, here, there)
                out_ref[1, line + i] = jnp.where(
                    row > column, here, jnp.where(row < column, -there, 0.0)
                )


def unpack(parts, order, factor):
    lines = sum(p.shape[0] for p in parts) * PACK
    return pl.pallas_call(
        functools.partial(unpack_kernel, factor),
        name="unpack",
        in_specs=[pl.BlockSpec(memory_space=SMEM)]
        + [pl.BlockSpec(memory_space=VMEM)] * len(parts),
        out_specs=pl.BlockSpec(memory_space=VMEM),
        out_shape=jax.ShapeDtypeStruct((2, lines, NB, NB), F32),
    )(order, *parts)


def swap(value, axis, bits):
    return lax.ppermute(value, axis, [(i, i ^ bits) for i in range(lax.axis_size(axis))])


def exchanged_small(snapshots):
    me = lax.axis_index("tm")
    order = (4, 5, 2, 6, 3, 7, 1)
    rows = snapshots.shape[0]
    pieces = [
        lax.dynamic_slice(snapshots, (0, (me ^ k) * LANES), (rows, LANES)) for k in (*order, 0)
    ]
    pieces = lax.optimization_barrier(pieces)
    pieces = [swap(p, "tm", k) for p, k in zip(pieces, order)] + [pieces[-1]]
    return pieces, jnp.stack([me ^ k for k in (*order, 0)])


def summed_small(spec):
    tm = lax.axis_index("tm")
    core = lax.axis_index("space") % 2
    z, x = tm // 2, tm % 2
    groups = NF // PACK // 4
    order = [(x_ * 4 + i, x_ * 2 + i) for x_ in range(2) for i in range(2)]
    total = None
    for j in (2, 3, 1, 0):
        kept, sent = packed_grams((z ^ j) * groups, core, order, 2, spec)
        part = kept + swap(sent, "space", 1)
        if j:
            part = swap(part, "tm", 2 * j)
        total = part if total is None else total + part
    kept = total.reshape(2, 2, NB, LANES)
    mine = lax.dynamic_index_in_dim(kept, x, 0, keepdims=False)
    other = lax.dynamic_index_in_dim(kept, 1 - x, 0, keepdims=False)
    from_y = swap(mine, "space", 2)
    from_x = swap(other, "tm", 1)
    from_xy = lax.ppermute(
        other,
        ("tm", "space"),
        [(i * 4 + s, (i ^ 1) * 4 + (s ^ 2)) for i in range(8) for s in range(4)],
    )
    mine = mine + from_y + from_x + from_xy
    return [mine, swap(mine, "space", 1)], jnp.stack([core, 1 - core])


def summed_any(spec):
    zero = jnp.int32(0)
    order = [(j, j) for j in range(NF // PACK)]
    (packed,) = packed_grams(zero, zero, order, 1, spec)
    own = lax.psum_scatter(packed, "tm", scatter_dimension=0, tiled=True)
    return [lax.psum(own, "space")], jnp.zeros((1,), jnp.int32)


def body(snapshots, starts, freq_lines):
    groups = lax.axis_size("tm")
    spaces = lax.axis_size("space")
    columns = snapshots.shape[1] // groups
    small = (groups, spaces) == (8, 4)
    if small:
        pieces, where = exchanged_small(snapshots)
    else:
        arranged = snapshots.reshape(snapshots.shape[0], groups, columns)
        series = lax.all_to_all(arranged, "tm", split_axis=1, concat_axis=0, tiled=True)[:, 0, :]
        pieces, where = [series], jnp.zeros((1,), jnp.int32)
    table = spectral_table(freq_lines)
    spec, power_density = block_spectra(starts, table, pieces, where)
    parts, order = summed_small(spec) if small else summed_any(spec)
    return power_density, unpack(parts, order, 1.0 / (NB * columns * groups * spaces))


def solution(mesh):
    placed = (P("tm", "space"), P(), P())
    return jax.shard_map(
        body,
        mesh=mesh,
        in_specs=placed,
        out_specs=(P(None, ("space", "tm")), P(None, "tm", None, None)),
        check_vma=False,
    )
```

time: 97.4 us -> 81.5 us (0.84)
  waiting for transfers between devices: 60.9 us -> 39.1 us
  starting transfers between devices: 14.7 us -> 27.2 us
  Pallas kernels: 12.6 us -> 8.91 us
  local copies, waits for them, and re-layouts: 5.3 us -> 2.44 us
    all_to_all x1 -> x0, waiting for transfers between devices: 47.7 us -> none  [body(): lax.all_to_all(arranged, 'tm', split_axis=1, concat_axis=0, tiled=True)]
    ppermute x7 -> x17, waiting for transfers between devices: 11.6 us -> 37.6 us  [swap(): lax.ppermute(value, axis, [(i, i ^ bits) for i in range(lax.axis_size(axi...]
    ppermute x7 -> x17, starting transfers between devices: 5.39 us -> 25.8 us  [swap(): lax.ppermute(value, axis, [(i, i ^ bits) for i in range(lax.axis_size(axi...]
    all_to_all x1 -> x0, starting transfers between devices: 7.38 us -> none  [body(): lax.all_to_all(arranged, 'tm', split_axis=1, concat_axis=0, tiled=True)]
    pallas_call x6, Pallas kernels: 12.6 us -> 8.91 us  [the longest x1 4.07 us: block_spectra(): pl.pallas_call(functools.partial(dft_kernel, count, rows), name='dft', in...]
    unnamed x10 -> x8, local copies, waits for them, and re-layouts: 3.81 us -> 0.62 us
    dynamic_slice x0 -> x1, local copies, waits for them, and re-layouts: none -> 1.72 us  [exchanged_small(): lax.dynamic_slice(snapshots, (0, (me ^ k) * LANES), (rows, LANES))]
    reshape x1 -> x0, local copies, waits for them, and re-layouts: 1.46 us -> none  [body(): arranged = snapshots.reshape(snapshots.shape[0], groups, columns)]
  transfers between devices with their start and end apart: 9 -> 18, of which waited for: 8 -> 10; matrix products, arithmetic and copies ran while one was open for 1% -> 3% of each run, Pallas kernels for 2% -> 3%
where the time goes in v2:
time: 81.5 us; the launch traced here: 81.3 us
  waiting for transfers between devices  39.1 us (48%)
  starting transfers between devices  27.2 us (33%)
  Pallas kernels  8.91 us (11%)
  local copies, waits for them, and re-layouts  2.44 us (3%)
  other arithmetic  2.04 us (3%)
  between operations  1.59 us (2%)
    ppermute x17, waiting for transfers between devices, swap(): lax.ppermute(value, axis, [(i, i ^ bits) for i in range(lax.axis_size(axi...  37.6 us
    ppermute x17, starting transfers between devices, swap(): lax.ppermute(value, axis, [(i, i ^ bits) for i in range(lax.axis_size(axi...  25.8 us
    pallas_call x1, Pallas kernels, block_spectra(): pl.pallas_call(functools.partial(dft_kernel, count, rows), name='dft', in...  4.07 us
    pallas_call x4, Pallas kernels, packed_grams(): pl.pallas_call(functools.partial(gram_kernel, order), name='gram', in_spe...  3.06 us
    pallas_call x1, Pallas kernels, unpack(): pl.pallas_call(functools.partial(unpack_kernel, factor), name='unpack', i...  1.78 us
    dynamic_slice x1, local copies, waits for them, and re-layouts, exchanged_small(): lax.dynamic_slice(snapshots, (0, (me ^ k) * LANES), (rows, LANES))  1.72 us
  transfers between devices with their start and end apart: 18, of which 10 were waited for; matrix products, arithmetic and copies ran while one was open for 3% of the time, Pallas kernels for 3%

profile of v2, /device:TPU:0, one launch (start us, length us, event | category | flops | bytes accessed | tf_op | source)
XLA Modules:
  0.0 81.3 jit_solution(6326508474977735182)
XLA Ops:
  0.7 0.0 copy-start.3
  0.7 0.0 copy-start
  0.7 1.7 %constant_dynamic-slice_fusion = (f32[528,128]{1,0:T(8,128)S(1)}, f32[528,128]{1,0:T(8,128)S(1)}, f32[528,128]{1,0:T(8,128)S(1)}, f32[528,128]{1,0:T(8,128)S(1)}...) fusion(f32[528,1024]{1,0:T(8,128)} %param.3, ...), kind=kLoop, calls=%fused_computation.16 | loop fusion | bytes 4325408 | tf_op jit(solution)/shard_map/dynamic_slice | solution.py:182
  2.4 4.1 %collective-permute-start = (f32[528,128]{1,0:T(8,128)S(1)}, f32[528,128]{1,0:T(8,128)S(1)}, u32[]{:S(2)}, u32[]{:S(2)}) collective-permute-start(f32[528,128]{1,0:T(8,128)S(1)} %get-tuple-element.20), channel_id=1, source_target_pairs={{0,16},{4,20},{8,24},{12,28},{16,0},{20,4},{24,8},{28,12},{1,17},{... | collective-permute-start | bytes 811016 | tf_op jit(solution)/shard_map/ppermute | solution.py:174
  6.5 1.3 %collective-permute-start.1 = (f32[528,128]{1,0:T(8,128)S(1)}, f32[528,128]{1,0:T(8,128)S(1)}, u32[]{:S(2)}, u32[]{:S(2)}) collective-permute-start(f32[528,128]{1,0:T(8,128)S(1)} %get-tuple-element.21), channel_id=1, source_target_pairs={{0,20},{4,16},{8,28},{12,24},{16,4},{20,0},{24,12},{28,8},{1,21},{... | collective-permute-start | bytes 811016 | tf_op jit(solution)/shard_map/ppermute | solution.py:174
  7.8 1.6 %collective-permute-start.2 = (f32[528,128]{1,0:T(8,128)S(1)}, f32[528,128]{1,0:T(8,128)S(1)}, u32[]{:S(2)}, u32[]{:S(2)}) collective-permute-start(f32[528,128]{1,0:T(8,128)S(1)} %get-tuple-element.22), channel_id=1, source_target_pairs={{0,8},{4,12},{8,0},{12,4},{16,24},{20,28},{24,16},{28,20},{1,9},{5... | collective-permute-start | bytes 811016 | tf_op jit(solution)/shard_map/ppermute | solution.py:174
  9.4 2.5 %collective-permute-start.3 = (f32[528,128]{1,0:T(8,128)S(1)}, f32[528,128]{1,0:T(8,128)S(1)}, u32[]{:S(2)}, u32[]{:S(2)}) collective-permute-start(f32[528,128]{1,0:T(8,128)S(1)} %get-tuple-element.23), channel_id=1, source_target_pairs={{0,24},{4,28},{8,16},{12,20},{16,8},{20,12},{24,0},{28,4},{1,25},{... | collective-permute-start | bytes 811016 | tf_op jit(solution)/shard_map/ppermute | solution.py:174
  11.8 0.6 collective-permute-start.4
  12.5 0.7 multiply_reduce_fusion
  14.0 0.1 stack.44.where_ref
  14.1 12.3 %collective-permute-done.refs_0_ = f32[528,128]{1,0:T(8,128)S(1)} collective-permute-done((f32[528,128]{1,0:T(8,128)S(1)}, f32[528,128]{1,0:T(8,128)S(1)}, u32[]{:S(2)}, u32[]{:S(2)}) %collective-permute-start) | collective-permute-done | bytes 270368 | tf_op jit(solution)/shard_map/ppermute | solution.py:174
  26.4 4.0 %collective-permute-start.5 = (f32[528,128]{1,0:T(8,128)S(1)}, f32[528,128]{1,0:T(8,128)S(1)}, u32[]{:S(2)}, u32[]{:S(2)}) collective-permute-start(f32[528,128]{1,0:T(8,128)S(1)} %get-tuple-element.25), channel_id=1, source_target_pairs={{0,28},{4,24},{8,20},{12,16},{16,12},{20,8},{24,4},{28,0},{1,29},{... | collective-permute-start | bytes 811016 | tf_op jit(solution)/shard_map/ppermute | solution.py:174
  30.4 9.0 %collective-permute-done.1.refs_1_ = f32[528,128]{1,0:T(8,128)S(1)} collective-permute-done((f32[528,128]{1,0:T(8,128)S(1)}, f32[528,128]{1,0:T(8,128)S(1)}, u32[]{:S(2)}, u32[]{:S(2)}) %collective-permute-start.1) | collective-permute-done | bytes 270368 | tf_op jit(solution)/shard_map/ppermute | solution.py:174
  39.4 0.0 collective-permute-start.6
  39.4 0.0 copy-done.3
  39.4 0.6 cosine_multiply_fusion
  40.1 0.0 collective-permute-done.2.refs_2_
  40.1 0.0 collective-permute-done.3.refs_3_
  40.1 0.0 collective-permute-done.4.refs_4_
  40.1 4.1 %collective-permute-done.5.refs_5_ = f32[528,128]{1,0:T(8,128)S(1)} collective-permute-done((f32[528,128]{1,0:T(8,128)S(1)}, f32[528,128]{1,0:T(8,128)S(1)}, u32[]{:S(2)}, u32[]{:S(2)}) %collective-permute-start.5) | collective-permute-done | bytes 270368 | tf_op jit(solution)/shard_map/ppermute | solution.py:174
  44.2 5.5 %collective-permute-done.6.refs_6_ = f32[528,128]{1,0:T(8,128)S(1)} collective-permute-done((f32[528,128]{1,0:T(8,128)S(1)}, f32[528,128]{1,0:T(8,128)S(1)}, u32[]{:S(2)}, u32[]{:S(2)}) %collective-permute-start.6) | collective-permute-done | bytes 270368 | tf_op jit(solution)/shard_map/ppermute | solution.py:174
  49.7 0.0 copy-done
  49.7 4.1 %dft.1 = (f32[10240,128]{1,0:T(8,128)S(1)}, f32[128,128]{1,0:T(8,128)}) custom-call(s32[8]{0:T(128)S(1)} %stack.44.where_ref, s32[32]{0:T(128)S(1)} %copy-done, f32[256,256]{1,0:T(8,128)S(1)} %pad_maximum_fusion.table_ref, f32[528,128]{1,0:T(8,128)S(1)} %collective-permute-done.refs_0_, f32[528,128]{1,0:T(8,128)S(1)} %collective-permute-done.1.refs_1_, ...), custom_call_target="tpu_custom_call" | custom-call | flops 1610612736 | bytes 6291456 | tf_op jit(solution)/shard_map/dft/pallas_call | solution.py:72
  53.8 0.8 gram.5
  54.6 0.1 collective-permute-start.9
  54.6 0.8 gram.4
  55.4 0.6 collective-permute-start.7
  56.0 0.8 gram.6
  56.7 0.1 collective-permute-start.11
  56.8 0.8 gram.7
  57.6 0.6 collective-permute-start.13
  58.2 0.0 collective-permute-done.9
  58.2 4.0 %collective-permute-start.10 = (f32[4,32,128]{2,1,0:T(8,128)S(1)}, f32[4,32,128]{2,1,0:T(8,128)S(1)}, u32[]{:S(2)}, u32[]{:S(2)}) collective-permute-start(f32[4,32,128]{2,1,0:T(8,128)S(1)} %add.87), channel_id=1, source_target_pairs={{0,24},{4,28},{8,16},{12,20},{16,8},{20,12},{24,0},{28,4},{1,25},{... | collective-permute-start | bytes 196616 | tf_op jit(solution)/shard_map/ppermute | solution.py:174
  62.2 0.0 collective-permute-done.7
  62.2 3.6 %collective-permute-start.8 = (f32[4,32,128]{2,1,0:T(8,128)S(1)}, f32[4,32,128]{2,1,0:T(8,128)S(1)}, u32[]{:S(2)}, u32[]{:S(2)}) collective-permute-start(f32[4,32,128]{2,1,0:T(8,128)S(1)} %add.86), channel_id=1, source_target_pairs={{0,16},{4,20},{8,24},{12,28},{16,0},{20,4},{24,8},{28,12},{1,17},{... | collective-permute-start | bytes 196616 | tf_op jit(solution)/shard_map/ppermute | solution.py:174
  65.8 0.0 collective-permute-done.11
  65.8 0.6 collective-permute-start.12
  66.4 0.0 collective-permute-done.13
  66.4 0.0 collective-permute-done.10
  66.4 3.7 %collective-permute-done.8 = f32[4,32,128]{2,1,0:T(8,128)S(1)} collective-permute-done((f32[4,32,128]{2,1,0:T(8,128)S(1)}, f32[4,32,128]{2,1,0:T(8,128)S(1)}, u32[]{:S(2)}, u32[]{:S(2)}) %collective-permute-start.8) | collective-permute-done | bytes 65568 | tf_op jit(solution)/shard_map/ppermute | solution.py:174
  70.2 0.4 collective-permute-done.12
  70.6 1.6 %collective-permute-start.14 = (f32[2,32,128]{2,1,0:T(8,128)S(1)}, f32[2,32,128]{2,1,0:T(8,128)S(1)}, u32[]{:S(2)}, u32[]{:S(2)}) collective-permute-start(f32[2,32,128]{2,1,0:T(8,128)S(1)} %get-tuple-element.46), channel_id=1, source_target_pairs={{0,2},{1,3},{2,0},{3,1},{4,6},{5,7},{6,4},{7,5},{8,10},{9,11},{10,... | collective-permute-start | bytes 98312 | tf_op jit(solution)/shard_map/ppermute | solution.py:174
  72.2 0.5 collective-permute-start.15
  72.8 1.4 %collective-permute-start.16 = (f32[2,32,128]{2,1,0:T(8,128)S(1)}, f32[2,32,128]{2,1,0:T(8,128)S(1)}, u32[]{:S(2)}, u32[]{:S(2)}) collective-permute-start(f32[2,32,128]{2,1,0:T(8,128)S(1)} %get-tuple-element.47), channel_id=1, source_target_pairs={{0,6},{1,7},{2,4},{3,5},{4,2},{5,3},{6,0},{7,1},{8,14},{9,15},{10,... | collective-permute-start | bytes 98312 | tf_op jit(solution)/shard_map/ppermute | solution.py:207
  74.2 0.4 collective-permute-done.14
  74.6 1.5 %collective-permute-done.15 = f32[2,32,128]{2,1,0:T(8,128)S(1)} collective-permute-done((f32[2,32,128]{2,1,0:T(8,128)S(1)}, f32[2,32,128]{2,1,0:T(8,128)S(1)}, u32[]{:S(2)}, u32[]{:S(2)}) %collective-permute-start.15) | collective-permute-done | bytes 32800 | tf_op jit(solution)/shard_map/ppermute | solution.py:174
  76.1 1.4 %collective-permute-done.16 = f32[2,32,128]{2,1,0:T(8,128)S(1)} collective-permute-done((f32[2,32,128]{2,1,0:T(8,128)S(1)}, f32[2,32,128]{2,1,0:T(8,128)S(1)}, u32[]{:S(2)}, u32[]{:S(2)}) %collective-permute-start.16) | collective-permute-done | bytes 32800 | tf_op jit(solution)/shard_map/ppermute | solution.py:207
  77.6 0.0 copy-start.1
  77.6 0.1 collective-permute-start.17
  77.7 0.6 pad_add_fusion.order_ref
  78.2 0.6 collective-permute-done.17.refs_1_
  78.9 0.0 copy-done.1
  78.9 0.0 copy-start.2
  78.9 0.6 copy-done.2
  79.5 1.8 %unpack.1 = f32[2,16,32,32]{3,2,1,0:T(8,128)} custom-call(s32[2]{0:T(128)} %pad_add_fusion.order_ref, f32[2,32,128]{2,1,0:T(8,128)} %copy-done.1, f32[2,32,128]{2,1,0:T(8,128)} %copy-done.2), custom_call_target="tpu_custom_call" | custom-call | tf_op jit(solution)/shard_map/unpack/pallas_call | solution.py:163
  (8 shorter events, 0.1 us)
Async XLA Ops:
  0.7 38.8 %copy-start.3 = (s32[128]{0:T(128)S(1)}, s32[128]{0:T(128)}, u32[]{:S(2)}) copy-start(s32[128]{0:T(128)} %param.5) | copy-start | bytes 1540
  0.7 49.0 %copy-start = (s32[32]{0:T(128)S(1)}, s32[32]{0:T(128)}, u32[]{:S(2)}) copy-start(s32[32]{0:T(128)} %starts_ref.1) | copy-start | bytes 388
  2.4 24.0 %collective-permute-start = (f32[528,128]{1,0:T(8,128)S(1)}, f32[528,128]{1,0:T(8,128)S(1)}, u32[]{:S(2)}, u32[]{:S(2)}) collective-permute-start(f32[528,128]{1,0:T(8,128)S(1)} %get-tuple-element.20), channel_id=1, source_target_pairs={{0,16},{4,20},{8,24},{12,28},{16,0},{20,4},{24,8},{28,12},{1,17},{... | collective-permute-start | bytes 811016 | tf_op jit(solution)/shard_map/ppermute | solution.py:174
  6.5 32.9 %collective-permute-start.1 = (f32[528,128]{1,0:T(8,128)S(1)}, f32[528,128]{1,0:T(8,128)S(1)}, u32[]{:S(2)}, u32[]{:S(2)}) collective-permute-start(f32[528,128]{1,0:T(8,128)S(1)} %get-tuple-element.21), channel_id=1, source_target_pairs={{0,20},{4,16},{8,28},{12,24},{16,4},{20,0},{24,12},{28,8},{1,21},{... | collective-permute-start | bytes 811016 | tf_op jit(solution)/shard_map/ppermute | solution.py:174
  7.8 32.3 %collective-permute-start.2 = (f32[528,128]{1,0:T(8,128)S(1)}, f32[528,128]{1,0:T(8,128)S(1)}, u32[]{:S(2)}, u32[]{:S(2)}) collective-permute-start(f32[528,128]{1,0:T(8,128)S(1)} %get-tuple-element.22), channel_id=1, source_target_pairs={{0,8},{4,12},{8,0},{12,4},{16,24},{20,28},{24,16},{28,20},{1,9},{5... | collective-permute-start | bytes 811016 | tf_op jit(solution)/shard_map/ppermute | solution.py:174
  9.4 30.7 %collective-permute-start.3 = (f32[528,128]{1,0:T(8,128)S(1)}, f32[528,128]{1,0:T(8,128)S(1)}, u32[]{:S(2)}, u32[]{:S(2)}) collective-permute-start(f32[528,128]{1,0:T(8,128)S(1)} %get-tuple-element.23), channel_id=1, source_target_pairs={{0,24},{4,28},{8,16},{12,20},{16,8},{20,12},{24,0},{28,4},{1,25},{... | collective-permute-start | bytes 811016 | tf_op jit(solution)/shard_map/ppermute | solution.py:174
  11.8 28.3 %collective-permute-start.4 = (f32[528,128]{1,0:T(8,128)S(1)}, f32[528,128]{1,0:T(8,128)S(1)}, u32[]{:S(2)}, u32[]{:S(2)}) collective-permute-start(f32[528,128]{1,0:T(8,128)S(1)} %get-tuple-element.24), channel_id=1, source_target_pairs={{0,12},{4,8},{8,4},{12,0},{16,28},{20,24},{24,20},{28,16},{1,13},{... | collective-permute-start | bytes 811016 | tf_op jit(solution)/shard_map/ppermute | solution.py:174
  26.4 17.8 %collective-permute-start.5 = (f32[528,128]{1,0:T(8,128)S(1)}, f32[528,128]{1,0:T(8,128)S(1)}, u32[]{:S(2)}, u32[]{:S(2)}) collective-permute-start(f32[528,128]{1,0:T(8,128)S(1)} %get-tuple-element.25), channel_id=1, source_target_pairs={{0,28},{4,24},{8,20},{12,16},{16,12},{20,8},{24,4},{28,0},{1,29},{... | collective-permute-start | bytes 811016 | tf_op jit(solution)/shard_map/ppermute | solution.py:174
  39.4 10.3 %collective-permute-start.6 = (f32[528,128]{1,0:T(8,128)S(1)}, f32[528,128]{1,0:T(8,128)S(1)}, u32[]{:S(2)}, u32[]{:S(2)}) collective-permute-start(f32[528,128]{1,0:T(8,128)S(1)} %get-tuple-element.26), channel_id=1, source_target_pairs={{0,4},{4,0},{8,12},{12,8},{16,20},{20,16},{24,28},{28,24},{1,5},{5... | collective-permute-start | bytes 811016 | tf_op jit(solution)/shard_map/ppermute | solution.py:174
  54.6 3.6 %collective-permute-start.9 = (f32[4,32,128]{2,1,0:T(8,128)S(1)}, f32[4,32,128]{2,1,0:T(8,128)S(1)}, u32[]{:S(2)}, u32[]{:S(2)}) collective-permute-start(f32[4,32,128]{2,1,0:T(8,128)S(1)} %get-tuple-element.33), channel_id=1, source_target_pairs={{0,1},{1,0},{2,3},{3,2},{4,5},{5,4},{6,7},{7,6},{8,9},{9,8},{10,11... | collective-permute-start | bytes 196616 | tf_op jit(solution)/shard_map/ppermute | solution.py:174
  55.4 6.8 %collective-permute-start.7 = (f32[4,32,128]{2,1,0:T(8,128)S(1)}, f32[4,32,128]{2,1,0:T(8,128)S(1)}, u32[]{:S(2)}, u32[]{:S(2)}) collective-permute-start(f32[4,32,128]{2,1,0:T(8,128)S(1)} %get-tuple-element.31), channel_id=1, source_target_pairs={{0,1},{1,0},{2,3},{3,2},{4,5},{5,4},{6,7},{7,6},{8,9},{9,8},{10,11... | collective-permute-start | bytes 196616 | tf_op jit(solution)/shard_map/ppermute | solution.py:174
  56.7 9.0 %collective-permute-start.11 = (f32[4,32,128]{2,1,0:T(8,128)S(1)}, f32[4,32,128]{2,1,0:T(8,128)S(1)}, u32[]{:S(2)}, u32[]{:S(2)}) collective-permute-start(f32[4,32,128]{2,1,0:T(8,128)S(1)} %get-tuple-element.35), channel_id=1, source_target_pairs={{0,1},{1,0},{2,3},{3,2},{4,5},{5,4},{6,7},{7,6},{8,9},{9,8},{10,11... | collective-permute-start | bytes 196616 | tf_op jit(solution)/shard_map/ppermute | solution.py:174
  57.6 8.8 %collective-permute-start.13 = (f32[4,32,128]{2,1,0:T(8,128)S(1)}, f32[4,32,128]{2,1,0:T(8,128)S(1)}, u32[]{:S(2)}, u32[]{:S(2)}) collective-permute-start(f32[4,32,128]{2,1,0:T(8,128)S(1)} %get-tuple-element.37), channel_id=1, source_target_pairs={{0,1},{1,0},{2,3},{3,2},{4,5},{5,4},{6,7},{7,6},{8,9},{9,8},{10,11... | collective-permute-start | bytes 196616 | tf_op jit(solution)/shard_map/ppermute | solution.py:174
  58.2 8.3 %collective-permute-start.10 = (f32[4,32,128]{2,1,0:T(8,128)S(1)}, f32[4,32,128]{2,1,0:T(8,128)S(1)}, u32[]{:S(2)}, u32[]{:S(2)}) collective-permute-start(f32[4,32,128]{2,1,0:T(8,128)S(1)} %add.87), channel_id=1, source_target_pairs={{0,24},{4,28},{8,16},{12,20},{16,8},{20,12},{24,0},{28,4},{1,25},{... | collective-permute-start | bytes 196616 | tf_op jit(solution)/shard_map/ppermute | solution.py:174
  62.2 8.0 %collective-permute-start.8 = (f32[4,32,128]{2,1,0:T(8,128)S(1)}, f32[4,32,128]{2,1,0:T(8,128)S(1)}, u32[]{:S(2)}, u32[]{:S(2)}) collective-permute-start(f32[4,32,128]{2,1,0:T(8,128)S(1)} %add.86), channel_id=1, source_target_pairs={{0,16},{4,20},{8,24},{12,28},{16,0},{20,4},{24,8},{28,12},{1,17},{... | collective-permute-start | bytes 196616 | tf_op jit(solution)/shard_map/ppermute | solution.py:174
  65.8 4.8 %collective-permute-start.12 = (f32[4,32,128]{2,1,0:T(8,128)S(1)}, f32[4,32,128]{2,1,0:T(8,128)S(1)}, u32[]{:S(2)}, u32[]{:S(2)}) collective-permute-start(f32[4,32,128]{2,1,0:T(8,128)S(1)} %add.89), channel_id=1, source_target_pairs={{0,8},{4,12},{8,0},{12,4},{16,24},{20,28},{24,16},{28,20},{1,9},{5... | collective-permute-start | bytes 196616 | tf_op jit(solution)/shard_map/ppermute | solution.py:174
  70.6 4.0 %collective-permute-start.14 = (f32[2,32,128]{2,1,0:T(8,128)S(1)}, f32[2,32,128]{2,1,0:T(8,128)S(1)}, u32[]{:S(2)}, u32[]{:S(2)}) collective-permute-start(f32[2,32,128]{2,1,0:T(8,128)S(1)} %get-tuple-element.46), channel_id=1, source_target_pairs={{0,2},{1,3},{2,0},{3,1},{4,6},{5,7},{6,4},{7,5},{8,10},{9,11},{10,... | collective-permute-start | bytes 98312 | tf_op jit(solution)/shard_map/ppermute | solution.py:174
  72.2 3.9 %collective-permute-start.15 = (f32[2,32,128]{2,1,0:T(8,128)S(1)}, f32[2,32,128]{2,1,0:T(8,128)S(1)}, u32[]{:S(2)}, u32[]{:S(2)}) collective-permute-start(f32[2,32,128]{2,1,0:T(8,128)S(1)} %get-tuple-element.47), channel_id=1, source_target_pairs={{0,4},{4,0},{8,12},{12,8},{16,20},{20,16},{24,28},{28,24},{1,5},{5... | collective-permute-start | bytes 98312 | tf_op jit(solution)/shard_map/ppermute | solution.py:174
  72.8 4.8 %collective-permute-start.16 = (f32[2,32,128]{2,1,0:T(8,128)S(1)}, f32[2,32,128]{2,1,0:T(8,128)S(1)}, u32[]{:S(2)}, u32[]{:S(2)}) collective-permute-start(f32[2,32,128]{2,1,0:T(8,128)S(1)} %get-tuple-element.47), channel_id=1, source_target_pairs={{0,6},{1,7},{2,4},{3,5},{4,2},{5,3},{6,0},{7,1},{8,14},{9,15},{10,... | collective-permute-start | bytes 98312 | tf_op jit(solution)/shard_map/ppermute | solution.py:207
  77.6 1.3 %copy-start.1 = (f32[2,32,128]{2,1,0:T(8,128)}, f32[2,32,128]{2,1,0:T(8,128)S(1)}, u32[]{:S(2)}) copy-start(f32[2,32,128]{2,1,0:T(8,128)S(1)} %add_add_fusion.1.refs_0_) | copy-start | bytes 98308
  77.6 1.3 %collective-permute-start.17 = (f32[2,32,128]{2,1,0:T(8,128)S(1)}, f32[2,32,128]{2,1,0:T(8,128)S(1)}, u32[]{:S(2)}, u32[]{:S(2)}) collective-permute-start(f32[2,32,128]{2,1,0:T(8,128)S(1)} %add_add_fusion.1.refs_0_), channel_id=1, source_target_pairs={{0,1},{1,0},{2,3},{3,2},{4,5},{5,4},{6,7},{7,6},{8,9},{9,8},{10,11... | collective-permute-start | bytes 98312 | tf_op jit(solution)/shard_map/ppermute | solution.py:174
  78.9 0.6 copy-start.2

commit v3 on v0

v3 whole, which is shorter than its diff:
```python
import functools
import math

import jax
import jax.numpy as jnp
from jax import lax
from jax.experimental import pallas as pl
from jax.experimental.pallas import tpu as pltpu
from jax.sharding import PartitionSpec as P

NFFT = 256
NF = 128
NB = 32
LANES = 128
PACK = LANES // NB
PITCH = NB + 8
LAST = 2
LATE = 12
CORE_STEP = 2
F32 = jnp.float32
BF16 = jnp.bfloat16
VMEM = pltpu.VMEM
SMEM = pltpu.SMEM


def spectral_table(freq_lines):
    moments = jnp.arange(NFFT, dtype=jnp.int32)
    cycle = freq_lines[:, None] * moments[None, :] % NFFT
    angles = 2.0 * math.pi / NFFT * cycle.astype(jnp.float32)
    window = 0.5 - 0.5 * jnp.cos(2.0 * math.pi / NFFT * moments.astype(jnp.float32))
    window = window / jnp.sqrt(jnp.sum(window * window))
    return jnp.concatenate(
        [window[None, :] * jnp.cos(angles), -window[None, :] * jnp.sin(angles)], axis=0
    )


def split(x):
    high = x.astype(BF16)
    return high, (x - high.astype(F32)).astype(BF16)


def transform(halves, series, starts_ref, numbers, spec_ref):
    block = jnp.concatenate([series[pl.ds(starts_ref[b], NFFT), :] for b in numbers], axis=1)
    x_high, x_low = split(block)
    both = jnp.dot(halves[...], x_high, preferred_element_type=F32)
    out = jnp.dot(halves[:NFFT], x_low, preferred_element_type=F32)
    out = out + both[:NFFT] + both[NFFT:]
    power = []
    for i, b in enumerate(numbers):
        part = out[:, i * LANES : (i + 1) * LANES]
        spec_ref[pl.ds(b, 2 * NF, stride=PITCH), :] = part
        square = part * part
        power.append(square[:NF] + square[NF:])
    return (power[0] + power[1]) * (1.0 / NB)


def split_table(table_ref, halves):
    high, low = split(table_ref[...])
    halves[:NFFT] = high
    halves[NFFT:] = low


def gram(rows_of, line):
    rows = PACK * NB
    row = lax.broadcasted_iota(jnp.int32, (rows, LANES), 0) % NB
    lane = lax.broadcasted_iota(jnp.int32, (rows, LANES), 1)
    spectra = jnp.concatenate(
        [
            jnp.concatenate([rows_of(part, line + i) for i in range(PACK)], axis=0)
            for part in range(2)
        ],
        axis=1,
    )
    high, low = split(spectra)
    turned = jnp.concatenate([high[:, LANES:], -high[:, :LANES]], axis=1)
    both = lax.dot_general(
        jnp.concatenate([high, low], axis=0),
        jnp.concatenate([high, turned], axis=0),
        (((1,), (1,)), ((), ())),
        preferred_element_type=F32,
    )
    cross = both[rows:]
    mirrored = jnp.where(row >= lane % NB, cross[:, :LANES], -cross[:, LANES:])
    full = both[:rows] + cross
    full = jnp.where(row <= lane % NB, full[:, :LANES], full[:, LANES:]) + mirrored.T
    packed = full[:NB]
    for i in range(1, PACK):
        packed = jnp.where(lane[:NB] // NB == i, full[i * NB : (i + 1) * NB], packed)
    return packed


def line_rows(spec_ref, part, line):
    return spec_ref[pl.ds(pl.multiple_of((part * NF + line) * PITCH, 8), NB), :]


def cut_kernel(order, snapshots_ref, *refs):
    me = lax.axis_index("tm")
    pieces, sems = refs[:-1], refs[-1]
    copies = [
        pltpu.make_async_copy(
            snapshots_ref.at[:, pl.ds(pl.multiple_of((me ^ k) * LANES, LANES), LANES)],
            piece,
            sems.at[i],
        )
        for i, (k, piece) in enumerate(zip(order, pieces))
    ]
    for copy in copies:
        copy.start()
    for copy in copies:
        copy.wait()


def cut(order, snapshots):
    rows = snapshots.shape[0]
    return pl.pallas_call(
        functools.partial(cut_kernel, order),
        name="cut",
        in_specs=[pl.BlockSpec(memory_space=pltpu.HBM)],
        out_specs=[pl.BlockSpec(memory_space=VMEM)] * len(order),
        out_shape=[jax.ShapeDtypeStruct((rows, LANES), F32)] * len(order),
        scratch_shapes=[pltpu.SemaphoreType.DMA((len(order),))],
        compiler_params=pltpu.CompilerParams(vmem_limit_bytes=8 << 20),
    )(snapshots)


def early_kernel(rows, base_ref, where_ref, starts_ref, table_ref, *refs):
    pieces, (series, spec_ref, power_ref, halves) = refs[:-4], refs[-4:]
    for k, piece in enumerate(pieces):
        series[pl.ds(pl.multiple_of(where_ref[k] * rows, 8), rows), :] = piece[...]
    split_table(table_ref, halves)
    power_ref[...] = jnp.zeros_like(power_ref)

    def step(pair, carry):
        numbers = [2 * pair + i for i in range(2)]
        numbers = [jnp.where(b < base_ref[0], b, b + LATE) for b in numbers]
        power_ref[...] += transform(halves, series, starts_ref, numbers, spec_ref)
        return carry

    lax.fori_loop(0, (NB - LATE) // 2, step, 0, unroll=5)


def early(base, where, starts, table, pieces):
    rows = pieces[0].shape[0]
    smem, vmem = pl.BlockSpec(memory_space=SMEM), pl.BlockSpec(memory_space=VMEM)
    return pl.pallas_call(
        functools.partial(early_kernel, rows),
        name="early",
        in_specs=[smem] * 3 + [vmem] * (1 + len(pieces)),
        out_specs=[vmem] * 4,
        out_shape=[
            jax.ShapeDtypeStruct(((len(pieces) + LAST) * rows, LANES), F32),
            jax.ShapeDtypeStruct((2 * NF * PITCH, LANES), F32),
            jax.ShapeDtypeStruct((NF, LANES), F32),
            jax.ShapeDtypeStruct((2 * NFFT, NFFT), BF16),
        ],
        compiler_params=pltpu.CompilerParams(vmem_limit_bytes=20 << 20),
        cost_estimate=pl.CostEstimate(
            flops=6 * 2 * NF * NFFT * (NB - LATE) * LANES, bytes_accessed=4 << 20, transcendentals=0
        ),
    )(base, where, starts, table, *pieces)


def late_kernel(
    base_ref, where_ref, core_ref, firsts_ref, starts_ref,
    halves, series_ref, spec_ref, early_power_ref, *refs,
):
    pieces, (power_ref, sent_ref) = refs[:LAST], refs[LAST : LAST + 2]
    kept_refs, (series, late_spec) = refs[LAST + 2 : -2], refs[-2:]
    rows, base = pieces[0].shape[0], base_ref[0]
    series[...] = series_ref[...]
    for k, piece in enumerate(pieces):
        series[pl.ds(pl.multiple_of(where_ref[k] * rows, 8), rows), :] = piece[...]
    power = early_power_ref[...]
    for pair in range(LATE // 2):
        numbers = [base + 2 * pair + i for i in range(2)]
        power = power + transform(halves, series, starts_ref, numbers, late_spec)
    power_ref[...] = power
    block = lax.broadcasted_iota(jnp.int32, (NB, LANES), 0)
    is_late = (block >= base) & (block < base + LATE)

    def rows_of(part, line):
        return jnp.where(
            is_late, line_rows(late_spec, part, line), line_rows(spec_ref, part, line)
        )

    core = core_ref[0]
    half = len(kept_refs)
    for n, kept_ref in enumerate(kept_refs):
        for i in range(half):
            group = firsts_ref[n] + (i // CORE_STEP) * 2 * CORE_STEP + i % CORE_STEP
            kept_ref[i] = gram(rows_of, (group + core * CORE_STEP) * PACK)
            sent_ref[n * half + i] = gram(rows_of, (group + (1 - core) * CORE_STEP) * PACK)


def late(base, where, core, firsts, starts, halves, series, spec, power, pieces):
    quarters = firsts.shape[0]
    half = NF // PACK // quarters // 2
    smem, vmem = pl.BlockSpec(memory_space=SMEM), pl.BlockSpec(memory_space=VMEM)
    return pl.pallas_call(
        late_kernel,
        name="late",
        in_specs=[smem] * 5 + [vmem] * (4 + len(pieces)),
        out_specs=[vmem] * (2 + quarters),
        out_shape=[
            jax.ShapeDtypeStruct((NF, LANES), F32),
            jax.ShapeDtypeStruct((quarters * half, NB, LANES), F32),
        ]
        + [jax.ShapeDtypeStruct((half, NB, LANES), F32)] * quarters,
        scratch_shapes=[VMEM(series.shape, F32), VMEM(spec.shape, F32)],
        compiler_params=pltpu.CompilerParams(vmem_limit_bytes=28 << 20),
        cost_estimate=pl.CostEstimate(
            flops=NF // PACK * 6 * LANES * 4 * LANES * LANES * 2,
            bytes_accessed=8 << 20,
            transcendentals=0,
        ),
    )(base, where, core, firsts, starts, halves, series, spec, power, *pieces)


def whole_kernel(starts_ref, table_ref, series_ref, power_ref, packed_ref, halves, spec):
    split_table(table_ref, halves)
    power_ref[...] = jnp.zeros_like(power_ref)

    def step(pair, carry):
        numbers = [2 * pair + i for i in range(2)]
        power_ref[...] += transform(halves, series_ref, starts_ref, numbers, spec)
        return carry

    lax.fori_loop(0, NB // 2, step, 0, unroll=4)

    def step_gram(group, carry):
        packed_ref[group] = gram(functools.partial(line_rows, spec), group * PACK)
        return carry

    lax.fori_loop(0, NF // PACK, step_gram, 0, unroll=8)


def whole(starts, table, series):
    smem, vmem = pl.BlockSpec(memory_space=SMEM), pl.BlockSpec(memory_space=VMEM)
    return pl.pallas_call(
        whole_kernel,
        name="whole",
        in_specs=[smem, vmem, vmem],
        out_specs=[vmem] * 2,
        out_shape=[
            jax.ShapeDtypeStruct((NF, LANES), F32),
            jax.ShapeDtypeStruct((NF // PACK, NB, LANES), F32),
        ],
        scratch_shapes=[VMEM((2 * NFFT, NFFT), BF16), VMEM((2 * NF * PITCH, LANES), F32)],
        compiler_params=pltpu.CompilerParams(vmem_limit_bytes=28 << 20),
    )(starts, table, series)


def unpack_kernel(factor, order_ref, *refs):
    packed_refs, out_ref = refs[:-1], refs[-1]
    row = lax.broadcasted_iota(jnp.int32, (NB, NB), 0)
    column = lax.broadcasted_iota(jnp.int32, (NB, NB), 1)
    for n, packed_ref in enumerate(packed_refs):
        count = packed_ref.shape[0]
        for j in range(count):
            packed = packed_ref[j] * factor
            turned = packed.T
            line = (order_ref[n] * count + j) * PACK
            for i in range(PACK):
                here = packed[:, i * NB : (i + 1) * NB]
                there = turned[i * NB : (i + 1) * NB, :]
                out_ref[0, line + i] = jnp.where(row <= column, here, there)
                out_ref[1, line + i] = jnp.where(
                    row > column, here, jnp.where(row < column, -there, 0.0)
                )


def unpack(parts, order, factor):
    lines = sum(p.shape[0] for p in parts) * PACK
    return pl.pallas_call(
        functools.partial(unpack_kernel, factor),
        name="unpack",
        in_specs=[pl.BlockSpec(memory_space=SMEM)]
        + [pl.BlockSpec(memory_space=VMEM)] * len(parts),
        out_specs=pl.BlockSpec(memory_space=VMEM),
        out_shape=jax.ShapeDtypeStruct((2, lines, NB, NB), F32),
        compiler_params=pltpu.CompilerParams(vmem_limit_bytes=8 << 20),
    )(order, *parts)


def swap(value, axis, bits):
    return lax.ppermute(value, axis, [(i, i ^ bits) for i in range(lax.axis_size(axis))])


def spread_small(snapshots, starts, table):
    me = lax.axis_index("tm")
    core = lax.axis_index("space") % 2
    z, x = me // 2, me % 2
    order = (4, 2, 1, 5, 3, 6, 7)
    rows = snapshots.shape[0]
    *pieces, own = cut((*order, 0), snapshots)
    pieces = [swap(p, "tm", k) for p, k in zip(pieces, order)]
    pieces, last = pieces[:-LAST] + [own], pieces[-LAST:]
    where = jnp.stack([me ^ k for k in (*order[:-LAST], 0)])
    before = jnp.sum((starts + (NFFT - 1) < (z ^ 3) * LAST * rows).astype(jnp.int32))
    base = jnp.minimum(before, NB - LATE).reshape(1)
    series, spec, power, halves = early(base, where, starts, table, pieces)
    groups = NF // PACK // 4
    away = (2, 1, 3)
    firsts = jnp.stack([(z ^ j) * groups for j in (*away, 0)])
    power, sent, *kept = late(
        base, jnp.stack([me ^ k for k in order[-LAST:]]), core.reshape(1), firsts, starts,
        halves, series, spec, power, last,
    )
    theirs = swap(sent, "space", 1)
    half = groups // 2
    terms = [k + theirs[n * half : (n + 1) * half] for n, k in enumerate(kept)]
    terms = [swap(t, "tm", 2 * j) for j, t in zip(away, terms)] + terms[-1:]
    lower, upper = (sum(t[i * half // 2 : (i + 1) * half // 2] for t in terms) for i in range(2))
    mine, other = jnp.where(x == 0, lower, upper), jnp.where(x == 0, upper, lower)
    from_y = swap(mine, "space", 2)
    from_x = swap(other, "tm", 1)
    from_xy = lax.ppermute(
        other,
        ("tm", "space"),
        [(i * 4 + s, (i ^ 1) * 4 + (s ^ 2)) for i in range(8) for s in range(4)],
    )
    mine = mine + from_y + from_x + from_xy
    return power, [mine, swap(mine, "space", 1)], jnp.stack([core, 1 - core])


def spread_any(snapshots, starts, table):
    groups = lax.axis_size("tm")
    arranged = snapshots.reshape(snapshots.shape[0], groups, -1)
    series = lax.all_to_all(arranged, "tm", split_axis=1, concat_axis=0, tiled=True)[:, 0, :]
    power, packed = whole(starts, table, series)
    own = lax.psum_scatter(packed, "tm", scatter_dimension=0, tiled=True)
    return power, [lax.psum(own, "space")], jnp.zeros((1,), jnp.int32)


def body(snapshots, starts, freq_lines):
    groups = lax.axis_size("tm")
    spaces = lax.axis_size("space")
    table = spectral_table(freq_lines)
    spread = spread_small if (groups, spaces) == (8, 4) else spread_any
    power_density, parts, order = spread(snapshots, starts, table)
    return power_density, unpack(parts, order, 1.0 / (NB * snapshots.shape[1] * spaces))


def solution(mesh):
    placed = (P("tm", "space"), P(), P())
    return jax.shard_map(
        body,
        mesh=mesh,
        in_specs=placed,
        out_specs=(P(None, ("space", "tm")), P(None, "tm", None, None)),
        check_vma=False,
    )
```

time: 277 us -> 79.5 us (0.29)
  waiting for transfers between devices: 176 us -> 28.9 us
  local copies, waits for them, and re-layouts: 40.6 us -> 1.69 us
  matrix products: 33.9 us -> 0 us
  starting transfers between devices: 7.42 us -> 34.2 us
  between operations: 14.8 us -> 2.03 us
  Pallas kernels: 0 us -> 8.54 us
    psum x1 -> x0, waiting for transfers between devices: 128 us -> none  [body(): summed = lax.psum(own_gram, ('tm', 'space'))]
    all_to_all x1 -> x0, waiting for transfers between devices: 47.6 us -> none  [body(): lax.all_to_all(arranged, 'tm', split_axis=1, concat_axis=0, tiled=True)]
    ppermute x0 -> x15, starting transfers between devices: none -> 34.2 us  [the longest x14 32.6 us: swap(): lax.ppermute(value, axis, [(i, i ^ bits) for i in range(lax.axis_size(axi...]
    dot_general x5 -> x0, matrix products: 33.9 us -> none  [the longest x1 9.72 us: local_terms(): jnp.einsum('fbp,fcp->fbc', real_part, real_part, precision=highest)]
    gather x1 -> x0, local copies, waits for them, and re-layouts: 29.4 us -> none  [block_spectra(): blocks = series[offsets]]
    ppermute x0 -> x15, waiting for transfers between devices: none -> 28.9 us  [the longest x14 27.5 us: swap(): lax.ppermute(value, axis, [(i, i ^ bits) for i in range(lax.axis_size(axi...]
    pallas_call x0 -> x4, Pallas kernels: none -> 8.54 us  [the longest x1 3.89 us: late(): pl.pallas_call(late_kernel, name='late', in_specs=[smem] * 5 + [vmem] * (...]
    all_to_all x1 -> x0, starting transfers between devices: 7.38 us -> none  [body(): lax.all_to_all(arranged, 'tm', split_axis=1, concat_axis=0, tiled=True)]
  transfers between devices with their start and end apart: 2 -> 15, of which waited for: 2 -> 12; matrix products, arithmetic and copies ran while one was open for 1% -> 5% of each run, Pallas kernels for 0% -> 3%
where the time goes in v3:
time: 79.5 us; the launch traced here: 79.3 us
  starting transfers between devices  34.2 us (43%)
  waiting for transfers between devices  28.9 us (36%)
  Pallas kernels  8.54 us (11%)
  other arithmetic  3.96 us (5%)
  between operations  2.03 us (3%)
  local copies, waits for them, and re-layouts  1.69 us (2%)
    ppermute x14, starting transfers between devices, swap(): lax.ppermute(value, axis, [(i, i ^ bits) for i in range(lax.axis_size(axi...  32.6 us
    ppermute x14, waiting for transfers between devices, swap(): lax.ppermute(value, axis, [(i, i ^ bits) for i in range(lax.axis_size(axi...  27.5 us
    pallas_call x1, Pallas kernels, late(): pl.pallas_call(late_kernel, name='late', in_specs=[smem] * 5 + [vmem] * (...  3.89 us
    pallas_call x1, Pallas kernels, early(): pl.pallas_call(functools.partial(early_kernel, rows), name='early', in_sp...  2.73 us
    unnamed x6, local copies, waits for them, and re-layouts  1.61 us
  transfers between devices with their start and end apart: 15, of which 12 were waited for; matrix products, arithmetic and copies ran while one was open for 5% of the time, Pallas kernels for 3%

profile of v3, /device:TPU:0, one launch (start us, length us, event | category | flops | bytes accessed | tf_op | source)
XLA Modules:
  0.0 79.3 jit_solution(9247505419217732512)
XLA Ops:
  0.6 0.0 copy-start
  0.6 1.6 %copy-done = f32[528,1024]{1,0:T(8,128)S(1)} copy-done((f32[528,1024]{1,0:T(8,128)S(1)}, f32[528,1024]{1,0:T(8,128)}, u32[]{:S(2)}) %copy-start) | copy-done | bytes 2162712
  2.2 0.0 copy-start.2
  2.2 0.0 copy-start.1
  2.2 0.4 cut.1
  2.6 4.1 %collective-permute-start = (f32[528,128]{1,0:T(8,128)S(1)}, f32[528,128]{1,0:T(8,128)S(1)}, u32[]{:S(2)}, u32[]{:S(2)}) collective-permute-start(f32[528,128]{1,0:T(8,128)S(1)} %get-tuple-element.20), channel_id=1, source_target_pairs={{0,16},{4,20},{8,24},{12,28},{16,0},{20,4},{24,8},{28,12},{1,17},{... | collective-permute-start | bytes 811016 | tf_op jit(solution)/shard_map/ppermute | solution.py:286
  6.7 1.6 %collective-permute-start.1 = (f32[528,128]{1,0:T(8,128)S(1)}, f32[528,128]{1,0:T(8,128)S(1)}, u32[]{:S(2)}, u32[]{:S(2)}) collective-permute-start(f32[528,128]{1,0:T(8,128)S(1)} %get-tuple-element.21), channel_id=1, source_target_pairs={{0,8},{4,12},{8,0},{12,4},{16,24},{20,28},{24,16},{28,20},{1,9},{5... | collective-permute-start | bytes 811016 | tf_op jit(solution)/shard_map/ppermute | solution.py:286
  8.3 1.5 %collective-permute-start.2 = (f32[528,128]{1,0:T(8,128)S(1)}, f32[528,128]{1,0:T(8,128)S(1)}, u32[]{:S(2)}, u32[]{:S(2)}) collective-permute-start(f32[528,128]{1,0:T(8,128)S(1)} %get-tuple-element.22), channel_id=1, source_target_pairs={{0,4},{4,0},{8,12},{12,8},{16,20},{20,16},{24,28},{28,24},{1,5},{5... | collective-permute-start | bytes 811016 | tf_op jit(solution)/shard_map/ppermute | solution.py:286
  9.8 0.3 collective-permute-start.3
  10.1 1.4 %collective-permute-start.4 = (f32[528,128]{1,0:T(8,128)S(1)}, f32[528,128]{1,0:T(8,128)S(1)}, u32[]{:S(2)}, u32[]{:S(2)}) collective-permute-start(f32[528,128]{1,0:T(8,128)S(1)} %get-tuple-element.24), channel_id=1, source_target_pairs={{0,12},{4,8},{8,4},{12,0},{16,28},{20,24},{24,20},{28,16},{1,13},{... | collective-permute-start | bytes 811016 | tf_op jit(solution)/shard_map/ppermute | solution.py:286
  11.5 0.6 multiply_reduce_fusion
  12.9 0.0 copy-done.2
  12.9 1.3 %cosine_multiply_fusion = (f32[128,256]{1,0:T(8,128)}, f32[128,256]{1,0:T(8,128)}) fusion(s32[128]{0:T(128)S(1)} %copy-done.2, f32[256]{0:T(256)S(1)} %get-tuple-element.47, f32[256]{0:T(256)S(1)} %get-tuple-element.48), kind=kLoop, calls=%fused_computation.8 | loop fusion | flops 524288 | bytes 264704 | tf_op jit(solution)/shard_map/mul | solution.py:33
  14.2 0.0 copy-done.1
  14.2 0.7 fusion.7
  14.9 0.1 pad_add_fusion.where_ref
  15.6 0.1 stack.66.where_ref
  15.6 5.1 %collective-permute-done.refs_0_ = f32[528,128]{1,0:T(8,128)S(1)} collective-permute-done((f32[528,128]{1,0:T(8,128)S(1)}, f32[528,128]{1,0:T(8,128)S(1)}, u32[]{:S(2)}, u32[]{:S(2)}) %collective-permute-start) | collective-permute-done | bytes 270368 | tf_op jit(solution)/shard_map/ppermute | solution.py:286
  20.8 3.1 %collective-permute-start.5 = (f32[528,128]{1,0:T(8,128)S(1)}, f32[528,128]{1,0:T(8,128)S(1)}, u32[]{:S(2)}, u32[]{:S(2)}) collective-permute-start(f32[528,128]{1,0:T(8,128)S(1)} %get-tuple-element.30), channel_id=1, source_target_pairs={{0,24},{4,28},{8,16},{12,20},{16,8},{20,12},{24,0},{28,4},{1,25},{... | collective-permute-start | bytes 811016 | tf_op jit(solution)/shard_map/ppermute | solution.py:286
  23.9 0.0 collective-permute-done.1.refs_1_
  23.9 5.9 %collective-permute-start.6 = (f32[528,128]{1,0:T(8,128)S(1)}, f32[528,128]{1,0:T(8,128)S(1)}, u32[]{:S(2)}, u32[]{:S(2)}) collective-permute-start(f32[528,128]{1,0:T(8,128)S(1)} %get-tuple-element.31), channel_id=1, source_target_pairs={{0,28},{4,24},{8,20},{12,16},{16,12},{20,8},{24,4},{28,0},{1,29},{... | collective-permute-start | bytes 811016 | tf_op jit(solution)/shard_map/ppermute | solution.py:286
  29.7 0.1 pad_add_fusion.1.firsts_ref
  29.8 1.0 %pad_maximum_fusion.table_ref = f32[256,256]{1,0:T(8,128)S(1)} fusion(f32[128,256]{1,0:T(8,128)} %get-tuple-element.46, f32[128,256]{1,0:T(8,128)} %get-tuple-element.45), kind=kLoop, calls=%fused_computation | loop fusion | flops 65536 | bytes 524288 | tf_op jit(solution)/shard_map/concatenate | solution.py:32
  30.8 0.0 collective-permute-done.2.refs_2_
  30.8 2.2 %collective-permute-done.3.refs_3_ = f32[528,128]{1,0:T(8,128)S(1)} collective-permute-done((f32[528,128]{1,0:T(8,128)S(1)}, f32[528,128]{1,0:T(8,128)S(1)}, u32[]{:S(2)}, u32[]{:S(2)}) %collective-permute-start.3) | collective-permute-done | bytes 270368 | tf_op jit(solution)/shard_map/ppermute | solution.py:286
  33.0 0.0 collective-permute-done.4.refs_4_
  33.0 2.7 %early.1 = (f32[4224,128]{1,0:T(8,128)S(1)}, f32[10240,128]{1,0:T(8,128)S(1)}, f32[128,128]{1,0:T(8,128)S(1)}, bf16[512,256]{1,0:T(8,128)(2,1)S(1)}) custom-call(s32[1]{0:T(128)} %bitcast.base_ref, s32[6]{0:T(128)S(1)} %stack.66.where_ref, s32[32]{0:T(128)S(1)} %copy-done.1, f32[256,256]{1,0:T(8,128)S(1)} %pad_maximum_fusion.table_ref, ...), custom_call_target="tpu_custom_call" | custom-call | flops 1006632960 | bytes 4194304 | tf_op jit(solution)/shard_map/early/pallas_call | solution.py:145
  35.7 4.0 %collective-permute-done.5.refs_0_ = f32[528,128]{1,0:T(8,128)S(1)} collective-permute-done((f32[528,128]{1,0:T(8,128)S(1)}, f32[528,128]{1,0:T(8,128)S(1)}, u32[]{:S(2)}, u32[]{:S(2)}) %collective-permute-start.5) | collective-permute-done | bytes 270368 | tf_op jit(solution)/shard_map/ppermute | solution.py:286
  39.8 5.6 %collective-permute-done.6.refs_1_ = f32[528,128]{1,0:T(8,128)S(1)} collective-permute-done((f32[528,128]{1,0:T(8,128)S(1)}, f32[528,128]{1,0:T(8,128)S(1)}, u32[]{:S(2)}, u32[]{:S(2)}) %collective-permute-start.6) | collective-permute-done | bytes 270368 | tf_op jit(solution)/shard_map/ppermute | solution.py:286
  45.4 3.9 %late.1 = (f32[128,128]{1,0:T(8,128)}, f32[16,32,128]{2,1,0:T(8,128)S(1)}, f32[4,32,128]{2,1,0:T(8,128)S(1)}, f32[4,32,128]{2,1,0:T(8,128)S(1)}, f32[4,32,128]{2,1,0:T(8,128)S(1)}, /*index=5*/f32[4,32,128]{2,1,0:T(8,128)S(1)}) custom-call(s32[1]{0:T(128)} %bitcast.base_ref, s32[2]{0:T(128)S(1)} %pad_add_fusion.where_ref, s32[1]{0:T(128)} %bitcast.3.core_ref, ...), custom_call_target="tpu_custom_call" | custom-call | flops 3221225472 | bytes 8388608 | tf_op jit(solution)/shard_map/late/pallas_call | solution.py:199
  49.3 0.0 collective-permute-start.7
  49.3 1.5 %collective-permute-done.7 = f32[16,32,128]{2,1,0:T(8,128)S(1)} collective-permute-done((f32[16,32,128]{2,1,0:T(8,128)S(1)}, f32[16,32,128]{2,1,0:T(8,128)S(1)}, u32[]{:S(2)}, u32[]{:S(2)}) %collective-permute-start.7) | collective-permute-done | bytes 262176 | tf_op jit(solution)/shard_map/ppermute | solution.py:286
  50.9 12.1 %collective-permute-start.8 = (f32[4,32,128]{2,1,0:T(8,128)S(1)}, f32[4,32,128]{2,1,0:T(8,128)S(1)}, u32[]{:S(2)}, u32[]{:S(2)}) collective-permute-start(f32[4,32,128]{2,1,0:T(8,128)S(1)} %get-tuple-element.41), channel_id=1, source_target_pairs={{0,16},{4,20},{8,24},{12,28},{16,0},{20,4},{24,8},{28,12},{1,17},{... | collective-permute-start | bytes 196616 | tf_op jit(solution)/shard_map/ppermute | solution.py:286
  62.9 0.4 collective-permute-start.10
  63.3 0.2 collective-permute-start.9
  63.6 3.4 %collective-permute-done.8 = f32[4,32,128]{2,1,0:T(8,128)S(1)} collective-permute-done((f32[4,32,128]{2,1,0:T(8,128)S(1)}, f32[4,32,128]{2,1,0:T(8,128)S(1)}, u32[]{:S(2)}, u32[]{:S(2)}) %collective-permute-start.8) | collective-permute-done | bytes 65568 | tf_op jit(solution)/shard_map/ppermute | solution.py:286
  67.0 2.4 %collective-permute-done.10 = f32[4,32,128]{2,1,0:T(8,128)S(1)} collective-permute-done((f32[4,32,128]{2,1,0:T(8,128)S(1)}, f32[4,32,128]{2,1,0:T(8,128)S(1)}, u32[]{:S(2)}, u32[]{:S(2)}) %collective-permute-start.10) | collective-permute-done | bytes 65568 | tf_op jit(solution)/shard_map/ppermute | solution.py:286
  69.3 0.1 collective-permute-done.9
  69.5 1.6 %collective-permute-start.13 = (f32[2,32,128]{2,1,0:T(8,128)S(1)}, f32[2,32,128]{2,1,0:T(8,128)S(1)}, u32[]{:S(2)}, u32[]{:S(2)}) collective-permute-start(f32[2,32,128]{2,1,0:T(8,128)S(1)} %broadcast_select_fusion), channel_id=1, source_target_pairs={{0,6},{1,7},{2,4},{3,5},{4,2},{5,3},{6,0},{7,1},{8,14},{9,15},{10,... | collective-permute-start | bytes 98312 | tf_op jit(solution)/shard_map/ppermute | solution.py:317
  71.1 1.5 %collective-permute-start.12 = (f32[2,32,128]{2,1,0:T(8,128)S(1)}, f32[2,32,128]{2,1,0:T(8,128)S(1)}, u32[]{:S(2)}, u32[]{:S(2)}) collective-permute-start(f32[2,32,128]{2,1,0:T(8,128)S(1)} %broadcast_select_fusion), channel_id=1, source_target_pairs={{0,4},{4,0},{8,12},{12,8},{16,20},{20,16},{24,28},{28,24},{1,5},{5... | collective-permute-start | bytes 98312 | tf_op jit(solution)/shard_map/ppermute | solution.py:286
  72.5 0.5 collective-permute-start.11
  73.0 1.4 %collective-permute-done.13 = f32[2,32,128]{2,1,0:T(8,128)S(1)} collective-permute-done((f32[2,32,128]{2,1,0:T(8,128)S(1)}, f32[2,32,128]{2,1,0:T(8,128)S(1)}, u32[]{:S(2)}, u32[]{:S(2)}) %collective-permute-start.13) | collective-permute-done | bytes 32800 | tf_op jit(solution)/shard_map/ppermute | solution.py:317
  74.5 0.5 collective-permute-done.12
  75.0 1.5 %collective-permute-done.11 = f32[2,32,128]{2,1,0:T(8,128)S(1)} collective-permute-done((f32[2,32,128]{2,1,0:T(8,128)S(1)}, f32[2,32,128]{2,1,0:T(8,128)S(1)}, u32[]{:S(2)}, u32[]{:S(2)}) %collective-permute-start.11) | collective-permute-done | bytes 32800 | tf_op jit(solution)/shard_map/ppermute | solution.py:286
  76.5 0.1 collective-permute-start.14
  76.6 0.1 pad_add_fusion.2.order_ref
  76.6 1.1 %collective-permute-done.14.refs_1_ = f32[2,32,128]{2,1,0:T(8,128)S(1)} collective-permute-done((f32[2,32,128]{2,1,0:T(8,128)S(1)}, f32[2,32,128]{2,1,0:T(8,128)S(1)}, u32[]{:S(2)}, u32[]{:S(2)}) %collective-permute-start.14) | collective-permute-done | bytes 32800 | tf_op jit(solution)/shard_map/ppermute | solution.py:286
  77.7 1.5 %unpack.1 = f32[2,16,32,32]{3,2,1,0:T(8,128)} custom-call(s32[2]{0:T(128)S(1)} %pad_add_fusion.2.order_ref, f32[2,32,128]{2,1,0:T(8,128)S(1)} %add_add_fusion.refs_0_, f32[2,32,128]{2,1,0:T(8,128)S(1)} %collective-permute-done.14.refs_1_), custom_call_target="tpu_custom_call" | custom-call | tf_op jit(solution)/shard_map/unpack/pallas_call | solution.py:274
  (5 shorter events, 0.1 us)
Async XLA Ops:
  0.6 1.6 %copy-start = (f32[528,1024]{1,0:T(8,128)S(1)}, f32[528,1024]{1,0:T(8,128)}, u32[]{:S(2)}) copy-start(f32[528,1024]{1,0:T(8,128)} %snapshots_ref.1) | copy-start | bytes 6488068
  2.2 10.6 %copy-start.2 = (s32[128]{0:T(128)S(1)}, s32[128]{0:T(128)}, u32[]{:S(2)}) copy-start(s32[128]{0:T(128)} %param.5) | copy-start | bytes 1540
  2.2 12.0 %copy-start.1 = (s32[32]{0:T(128)S(1)}, s32[32]{0:T(128)}, u32[]{:S(2)}) copy-start(s32[32]{0:T(128)} %starts_ref.3) | copy-start | bytes 388
  2.6 18.1 %collective-permute-start = (f32[528,128]{1,0:T(8,128)S(1)}, f32[528,128]{1,0:T(8,128)S(1)}, u32[]{:S(2)}, u32[]{:S(2)}) collective-permute-start(f32[528,128]{1,0:T(8,128)S(1)} %get-tuple-element.20), channel_id=1, source_target_pairs={{0,16},{4,20},{8,24},{12,28},{16,0},{20,4},{24,8},{28,12},{1,17},{... | collective-permute-start | bytes 811016 | tf_op jit(solution)/shard_map/ppermute | solution.py:286
  6.7 17.1 %collective-permute-start.1 = (f32[528,128]{1,0:T(8,128)S(1)}, f32[528,128]{1,0:T(8,128)S(1)}, u32[]{:S(2)}, u32[]{:S(2)}) collective-permute-start(f32[528,128]{1,0:T(8,128)S(1)} %get-tuple-element.21), channel_id=1, source_target_pairs={{0,8},{4,12},{8,0},{12,4},{16,24},{20,28},{24,16},{28,20},{1,9},{5... | collective-permute-start | bytes 811016 | tf_op jit(solution)/shard_map/ppermute | solution.py:286
  8.3 22.5 %collective-permute-start.2 = (f32[528,128]{1,0:T(8,128)S(1)}, f32[528,128]{1,0:T(8,128)S(1)}, u32[]{:S(2)}, u32[]{:S(2)}) collective-permute-start(f32[528,128]{1,0:T(8,128)S(1)} %get-tuple-element.22), channel_id=1, source_target_pairs={{0,4},{4,0},{8,12},{12,8},{16,20},{20,16},{24,28},{28,24},{1,5},{5... | collective-permute-start | bytes 811016 | tf_op jit(solution)/shard_map/ppermute | solution.py:286
  9.8 23.2 %collective-permute-start.3 = (f32[528,128]{1,0:T(8,128)S(1)}, f32[528,128]{1,0:T(8,128)S(1)}, u32[]{:S(2)}, u32[]{:S(2)}) collective-permute-start(f32[528,128]{1,0:T(8,128)S(1)} %get-tuple-element.23), channel_id=1, source_target_pairs={{0,20},{4,16},{8,28},{12,24},{16,4},{20,0},{24,12},{28,8},{1,21},{... | collective-permute-start | bytes 811016 | tf_op jit(solution)/shard_map/ppermute | solution.py:286
  10.1 22.9 %collective-permute-start.4 = (f32[528,128]{1,0:T(8,128)S(1)}, f32[528,128]{1,0:T(8,128)S(1)}, u32[]{:S(2)}, u32[]{:S(2)}) collective-permute-start(f32[528,128]{1,0:T(8,128)S(1)} %get-tuple-element.24), channel_id=1, source_target_pairs={{0,12},{4,8},{8,4},{12,0},{16,28},{20,24},{24,20},{28,16},{1,13},{... | collective-permute-start | bytes 811016 | tf_op jit(solution)/shard_map/ppermute | solution.py:286
  20.8 19.0 %collective-permute-start.5 = (f32[528,128]{1,0:T(8,128)S(1)}, f32[528,128]{1,0:T(8,128)S(1)}, u32[]{:S(2)}, u32[]{:S(2)}) collective-permute-start(f32[528,128]{1,0:T(8,128)S(1)} %get-tuple-element.30), channel_id=1, source_target_pairs={{0,24},{4,28},{8,16},{12,20},{16,8},{20,12},{24,0},{28,4},{1,25},{... | collective-permute-start | bytes 811016 | tf_op jit(solution)/shard_map/ppermute | solution.py:286
  23.9 21.5 %collective-permute-start.6 = (f32[528,128]{1,0:T(8,128)S(1)}, f32[528,128]{1,0:T(8,128)S(1)}, u32[]{:S(2)}, u32[]{:S(2)}) collective-permute-start(f32[528,128]{1,0:T(8,128)S(1)} %get-tuple-element.31), channel_id=1, source_target_pairs={{0,28},{4,24},{8,20},{12,16},{16,12},{20,8},{24,4},{28,0},{1,29},{... | collective-permute-start | bytes 811016 | tf_op jit(solution)/shard_map/ppermute | solution.py:286
  49.3 1.5 %collective-permute-start.7 = (f32[16,32,128]{2,1,0:T(8,128)S(1)}, f32[16,32,128]{2,1,0:T(8,128)S(1)}, u32[]{:S(2)}, u32[]{:S(2)}) collective-permute-start(f32[16,32,128]{2,1,0:T(8,128)S(1)} %get-tuple-element.34), channel_id=1, source_target_pairs={{0,1},{1,0},{2,3},{3,2},{4,5},{5,4},{6,7},{7,6},{8,9},{9,8},{10,11... | collective-permute-start | bytes 786440 | tf_op jit(solution)/shard_map/ppermute | solution.py:286
  50.9 16.1 %collective-permute-start.8 = (f32[4,32,128]{2,1,0:T(8,128)S(1)}, f32[4,32,128]{2,1,0:T(8,128)S(1)}, u32[]{:S(2)}, u32[]{:S(2)}) collective-permute-start(f32[4,32,128]{2,1,0:T(8,128)S(1)} %get-tuple-element.41), channel_id=1, source_target_pairs={{0,16},{4,20},{8,24},{12,28},{16,0},{20,4},{24,8},{28,12},{1,17},{... | collective-permute-start | bytes 196616 | tf_op jit(solution)/shard_map/ppermute | solution.py:286
  62.9 6.4 %collective-permute-start.10 = (f32[4,32,128]{2,1,0:T(8,128)S(1)}, f32[4,32,128]{2,1,0:T(8,128)S(1)}, u32[]{:S(2)}, u32[]{:S(2)}) collective-permute-start(f32[4,32,128]{2,1,0:T(8,128)S(1)} %get-tuple-element.43), channel_id=1, source_target_pairs={{0,24},{4,28},{8,16},{12,20},{16,8},{20,12},{24,0},{28,4},{1,25},{... | collective-permute-start | bytes 196616 | tf_op jit(solution)/shard_map/ppermute | solution.py:286
  63.3 6.1 %collective-permute-start.9 = (f32[4,32,128]{2,1,0:T(8,128)S(1)}, f32[4,32,128]{2,1,0:T(8,128)S(1)}, u32[]{:S(2)}, u32[]{:S(2)}) collective-permute-start(f32[4,32,128]{2,1,0:T(8,128)S(1)} %get-tuple-element.44), channel_id=1, source_target_pairs={{0,8},{4,12},{8,0},{12,4},{16,24},{20,28},{24,16},{28,20},{1,9},{5... | collective-permute-start | bytes 196616 | tf_op jit(solution)/shard_map/ppermute | solution.py:286
  69.5 5.0 %collective-permute-start.13 = (f32[2,32,128]{2,1,0:T(8,128)S(1)}, f32[2,32,128]{2,1,0:T(8,128)S(1)}, u32[]{:S(2)}, u32[]{:S(2)}) collective-permute-start(f32[2,32,128]{2,1,0:T(8,128)S(1)} %broadcast_select_fusion), channel_id=1, source_target_pairs={{0,6},{1,7},{2,4},{3,5},{4,2},{5,3},{6,0},{7,1},{8,14},{9,15},{10,... | collective-permute-start | bytes 98312 | tf_op jit(solution)/shard_map/ppermute | solution.py:317
  71.1 3.9 %collective-permute-start.12 = (f32[2,32,128]{2,1,0:T(8,128)S(1)}, f32[2,32,128]{2,1,0:T(8,128)S(1)}, u32[]{:S(2)}, u32[]{:S(2)}) collective-permute-start(f32[2,32,128]{2,1,0:T(8,128)S(1)} %broadcast_select_fusion), channel_id=1, source_target_pairs={{0,4},{4,0},{8,12},{12,8},{16,20},{20,16},{24,28},{28,24},{1,5},{5... | collective-permute-start | bytes 98312 | tf_op jit(solution)/shard_map/ppermute | solution.py:286
  72.5 3.9 %collective-permute-start.11 = (f32[2,32,128]{2,1,0:T(8,128)S(1)}, f32[2,32,128]{2,1,0:T(8,128)S(1)}, u32[]{:S(2)}, u32[]{:S(2)}) collective-permute-start(f32[2,32,128]{2,1,0:T(8,128)S(1)} %get-tuple-element.38), channel_id=1, source_target_pairs={{0,2},{1,3},{2,0},{3,1},{4,6},{5,7},{6,4},{7,5},{8,10},{9,11},{10,... | collective-permute-start | bytes 98312 | tf_op jit(solution)/shard_map/ppermute | solution.py:286
  76.5 1.3 %collective-permute-start.14 = (f32[2,32,128]{2,1,0:T(8,128)S(1)}, f32[2,32,128]{2,1,0:T(8,128)S(1)}, u32[]{:S(2)}, u32[]{:S(2)}) collective-permute-start(f32[2,32,128]{2,1,0:T(8,128)S(1)} %add_add_fusion.refs_0_), channel_id=1, source_target_pairs={{0,1},{1,0},{2,3},{3,2},{4,5},{5,4},{6,7},{7,6},{8,9},{9,8},{10,11... | collective-permute-start | bytes 98312 | tf_op jit(solution)/shard_map/ppermute | solution.py:286

commit v4 on v3

--- a/solution.py
+++ b/solution.py
@@ -14,8 +14,8 @@
 LANES = 128
 PACK = LANES // NB
 PITCH = NB + 8
-LAST = 2
-LATE = 12
+LATE = 8
+WINDOW = (LATE - 1) * NFFT // 2 + NFFT // 2 + NFFT + 8
 CORE_STEP = 2
 F32 = jnp.float32
 BF16 = jnp.bfloat16
@@ -39,9 +39,8 @@
     return high, (x - high.astype(F32)).astype(BF16)
 
 
-def transform(halves, series, starts_ref, numbers, spec_ref):
-    block = jnp.concatenate([series[pl.ds(starts_ref[b], NFFT), :] for b in numbers], axis=1)
-    x_high, x_low = split(block)
+def transform(halves, blocks, numbers, spec_ref):
+    x_high, x_low = split(jnp.concatenate(blocks, axis=1))
     both = jnp.dot(halves[...], x_high, preferred_element_type=F32)
     out = jnp.dot(halves[:NFFT], x_low, preferred_element_type=F32)
     out = out + both[:NFFT] + both[NFFT:]
@@ -123,57 +122,60 @@
     )(snapshots)
 
 
-def early_kernel(rows, base_ref, where_ref, starts_ref, table_ref, *refs):
-    pieces, (series, spec_ref, power_ref, halves) = refs[:-4], refs[-4:]
+def early_kernel(rows, base_ref, corner_ref, where_ref, starts_ref, table_ref, *refs):
+    pieces, (window_ref, spec_ref, power_ref, halves, series) = refs[:-5], refs[-5:]
     for k, piece in enumerate(pieces):
         series[pl.ds(pl.multiple_of(where_ref[k] * rows, 8), rows), :] = piece[...]
+    window_ref[...] = series[pl.ds(pl.multiple_of(corner_ref[0], 8), WINDOW), :]
     split_table(table_ref, halves)
     power_ref[...] = jnp.zeros_like(power_ref)
 
     def step(pair, carry):
         numbers = [2 * pair + i for i in range(2)]
         numbers = [jnp.where(b < base_ref[0], b, b + LATE) for b in numbers]
-        power_ref[...] += transform(halves, series, starts_ref, numbers, spec_ref)
+        blocks = [series[pl.ds(starts_ref[b], NFFT), :] for b in numbers]
+        power_ref[...] += transform(halves, blocks, numbers, spec_ref)
         return carry
 
-    lax.fori_loop(0, (NB - LATE) // 2, step, 0, unroll=5)
-
-
-def early(base, where, starts, table, pieces):
+    lax.fori_loop(0, (NB - LATE) // 2, step, 0, unroll=4)
+
+
+def early(base, corner, where, starts, table, pieces):
     rows = pieces[0].shape[0]
     smem, vmem = pl.BlockSpec(memory_space=SMEM), pl.BlockSpec(memory_space=VMEM)
     return pl.pallas_call(
         functools.partial(early_kernel, rows),
         name="early",
-        in_specs=[smem] * 3 + [vmem] * (1 + len(pieces)),
+        in_specs=[smem] * 4 + [vmem] * (1 + len(pieces)),
         out_specs=[vmem] * 4,
         out_shape=[
-            jax.ShapeDtypeStruct(((len(pieces) + LAST) * rows, LANES), F32),
+            jax.ShapeDtypeStruct((WINDOW, LANES), F32),
             jax.ShapeDtypeStruct((2 * NF * PITCH, LANES), F32),
             jax.ShapeDtypeStruct((NF, LANES), F32),
             jax.ShapeDtypeStruct((2 * NFFT, NFFT), BF16),
         ],
+        scratch_shapes=[VMEM(((len(pieces) + 1) * rows, LANES), F32)],
         compiler_params=pltpu.CompilerParams(vmem_limit_bytes=20 << 20),
         cost_estimate=pl.CostEstimate(
             flops=6 * 2 * NF * NFFT * (NB - LATE) * LANES, bytes_accessed=4 << 20, transcendentals=0
         ),
-    )(base, where, starts, table, *pieces)
+    )(base, corner, where, starts, table, *pieces)
 
 
 def late_kernel(
-    base_ref, where_ref, core_ref, firsts_ref, starts_ref,
-    halves, series_ref, spec_ref, early_power_ref, *refs,
+    base_ref, corner_ref, where_ref, core_ref, firsts_ref, starts_ref,
+    halves, window_ref, spec_ref, early_power_ref, piece_ref, power_ref, sent_ref, *refs,
 ):
-    pieces, (power_ref, sent_ref) = refs[:LAST], refs[LAST : LAST + 2]
-    kept_refs, (series, late_spec) = refs[LAST + 2 : -2], refs[-2:]
-    rows, base = pieces[0].shape[0], base_ref[0]
-    series[...] = series_ref[...]
-    for k, piece in enumerate(pieces):
-        series[pl.ds(pl.multiple_of(where_ref[k] * rows, 8), rows), :] = piece[...]
+    kept_refs, (series, late_spec) = refs[:-2], refs[-2:]
+    rows, base = piece_ref.shape[0], base_ref[0]
+    origin = corner_ref[0] - rows
+    series[pl.ds(rows, WINDOW), :] = window_ref[...]
+    series[pl.ds(pl.multiple_of(where_ref[0] * rows - origin, 8), rows), :] = piece_ref[...]
     power = early_power_ref[...]
     for pair in range(LATE // 2):
         numbers = [base + 2 * pair + i for i in range(2)]
-        power = power + transform(halves, series, starts_ref, numbers, late_spec)
+        blocks = [series[pl.ds(starts_ref[b] - origin, NFFT), :] for b in numbers]
+        power = power + transform(halves, blocks, numbers, late_spec)
     power_ref[...] = power
     block = lax.broadcasted_iota(jnp.int32, (NB, LANES), 0)
     is_late = (block >= base) & (block < base + LATE)
@@ -192,28 +194,28 @@
             sent_ref[n * half + i] = gram(rows_of, (group + (1 - core) * CORE_STEP) * PACK)
 
 
-def late(base, where, core, firsts, starts, halves, series, spec, power, pieces):
+def late(base, corner, where, core, firsts, starts, halves, window, spec, power, piece):
     quarters = firsts.shape[0]
     half = NF // PACK // quarters // 2
     smem, vmem = pl.BlockSpec(memory_space=SMEM), pl.BlockSpec(memory_space=VMEM)
     return pl.pallas_call(
         late_kernel,
         name="late",
-        in_specs=[smem] * 5 + [vmem] * (4 + len(pieces)),
+        in_specs=[smem] * 6 + [vmem] * 5,
         out_specs=[vmem] * (2 + quarters),
         out_shape=[
             jax.ShapeDtypeStruct((NF, LANES), F32),
             jax.ShapeDtypeStruct((quarters * half, NB, LANES), F32),
         ]
         + [jax.ShapeDtypeStruct((half, NB, LANES), F32)] * quarters,
-        scratch_shapes=[VMEM(series.shape, F32), VMEM(spec.shape, F32)],
+        scratch_shapes=[VMEM((2 * piece.shape[0] + WINDOW, LANES), F32), VMEM(spec.shape, F32)],
         compiler_params=pltpu.CompilerParams(vmem_limit_bytes=28 << 20),
         cost_estimate=pl.CostEstimate(
             flops=NF // PACK * 6 * LANES * 4 * LANES * LANES * 2,
             bytes_accessed=8 << 20,
             transcendentals=0,
         ),
-    )(base, where, core, firsts, starts, halves, series, spec, power, *pieces)
+    )(base, corner, where, core, firsts, starts, halves, window, spec, power, piece)
 
 
 def whole_kernel(starts_ref, table_ref, series_ref, power_ref, packed_ref, halves, spec):
@@ -222,7 +224,8 @@
 
     def step(pair, carry):
         numbers = [2 * pair + i for i in range(2)]
-        power_ref[...] += transform(halves, series_ref, starts_ref, numbers, spec)
+        blocks = [series_ref[pl.ds(starts_ref[b], NFFT), :] for b in numbers]
+        power_ref[...] += transform(halves, blocks, numbers, spec)
         return carry
 
     lax.fori_loop(0, NB // 2, step, 0, unroll=4)
@@ -250,36 +253,47 @@
     )(starts, table, series)
 
 
-def unpack_kernel(factor, order_ref, *refs):
-    packed_refs, out_ref = refs[:-1], refs[-1]
+def unpack_kernel(factor, order_ref, packed_ref, *refs):
+    out_ref, matrices, sem = refs[-3:]
     row = lax.broadcasted_iota(jnp.int32, (NB, NB), 0)
     column = lax.broadcasted_iota(jnp.int32, (NB, NB), 1)
-    for n, packed_ref in enumerate(packed_refs):
-        count = packed_ref.shape[0]
-        for j in range(count):
-            packed = packed_ref[j] * factor
-            turned = packed.T
-            line = (order_ref[n] * count + j) * PACK
-            for i in range(PACK):
-                here = packed[:, i * NB : (i + 1) * NB]
-                there = turned[i * NB : (i + 1) * NB, :]
-                out_ref[0, line + i] = jnp.where(row <= column, here, there)
-                out_ref[1, line + i] = jnp.where(
-                    row > column, here, jnp.where(row < column, -there, 0.0)
-                )
+    count = packed_ref.shape[0]
+    for j in range(count):
+        packed = packed_ref[j] * factor
+        turned = packed.T
+        for i in range(PACK):
+            here = packed[:, i * NB : (i + 1) * NB]
+            there = turned[i * NB : (i + 1) * NB, :]
+            matrices[0, j * PACK + i] = jnp.where(row <= column, here, there)
+            matrices[1, j * PACK + i] = jnp.where(
+                row > column, here, jnp.where(row < column, -there, 0.0)
+            )
+    lines = count * PACK
+    copy = pltpu.make_async_copy(
+        matrices, out_ref.at[:, pl.ds(order_ref[0] * lines, lines)], sem
+    )
+    copy.start()
+    copy.wait()
 
 
 def unpack(parts, order, factor):
-    lines = sum(p.shape[0] for p in parts) * PACK
-    return pl.pallas_call(
-        functools.partial(unpack_kernel, factor),
-        name="unpack",
-        in_specs=[pl.BlockSpec(memory_space=SMEM)]
-        + [pl.BlockSpec(memory_space=VMEM)] * len(parts),
-        out_specs=pl.BlockSpec(memory_space=VMEM),
-        out_shape=jax.ShapeDtypeStruct((2, lines, NB, NB), F32),
-        compiler_params=pltpu.CompilerParams(vmem_limit_bytes=8 << 20),
-    )(order, *parts)
+    lines = parts[0].shape[0] * PACK
+    out = []
+    for n, part in enumerate(parts):
+        out = [
+            pl.pallas_call(
+                functools.partial(unpack_kernel, factor),
+                name="unpack",
+                in_specs=[pl.BlockSpec(memory_space=SMEM), pl.BlockSpec(memory_space=VMEM)]
+                + [pl.BlockSpec(memory_space=pl.ANY)] * len(out),
+                out_specs=pl.BlockSpec(memory_space=pl.ANY),
+                out_shape=jax.ShapeDtypeStruct((2, len(parts) * lines, NB, NB), F32),
+                input_output_aliases={2: 0} if out else {},
+                scratch_shapes=[VMEM((2, lines, NB, NB), F32), pltpu.SemaphoreType.DMA],
+                compiler_params=pltpu.CompilerParams(vmem_limit_bytes=8 << 20),
+            )(order[n].reshape(1), part, *out)
+        ]
+    return out[0]
 
 
 def swap(value, axis, bits):
@@ -294,17 +308,20 @@
     rows = snapshots.shape[0]
     *pieces, own = cut((*order, 0), snapshots)
     pieces = [swap(p, "tm", k) for p, k in zip(pieces, order)]
-    pieces, last = pieces[:-LAST] + [own], pieces[-LAST:]
-    where = jnp.stack([me ^ k for k in (*order[:-LAST], 0)])
-    before = jnp.sum((starts + (NFFT - 1) < (z ^ 3) * LAST * rows).astype(jnp.int32))
-    base = jnp.minimum(before, NB - LATE).reshape(1)
-    series, spec, power, halves = early(base, where, starts, table, pieces)
+    pieces, last = pieces[:-1] + [own], pieces[-1]
+    where = jnp.stack([me ^ k for k in (*order[:-1], 0)])
+    late_part = me ^ order[-1]
+    before = jnp.sum((starts + (NFFT - 1) < late_part * rows).astype(jnp.int32))
+    base = jnp.minimum(before, NB - LATE)
+    corner = jnp.minimum(starts[base] // 8 * 8, lax.axis_size("tm") * rows - WINDOW).reshape(1)
+    base = base.reshape(1)
+    window, spec, power, halves = early(base, corner, where, starts, table, pieces)
     groups = NF // PACK // 4
     away = (2, 1, 3)
     firsts = jnp.stack([(z ^ j) * groups for j in (*away, 0)])
     power, sent, *kept = late(
-        base, jnp.stack([me ^ k for k in order[-LAST:]]), core.reshape(1), firsts, starts,
-        halves, series, spec, power, last,
+        base, corner, late_part.reshape(1), core.reshape(1), firsts, starts,
+        halves, window, spec, power, last,
     )
     theirs = swap(sent, "space", 1)
     half = groups // 2
@@ -320,7 +337,7 @@
         [(i * 4 + s, (i ^ 1) * 4 + (s ^ 2)) for i in range(8) for s in range(4)],
     )
     mine = mine + from_y + from_x + from_xy
-    return power, [mine, swap(mine, "space", 1)], jnp.stack([core, 1 - core])
+    return power, [mine, swap(mine, "space", 1)], [core, 1 - core]
 
 
 def spread_any(snapshots, starts, table):
@@ -329,7 +346,7 @@
     series = lax.all_to_all(arranged, "tm", split_axis=1, concat_axis=0, tiled=True)[:, 0, :]
     power, packed = whole(starts, table, series)
     own = lax.psum_scatter(packed, "tm", scatter_dimension=0, tiled=True)
-    return power, [lax.psum(own, "space")], jnp.zeros((1,), jnp.int32)
+    return power, [lax.psum(own, "space")], [jnp.int32(0)]
 
 
 def body(snapshots, starts, freq_lines):

time: 79.5 us -> 78.3 us (0.985)
  waiting for transfers between devices: 28.9 us -> 20 us
  between operations: 2.03 us -> 4.85 us
  local copies, waits for them, and re-layouts: 1.69 us -> 3.67 us
  starting transfers between devices: 34.2 us -> 35.5 us
  other arithmetic: 3.96 us -> 5.12 us
    ppermute x14, waiting for transfers between devices: 27.5 us -> 18.8 us  [swap(): lax.ppermute(value, axis, [(i, i ^ bits) for i in range(lax.axis_size(axi...]
    dynamic_slice x0 -> x1, local copies, waits for them, and re-layouts: none -> 1.32 us  [spread_small(): starts[base] // 8 * 8]
    ppermute x1, starting transfers between devices: 1.56 us -> 2.46 us  [spread_small(): lax.ppermute(other, ('tm', 'space'), [(i * 4 + s, (i ^ 1) * 4 + (s ^ 2))...]
    pallas_call x1 -> x2, Pallas kernels: 1.54 us -> 1.72 us  [unpack(): pl.pallas_call(functools.partial(unpack_kernel, factor), name='unpack', i...]
  transfers between devices with their start and end apart: 15 -> 15, of which waited for: 12 -> 10; matrix products, arithmetic and copies ran while one was open for 5% -> 8% of each run, Pallas kernels for 3% -> 5%
where the time goes in v4:
time: 78.3 us; the launch traced here: 78.1 us
  starting transfers between devices  35.5 us (45%)
  waiting for transfers between devices  20 us (26%)
  Pallas kernels  8.88 us (11%)
  other arithmetic  5.12 us (7%)
  between operations  4.85 us (6%)
  local copies, waits for them, and re-layouts  3.67 us (5%)
    ppermute x14, starting transfers between devices, swap(): lax.ppermute(value, axis, [(i, i ^ bits) for i in range(lax.axis_size(axi...  33 us
    ppermute x14, waiting for transfers between devices, swap(): lax.ppermute(value, axis, [(i, i ^ bits) for i in range(lax.axis_size(axi...  18.8 us
    pallas_call x1, Pallas kernels, late(): pl.pallas_call(late_kernel, name='late', in_specs=[smem] * 6 + [vmem] * 5...  3.46 us
    pallas_call x1, Pallas kernels, early(): pl.pallas_call(functools.partial(early_kernel, rows), name='early', in_sp...  3.32 us
    ppermute x1, starting transfers between devices, spread_small(): lax.ppermute(other, ('tm', 'space'), [(i * 4 + s, (i ^ 1) * 4 + (s ^ 2))...  2.46 us
    unnamed x6, local copies, waits for them, and re-layouts  2.26 us
    mul x1, other arithmetic, spectral_table(): window[None, :] * jnp.cos(angles)  1.96 us
    pallas_call x2, Pallas kernels, unpack(): pl.pallas_call(functools.partial(unpack_kernel, factor), name='unpack', i...  1.72 us
  transfers between devices with their start and end apart: 15, of which 10 were waited for; matrix products, arithmetic and copies ran while one was open for 8% of the time, Pallas kernels for 5%

profile of v4, /device:TPU:0, one launch (start us, length us, event | category | flops | bytes accessed | tf_op | source)
XLA Modules:
  0.0 78.1 jit_solution(10452784101410829263)
XLA Ops:
  0.6 0.0 copy-start
  0.6 1.6 %copy-done = f32[528,1024]{1,0:T(8,128)S(1)} copy-done((f32[528,1024]{1,0:T(8,128)S(1)}, f32[528,1024]{1,0:T(8,128)}, u32[]{:S(2)}) %copy-start) | copy-done | bytes 2162712
  2.2 0.0 copy-start.2
  2.2 0.4 cut.1
  2.6 4.1 %collective-permute-start = (f32[528,128]{1,0:T(8,128)S(1)}, f32[528,128]{1,0:T(8,128)S(1)}, u32[]{:S(2)}, u32[]{:S(2)}) collective-permute-start(f32[528,128]{1,0:T(8,128)S(1)} %get-tuple-element.20), channel_id=1, source_target_pairs={{0,16},{4,20},{8,24},{12,28},{16,0},{20,4},{24,8},{28,12},{1,17},{... | collective-permute-start | bytes 811016 | tf_op jit(solution)/shard_map/ppermute | solution.py:300
  6.7 1.6 %collective-permute-start.1 = (f32[528,128]{1,0:T(8,128)S(1)}, f32[528,128]{1,0:T(8,128)S(1)}, u32[]{:S(2)}, u32[]{:S(2)}) collective-permute-start(f32[528,128]{1,0:T(8,128)S(1)} %get-tuple-element.21), channel_id=1, source_target_pairs={{0,8},{4,12},{8,0},{12,4},{16,24},{20,28},{24,16},{28,20},{1,9},{5... | collective-permute-start | bytes 811016 | tf_op jit(solution)/shard_map/ppermute | solution.py:300
  8.3 1.5 %collective-permute-start.2 = (f32[528,128]{1,0:T(8,128)S(1)}, f32[528,128]{1,0:T(8,128)S(1)}, u32[]{:S(2)}, u32[]{:S(2)}) collective-permute-start(f32[528,128]{1,0:T(8,128)S(1)} %get-tuple-element.22), channel_id=1, source_target_pairs={{0,4},{4,0},{8,12},{12,8},{16,20},{20,16},{24,28},{28,24},{1,5},{5... | collective-permute-start | bytes 811016 | tf_op jit(solution)/shard_map/ppermute | solution.py:300
  9.8 0.3 collective-permute-start.3
  10.1 1.4 %collective-permute-start.4 = (f32[528,128]{1,0:T(8,128)S(1)}, f32[528,128]{1,0:T(8,128)S(1)}, u32[]{:S(2)}, u32[]{:S(2)}) collective-permute-start(f32[528,128]{1,0:T(8,128)S(1)} %get-tuple-element.24), channel_id=1, source_target_pairs={{0,12},{4,8},{8,4},{12,0},{16,28},{20,24},{24,20},{28,16},{1,13},{... | collective-permute-start | bytes 811016 | tf_op jit(solution)/shard_map/ppermute | solution.py:300
  11.5 0.6 multiply_reduce_fusion
  12.9 2.0 %cosine_multiply_fusion = (f32[128,256]{1,0:T(8,128)}, f32[128,256]{1,0:T(8,128)}) fusion(s32[128]{0:T(128)} %param.5, f32[256]{0:T(256)S(1)} %get-tuple-element.47, f32[256]{0:T(256)S(1)} %get-tuple-element.48), kind=kLoop, calls=%fused_computation.8 | loop fusion | flops 524288 | bytes 264704 | tf_op jit(solution)/shard_map/mul | solution.py:33
  14.9 5.9 %collective-permute-done.refs_0_ = f32[528,128]{1,0:T(8,128)S(1)} collective-permute-done((f32[528,128]{1,0:T(8,128)S(1)}, f32[528,128]{1,0:T(8,128)S(1)}, u32[]{:S(2)}, u32[]{:S(2)}) %collective-permute-start) | collective-permute-done | bytes 270368 | tf_op jit(solution)/shard_map/ppermute | solution.py:300
  20.8 3.1 %collective-permute-start.5 = (f32[528,128]{1,0:T(8,128)S(1)}, f32[528,128]{1,0:T(8,128)S(1)}, u32[]{:S(2)}, u32[]{:S(2)}) collective-permute-start(f32[528,128]{1,0:T(8,128)S(1)} %get-tuple-element.25), channel_id=1, source_target_pairs={{0,24},{4,28},{8,16},{12,20},{16,8},{20,12},{24,0},{28,4},{1,25},{... | collective-permute-start | bytes 811016 | tf_op jit(solution)/shard_map/ppermute | solution.py:300
  23.9 1.3 %fusion.7 = s32[]{:T(128)} fusion(s32[32]{0:T(128)} %starts_ref.3, s32[]{:T(128)S(6)} %mul.83), kind=kLoop, calls=%fused_computation.29 | loop fusion | flops 127 | bytes 136 | tf_op jit(solution)/shard_map/reduce_sum | solution.py:314
  25.2 0.0 collective-permute-done.1.refs_1_
  25.2 5.9 %collective-permute-start.6 = (f32[528,128]{1,0:T(8,128)S(1)}, f32[528,128]{1,0:T(8,128)S(1)}, u32[]{:S(2)}, u32[]{:S(2)}) collective-permute-start(f32[528,128]{1,0:T(8,128)S(1)} %get-tuple-element.31), channel_id=1, source_target_pairs={{0,28},{4,24},{8,20},{12,16},{16,12},{20,8},{24,4},{28,0},{1,29},{... | collective-permute-start | bytes 811016 | tf_op jit(solution)/shard_map/ppermute | solution.py:300
  31.1 0.1 pad_add_fusion.firsts_ref
  31.8 1.3 %dynamic_slice.3 = s32[1]{0:T(128)} dynamic-slice(s32[32]{0:T(128)} %starts_ref.3, s32[]{:T(128)S(6)} %select_n.39), dynamic_slice_sizes={1} | dynamic-slice | bytes 12 | tf_op jit(solution)/shard_map/dynamic_slice | solution.py:316
  35.9 0.1 stack.51.where_ref
  36.0 1.0 %pad_maximum_fusion.table_ref = f32[256,256]{1,0:T(8,128)S(1)} fusion(f32[128,256]{1,0:T(8,128)} %get-tuple-element.46, f32[128,256]{1,0:T(8,128)} %get-tuple-element.45), kind=kLoop, calls=%fused_computation | loop fusion | flops 65536 | bytes 524288 | tf_op jit(solution)/shard_map/concatenate | solution.py:32
  37.0 0.0 collective-permute-done.2.refs_2_
  37.0 0.0 collective-permute-done.3.refs_3_
  37.0 0.0 collective-permute-done.4.refs_4_
  37.0 2.8 %collective-permute-done.5.refs_5_ = f32[528,128]{1,0:T(8,128)S(1)} collective-permute-done((f32[528,128]{1,0:T(8,128)S(1)}, f32[528,128]{1,0:T(8,128)S(1)}, u32[]{:S(2)}, u32[]{:S(2)}) %collective-permute-start.5) | collective-permute-done | bytes 270368 | tf_op jit(solution)/shard_map/ppermute | solution.py:300
  39.8 0.0 copy-start.1
  39.8 0.7 copy-done.1
  40.4 3.3 %early.1 = (f32[1288,128]{1,0:T(8,128)S(1)}, f32[10240,128]{1,0:T(8,128)S(1)}, f32[128,128]{1,0:T(8,128)S(1)}, bf16[512,256]{1,0:T(8,128)(2,1)S(1)}) custom-call(s32[1]{0:T(128)} %bitcast.base_ref, s32[1]{0:T(128)} %bitcast.2.corner_ref, s32[7]{0:T(128)S(1)} %stack.51.where_ref, s32[32]{0:T(128)S(1)} %copy-done.1, f32[256,256]{1,0:T(8,128)S(1)} %pad_maximum_fusion.table_ref, ...), custom_call_target="tpu_custom_call" | custom-call | flops 1207959552 | bytes 4194304 | tf_op jit(solution)/shard_map/early/pallas_call | solution.py:146
  43.7 1.6 %collective-permute-done.6.piece_ref = f32[528,128]{1,0:T(8,128)S(1)} collective-permute-done((f32[528,128]{1,0:T(8,128)S(1)}, f32[528,128]{1,0:T(8,128)S(1)}, u32[]{:S(2)}, u32[]{:S(2)}) %collective-permute-start.6) | collective-permute-done | bytes 270368 | tf_op jit(solution)/shard_map/ppermute | solution.py:300
  45.4 0.0 copy-done.2
  45.4 3.5 %late.1 = (f32[128,128]{1,0:T(8,128)}, f32[16,32,128]{2,1,0:T(8,128)S(1)}, f32[4,32,128]{2,1,0:T(8,128)S(1)}, f32[4,32,128]{2,1,0:T(8,128)S(1)}, f32[4,32,128]{2,1,0:T(8,128)S(1)}, /*index=5*/f32[4,32,128]{2,1,0:T(8,128)S(1)}) custom-call(s32[1]{0:T(128)} %bitcast.base_ref, s32[1]{0:T(128)} %bitcast.2.corner_ref, s32[1]{0:T(128)} %bitcast.3.where_ref, ...), custom_call_target="tpu_custom_call" | custom-call | flops 3221225472 | bytes 8388608 | tf_op jit(solution)/shard_map/late/pallas_call | solution.py:201
  48.9 0.0 collective-permute-start.7
  48.9 1.5 %collective-permute-done.7 = f32[16,32,128]{2,1,0:T(8,128)S(1)} collective-permute-done((f32[16,32,128]{2,1,0:T(8,128)S(1)}, f32[16,32,128]{2,1,0:T(8,128)S(1)}, u32[]{:S(2)}, u32[]{:S(2)}) %collective-permute-start.7) | collective-permute-done | bytes 262176 | tf_op jit(solution)/shard_map/ppermute | solution.py:300
  50.4 1.5 %collective-permute-start.10 = (f32[4,32,128]{2,1,0:T(8,128)S(1)}, f32[4,32,128]{2,1,0:T(8,128)S(1)}, u32[]{:S(2)}, u32[]{:S(2)}) collective-permute-start(f32[4,32,128]{2,1,0:T(8,128)S(1)} %get-tuple-element.43), channel_id=1, source_target_pairs={{0,24},{4,28},{8,16},{12,20},{16,8},{20,12},{24,0},{28,4},{1,25},{... | collective-permute-start | bytes 196616 | tf_op jit(solution)/shard_map/ppermute | solution.py:300
  51.9 12.0 %collective-permute-start.8 = (f32[4,32,128]{2,1,0:T(8,128)S(1)}, f32[4,32,128]{2,1,0:T(8,128)S(1)}, u32[]{:S(2)}, u32[]{:S(2)}) collective-permute-start(f32[4,32,128]{2,1,0:T(8,128)S(1)} %get-tuple-element.41), channel_id=1, source_target_pairs={{0,16},{4,20},{8,24},{12,28},{16,0},{20,4},{24,8},{28,12},{1,17},{... | collective-permute-start | bytes 196616 | tf_op jit(solution)/shard_map/ppermute | solution.py:300
  64.0 0.5 collective-permute-start.9
  64.5 0.0 collective-permute-done.10
  64.5 4.0 %collective-permute-done.8 = f32[4,32,128]{2,1,0:T(8,128)S(1)} collective-permute-done((f32[4,32,128]{2,1,0:T(8,128)S(1)}, f32[4,32,128]{2,1,0:T(8,128)S(1)}, u32[]{:S(2)}, u32[]{:S(2)}) %collective-permute-start.8) | collective-permute-done | bytes 65568 | tf_op jit(solution)/shard_map/ppermute | solution.py:300
  68.5 0.4 collective-permute-done.9
  69.0 0.6 collective-permute-start.12
  69.6 2.5 %collective-permute-start.13 = (f32[2,32,128]{2,1,0:T(8,128)S(1)}, f32[2,32,128]{2,1,0:T(8,128)S(1)}, u32[]{:S(2)}, u32[]{:S(2)}) collective-permute-start(f32[2,32,128]{2,1,0:T(8,128)S(1)} %broadcast_select_fusion), channel_id=1, source_target_pairs={{0,6},{1,7},{2,4},{3,5},{4,2},{5,3},{6,0},{7,1},{8,14},{9,15},{10,... | collective-permute-start | bytes 98312 | tf_op jit(solution)/shard_map/ppermute | solution.py:334
  72.0 0.5 collective-permute-start.11
  72.5 0.7 collective-permute-done.12
  73.3 1.2 %collective-permute-done.13 = f32[2,32,128]{2,1,0:T(8,128)S(1)} collective-permute-done((f32[2,32,128]{2,1,0:T(8,128)S(1)}, f32[2,32,128]{2,1,0:T(8,128)S(1)}, u32[]{:S(2)}, u32[]{:S(2)}) %collective-permute-start.13) | collective-permute-done | bytes 32800 | tf_op jit(solution)/shard_map/ppermute | solution.py:334
  74.5 1.4 %collective-permute-done.11 = f32[2,32,128]{2,1,0:T(8,128)S(1)} collective-permute-done((f32[2,32,128]{2,1,0:T(8,128)S(1)}, f32[2,32,128]{2,1,0:T(8,128)S(1)}, u32[]{:S(2)}, u32[]{:S(2)}) %collective-permute-start.11) | collective-permute-done | bytes 32800 | tf_op jit(solution)/shard_map/ppermute | solution.py:300
  75.9 0.1 collective-permute-start.14
  76.0 0.9 %unpack.2.refs_0_ = f32[2,16,32,32]{3,2,1,0:T(8,128)} custom-call(s32[1]{0:T(128)} %bitcast.4.core_ref.order_ref, f32[2,32,128]{2,1,0:T(8,128)S(1)} %add_add_fusion.packed_ref), custom_call_target="tpu_custom_call" | custom-call | tf_op jit(solution)/shard_map/unpack/pallas_call | solution.py:284
  76.9 0.3 collective-permute-done.14.packed_ref
  77.2 0.9 %unpack.3 = f32[2,16,32,32]{3,2,1,0:T(8,128)} custom-call(s32[1]{0:T(128)} %bitcast.16.order_ref, f32[2,32,128]{2,1,0:T(8,128)S(1)} %collective-permute-done.14.packed_ref, f32[2,16,32,32]{3,2,1,0:T(8,128)} %unpack.2.refs_0_), custom_call_target="tpu_custom_call", output_to_operand_aliasing={{}: (2, {})} | custom-call | tf_op jit(solution)/shard_map/unpack/pallas_call | solution.py:284
  (5 shorter events, 0.1 us)
Async XLA Ops:
  0.6 1.6 %copy-start = (f32[528,1024]{1,0:T(8,128)S(1)}, f32[528,1024]{1,0:T(8,128)}, u32[]{:S(2)}) copy-start(f32[528,1024]{1,0:T(8,128)} %snapshots_ref.1) | copy-start | bytes 6488068
  2.2 43.2 %copy-start.2 = (s32[32]{0:T(128)S(1)}, s32[32]{0:T(128)}, u32[]{:S(2)}) copy-start(s32[32]{0:T(128)} %starts_ref.3) | copy-start | bytes 388
  2.6 18.1 %collective-permute-start = (f32[528,128]{1,0:T(8,128)S(1)}, f32[528,128]{1,0:T(8,128)S(1)}, u32[]{:S(2)}, u32[]{:S(2)}) collective-permute-start(f32[528,128]{1,0:T(8,128)S(1)} %get-tuple-element.20), channel_id=1, source_target_pairs={{0,16},{4,20},{8,24},{12,28},{16,0},{20,4},{24,8},{28,12},{1,17},{... | collective-permute-start | bytes 811016 | tf_op jit(solution)/shard_map/ppermute | solution.py:300
  6.7 18.4 %collective-permute-start.1 = (f32[528,128]{1,0:T(8,128)S(1)}, f32[528,128]{1,0:T(8,128)S(1)}, u32[]{:S(2)}, u32[]{:S(2)}) collective-permute-start(f32[528,128]{1,0:T(8,128)S(1)} %get-tuple-element.21), channel_id=1, source_target_pairs={{0,8},{4,12},{8,0},{12,4},{16,24},{20,28},{24,16},{28,20},{1,9},{5... | collective-permute-start | bytes 811016 | tf_op jit(solution)/shard_map/ppermute | solution.py:300
  8.3 28.6 %collective-permute-start.2 = (f32[528,128]{1,0:T(8,128)S(1)}, f32[528,128]{1,0:T(8,128)S(1)}, u32[]{:S(2)}, u32[]{:S(2)}) collective-permute-start(f32[528,128]{1,0:T(8,128)S(1)} %get-tuple-element.22), channel_id=1, source_target_pairs={{0,4},{4,0},{8,12},{12,8},{16,20},{20,16},{24,28},{28,24},{1,5},{5... | collective-permute-start | bytes 811016 | tf_op jit(solution)/shard_map/ppermute | solution.py:300
  9.8 27.2 %collective-permute-start.3 = (f32[528,128]{1,0:T(8,128)S(1)}, f32[528,128]{1,0:T(8,128)S(1)}, u32[]{:S(2)}, u32[]{:S(2)}) collective-permute-start(f32[528,128]{1,0:T(8,128)S(1)} %get-tuple-element.23), channel_id=1, source_target_pairs={{0,20},{4,16},{8,28},{12,24},{16,4},{20,0},{24,12},{28,8},{1,21},{... | collective-permute-start | bytes 811016 | tf_op jit(solution)/shard_map/ppermute | solution.py:300
  10.1 26.9 %collective-permute-start.4 = (f32[528,128]{1,0:T(8,128)S(1)}, f32[528,128]{1,0:T(8,128)S(1)}, u32[]{:S(2)}, u32[]{:S(2)}) collective-permute-start(f32[528,128]{1,0:T(8,128)S(1)} %get-tuple-element.24), channel_id=1, source_target_pairs={{0,12},{4,8},{8,4},{12,0},{16,28},{20,24},{24,20},{28,16},{1,13},{... | collective-permute-start | bytes 811016 | tf_op jit(solution)/shard_map/ppermute | solution.py:300
  20.8 19.0 %collective-permute-start.5 = (f32[528,128]{1,0:T(8,128)S(1)}, f32[528,128]{1,0:T(8,128)S(1)}, u32[]{:S(2)}, u32[]{:S(2)}) collective-permute-start(f32[528,128]{1,0:T(8,128)S(1)} %get-tuple-element.25), channel_id=1, source_target_pairs={{0,24},{4,28},{8,16},{12,20},{16,8},{20,12},{24,0},{28,4},{1,25},{... | collective-permute-start | bytes 811016 | tf_op jit(solution)/shard_map/ppermute | solution.py:300
  25.2 20.2 %collective-permute-start.6 = (f32[528,128]{1,0:T(8,128)S(1)}, f32[528,128]{1,0:T(8,128)S(1)}, u32[]{:S(2)}, u32[]{:S(2)}) collective-permute-start(f32[528,128]{1,0:T(8,128)S(1)} %get-tuple-element.31), channel_id=1, source_target_pairs={{0,28},{4,24},{8,20},{12,16},{16,12},{20,8},{24,4},{28,0},{1,29},{... | collective-permute-start | bytes 811016 | tf_op jit(solution)/shard_map/ppermute | solution.py:300
  39.8 0.7 copy-start.1
  48.9 1.5 %collective-permute-start.7 = (f32[16,32,128]{2,1,0:T(8,128)S(1)}, f32[16,32,128]{2,1,0:T(8,128)S(1)}, u32[]{:S(2)}, u32[]{:S(2)}) collective-permute-start(f32[16,32,128]{2,1,0:T(8,128)S(1)} %get-tuple-element.34), channel_id=1, source_target_pairs={{0,1},{1,0},{2,3},{3,2},{4,5},{5,4},{6,7},{7,6},{8,9},{9,8},{10,11... | collective-permute-start | bytes 786440 | tf_op jit(solution)/shard_map/ppermute | solution.py:300
  50.4 14.0 %collective-permute-start.10 = (f32[4,32,128]{2,1,0:T(8,128)S(1)}, f32[4,32,128]{2,1,0:T(8,128)S(1)}, u32[]{:S(2)}, u32[]{:S(2)}) collective-permute-start(f32[4,32,128]{2,1,0:T(8,128)S(1)} %get-tuple-element.43), channel_id=1, source_target_pairs={{0,24},{4,28},{8,16},{12,20},{16,8},{20,12},{24,0},{28,4},{1,25},{... | collective-permute-start | bytes 196616 | tf_op jit(solution)/shard_map/ppermute | solution.py:300
  51.9 16.6 %collective-permute-start.8 = (f32[4,32,128]{2,1,0:T(8,128)S(1)}, f32[4,32,128]{2,1,0:T(8,128)S(1)}, u32[]{:S(2)}, u32[]{:S(2)}) collective-permute-start(f32[4,32,128]{2,1,0:T(8,128)S(1)} %get-tuple-element.41), channel_id=1, source_target_pairs={{0,16},{4,20},{8,24},{12,28},{16,0},{20,4},{24,8},{28,12},{1,17},{... | collective-permute-start | bytes 196616 | tf_op jit(solution)/shard_map/ppermute | solution.py:300
  64.0 4.9 %collective-permute-start.9 = (f32[4,32,128]{2,1,0:T(8,128)S(1)}, f32[4,32,128]{2,1,0:T(8,128)S(1)}, u32[]{:S(2)}, u32[]{:S(2)}) collective-permute-start(f32[4,32,128]{2,1,0:T(8,128)S(1)} %get-tuple-element.44), channel_id=1, source_target_pairs={{0,8},{4,12},{8,0},{12,4},{16,24},{20,28},{24,16},{28,20},{1,9},{5... | collective-permute-start | bytes 196616 | tf_op jit(solution)/shard_map/ppermute | solution.py:300
  69.0 4.3 %collective-permute-start.12 = (f32[2,32,128]{2,1,0:T(8,128)S(1)}, f32[2,32,128]{2,1,0:T(8,128)S(1)}, u32[]{:S(2)}, u32[]{:S(2)}) collective-permute-start(f32[2,32,128]{2,1,0:T(8,128)S(1)} %broadcast_select_fusion), channel_id=1, source_target_pairs={{0,4},{4,0},{8,12},{12,8},{16,20},{20,16},{24,28},{28,24},{1,5},{5... | collective-permute-start | bytes 98312 | tf_op jit(solution)/shard_map/ppermute | solution.py:300
  69.6 4.9 %collective-permute-start.13 = (f32[2,32,128]{2,1,0:T(8,128)S(1)}, f32[2,32,128]{2,1,0:T(8,128)S(1)}, u32[]{:S(2)}, u32[]{:S(2)}) collective-permute-start(f32[2,32,128]{2,1,0:T(8,128)S(1)} %broadcast_select_fusion), channel_id=1, source_target_pairs={{0,6},{1,7},{2,4},{3,5},{4,2},{5,3},{6,0},{7,1},{8,14},{9,15},{10,... | collective-permute-start | bytes 98312 | tf_op jit(solution)/shard_map/ppermute | solution.py:334
  72.0 3.9 %collective-permute-start.11 = (f32[2,32,128]{2,1,0:T(8,128)S(1)}, f32[2,32,128]{2,1,0:T(8,128)S(1)}, u32[]{:S(2)}, u32[]{:S(2)}) collective-permute-start(f32[2,32,128]{2,1,0:T(8,128)S(1)} %get-tuple-element.38), channel_id=1, source_target_pairs={{0,2},{1,3},{2,0},{3,1},{4,6},{5,7},{6,4},{7,5},{8,10},{9,11},{10,... | collective-permute-start | bytes 98312 | tf_op jit(solution)/shard_map/ppermute | solution.py:300
  75.9 1.3 %collective-permute-start.14 = (f32[2,32,128]{2,1,0:T(8,128)S(1)}, f32[2,32,128]{2,1,0:T(8,128)S(1)}, u32[]{:S(2)}, u32[]{:S(2)}) collective-permute-start(f32[2,32,128]{2,1,0:T(8,128)S(1)} %add_add_fusion.packed_ref), channel_id=1, source_target_pairs={{0,1},{1,0},{2,3},{3,2},{4,5},{5,4},{6,7},{7,6},{8,9},{9,8},{10,11... | collective-permute-start | bytes 98312 | tf_op jit(solution)/shard_map/ppermute | solution.py:300

commit v5 on v4

--- a/solution.py
+++ b/solution.py
@@ -162,11 +162,28 @@
     )(base, corner, where, starts, table, *pieces)
 
 
+def packed_quarters(base, core, firsts_ref, spec_ref, late_spec, sent_ref, kept_refs):
+    block = lax.broadcasted_iota(jnp.int32, (NB, LANES), 0)
+    is_late = (block >= base) & (block < base + LATE)
+
+    def rows_of(part, line):
+        return jnp.where(
+            is_late, line_rows(late_spec, part, line), line_rows(spec_ref, part, line)
+        )
+
+    half = kept_refs[0].shape[0]
+    for n, kept_ref in enumerate(kept_refs):
+        for i in range(half):
+            group = firsts_ref[n] + (i // CORE_STEP) * 2 * CORE_STEP + i % CORE_STEP
+            kept_ref[i] = gram(rows_of, (group + core * CORE_STEP) * PACK)
+            sent_ref[n * half + i] = gram(rows_of, (group + (1 - core) * CORE_STEP) * PACK)
+
+
 def late_kernel(
     base_ref, corner_ref, where_ref, core_ref, firsts_ref, starts_ref,
-    halves, window_ref, spec_ref, early_power_ref, piece_ref, power_ref, sent_ref, *refs,
+    halves, window_ref, spec_ref, early_power_ref, piece_ref, power_ref, late_spec, sent_ref, *refs,
 ):
-    kept_refs, (series, late_spec) = refs[:-2], refs[-2:]
+    kept_refs, series = refs[:-1], refs[-1]
     rows, base = piece_ref.shape[0], base_ref[0]
     origin = corner_ref[0] - rows
     series[pl.ds(rows, WINDOW), :] = window_ref[...]
@@ -177,45 +194,46 @@
         blocks = [series[pl.ds(starts_ref[b] - origin, NFFT), :] for b in numbers]
         power = power + transform(halves, blocks, numbers, late_spec)
     power_ref[...] = power
-    block = lax.broadcasted_iota(jnp.int32, (NB, LANES), 0)
-    is_late = (block >= base) & (block < base + LATE)
-
-    def rows_of(part, line):
-        return jnp.where(
-            is_late, line_rows(late_spec, part, line), line_rows(spec_ref, part, line)
-        )
-
-    core = core_ref[0]
-    half = len(kept_refs)
-    for n, kept_ref in enumerate(kept_refs):
-        for i in range(half):
-            group = firsts_ref[n] + (i // CORE_STEP) * 2 * CORE_STEP + i % CORE_STEP
-            kept_ref[i] = gram(rows_of, (group + core * CORE_STEP) * PACK)
-            sent_ref[n * half + i] = gram(rows_of, (group + (1 - core) * CORE_STEP) * PACK)
+    packed_quarters(base, core_ref[0], firsts_ref, spec_ref, late_spec, sent_ref, kept_refs)
+
+
+def rest_kernel(base_ref, core_ref, firsts_ref, spec_ref, late_spec, sent_ref, *kept_refs):
+    packed_quarters(base_ref[0], core_ref[0], firsts_ref, spec_ref, late_spec, sent_ref, kept_refs)
+
+
+def quarter_shapes(quarters):
+    half = NF // PACK // 4 // 2
+    return [jax.ShapeDtypeStruct((n * half, NB, LANES), F32) for n in (quarters, *[1] * quarters)]
 
 
 def late(base, corner, where, core, firsts, starts, halves, window, spec, power, piece):
     quarters = firsts.shape[0]
-    half = NF // PACK // quarters // 2
     smem, vmem = pl.BlockSpec(memory_space=SMEM), pl.BlockSpec(memory_space=VMEM)
     return pl.pallas_call(
         late_kernel,
         name="late",
         in_specs=[smem] * 6 + [vmem] * 5,
-        out_specs=[vmem] * (2 + quarters),
-        out_shape=[
-            jax.ShapeDtypeStruct((NF, LANES), F32),
-            jax.ShapeDtypeStruct((quarters * half, NB, LANES), F32),
-        ]
-        + [jax.ShapeDtypeStruct((half, NB, LANES), F32)] * quarters,
-        scratch_shapes=[VMEM((2 * piece.shape[0] + WINDOW, LANES), F32), VMEM(spec.shape, F32)],
-        compiler_params=pltpu.CompilerParams(vmem_limit_bytes=28 << 20),
-        cost_estimate=pl.CostEstimate(
-            flops=NF // PACK * 6 * LANES * 4 * LANES * LANES * 2,
-            bytes_accessed=8 << 20,
-            transcendentals=0,
-        ),
+        out_specs=[vmem] * (3 + quarters),
+        out_shape=[jax.ShapeDtypeStruct(a.shape, F32) for a in (power, spec)]
+        + quarter_shapes(quarters),
+        scratch_shapes=[VMEM((2 * piece.shape[0] + WINDOW, LANES), F32)],
+        compiler_params=pltpu.CompilerParams(vmem_limit_bytes=20 << 20),
+        cost_estimate=pl.CostEstimate(flops=3 << 30, bytes_accessed=8 << 20, transcendentals=0),
     )(base, corner, where, core, firsts, starts, halves, window, spec, power, piece)
+
+
+def rest(base, core, firsts, spec, late_spec):
+    quarters = firsts.shape[0]
+    smem, vmem = pl.BlockSpec(memory_space=SMEM), pl.BlockSpec(memory_space=VMEM)
+    return pl.pallas_call(
+        rest_kernel,
+        name="rest",
+        in_specs=[smem] * 3 + [vmem] * 2,
+        out_specs=[vmem] * (1 + quarters),
+        out_shape=quarter_shapes(quarters),
+        compiler_params=pltpu.CompilerParams(vmem_limit_bytes=20 << 20),
+        cost_estimate=pl.CostEstimate(flops=2 << 30, bytes_accessed=4 << 20, transcendentals=0),
+    )(base, core, firsts, spec, late_spec)
 
 
 def whole_kernel(starts_ref, table_ref, series_ref, power_ref, packed_ref, halves, spec):
@@ -253,8 +271,12 @@
     )(starts, table, series)
 
 
-def unpack_kernel(factor, order_ref, packed_ref, *refs):
-    out_ref, matrices, sem = refs[-3:]
+def unpack_kernel(factor, order_ref, packed_ref, power_ref, *refs):
+    out_ref, power_out, matrices, sems = refs[-4:]
+    first = len(refs) == 4
+    power_copy = pltpu.make_async_copy(power_ref, power_out, sems.at[1])
+    if first:
+        power_copy.start()
     row = lax.broadcasted_iota(jnp.int32, (NB, NB), 0)
     column = lax.broadcasted_iota(jnp.int32, (NB, NB), 1)
     count = packed_ref.shape[0]
@@ -270,30 +292,35 @@
             )
     lines = count * PACK
     copy = pltpu.make_async_copy(
-        matrices, out_ref.at[:, pl.ds(order_ref[0] * lines, lines)], sem
+        matrices, out_ref.at[:, pl.ds(order_ref[0] * lines, lines)], sems.at[0]
     )
     copy.start()
     copy.wait()
-
-
-def unpack(parts, order, factor):
+    if first:
+        power_copy.wait()
+
+
+def unpack(parts, order, power, factor):
     lines = parts[0].shape[0] * PACK
+    anywhere = pl.BlockSpec(memory_space=pl.ANY)
     out = []
     for n, part in enumerate(parts):
-        out = [
-            pl.pallas_call(
-                functools.partial(unpack_kernel, factor),
-                name="unpack",
-                in_specs=[pl.BlockSpec(memory_space=SMEM), pl.BlockSpec(memory_space=VMEM)]
-                + [pl.BlockSpec(memory_space=pl.ANY)] * len(out),
-                out_specs=pl.BlockSpec(memory_space=pl.ANY),
-                out_shape=jax.ShapeDtypeStruct((2, len(parts) * lines, NB, NB), F32),
-                input_output_aliases={2: 0} if out else {},
-                scratch_shapes=[VMEM((2, lines, NB, NB), F32), pltpu.SemaphoreType.DMA],
-                compiler_params=pltpu.CompilerParams(vmem_limit_bytes=8 << 20),
-            )(order[n].reshape(1), part, *out)
-        ]
-    return out[0]
+        out = pl.pallas_call(
+            functools.partial(unpack_kernel, factor),
+            name="unpack",
+            in_specs=[pl.BlockSpec(memory_space=SMEM), pl.BlockSpec(memory_space=VMEM)]
+            + [pl.BlockSpec(memory_space=VMEM) if not out else anywhere]
+            + [anywhere] * len(out[:1]),
+            out_specs=[anywhere] * 2,
+            out_shape=[
+                jax.ShapeDtypeStruct((2, len(parts) * lines, NB, NB), F32),
+                jax.ShapeDtypeStruct(power.shape, F32),
+            ],
+            input_output_aliases={3: 0, 2: 1} if out else {},
+            scratch_shapes=[VMEM((2, lines, NB, NB), F32), pltpu.SemaphoreType.DMA((2,))],
+            compiler_params=pltpu.CompilerParams(vmem_limit_bytes=8 << 20),
+        )(order[n].reshape(1), part, out[1] if out else power, *out[:1])
+    return out[1], out[0]
 
 
 def swap(value, axis, bits):
@@ -317,15 +344,19 @@
     base = base.reshape(1)
     window, spec, power, halves = early(base, corner, where, starts, table, pieces)
     groups = NF // PACK // 4
-    away = (2, 1, 3)
+    away = (3, 2, 1)
     firsts = jnp.stack([(z ^ j) * groups for j in (*away, 0)])
-    power, sent, *kept = late(
-        base, corner, late_part.reshape(1), core.reshape(1), firsts, starts,
+    core_number = core.reshape(1)
+    power, late_spec, sent, *kept = late(
+        base, corner, late_part.reshape(1), core_number, firsts[:2], starts,
         halves, window, spec, power, last,
     )
-    theirs = swap(sent, "space", 1)
+    sent_rest, *kept_rest = rest(base, core_number, firsts[2:], spec, late_spec)
     half = groups // 2
-    terms = [k + theirs[n * half : (n + 1) * half] for n, k in enumerate(kept)]
+    terms = []
+    for sent, kept in ((sent, kept), (sent_rest, kept_rest)):
+        theirs = swap(sent, "space", 1)
+        terms += [k + theirs[n * half : (n + 1) * half] for n, k in enumerate(kept)]
     terms = [swap(t, "tm", 2 * j) for j, t in zip(away, terms)] + terms[-1:]
     lower, upper = (sum(t[i * half // 2 : (i + 1) * half // 2] for t in terms) for i in range(2))
     mine, other = jnp.where(x == 0, lower, upper), jnp.where(x == 0, upper, lower)
@@ -354,8 +385,8 @@
     spaces = lax.axis_size("space")
     table = spectral_table(freq_lines)
     spread = spread_small if (groups, spaces) == (8, 4) else spread_any
-    power_density, parts, order = spread(snapshots, starts, table)
-    return power_density, unpack(parts, order, 1.0 / (NB * snapshots.shape[1] * spaces))
+    power, parts, order = spread(snapshots, starts, table)
+    return unpack(parts, order, power, 1.0 / (NB * snapshots.shape[1] * spaces))
 
 
 def solution(mesh):

time: 78.3 us -> 77.8 us (level)
  waiting for transfers between devices: 20 us -> 18.3 us
    ppermute x14 -> x15, waiting for transfers between devices: 18.8 us -> 17 us  [swap(): lax.ppermute(value, axis, [(i, i ^ bits) for i in range(lax.axis_size(axi...]
    pallas_call x0 -> x1, Pallas kernels: none -> 1.62 us  [rest(): pl.pallas_call(rest_kernel, name='rest', in_specs=[smem] * 3 + [vmem] * 2...]
    ppermute x14 -> x15, starting transfers between devices: 33 us -> 34.7 us  [swap(): lax.ppermute(value, axis, [(i, i ^ bits) for i in range(lax.axis_size(axi...]
    pallas_call x1, Pallas kernels: 3.46 us -> 2.37 us  [late(): pl.pallas_call(late_kernel, name='late', in_specs=[smem] * 6 + [vmem] * 5...]
    ppermute x1, starting transfers between devices: 2.46 us -> 1.54 us  [spread_small(): lax.ppermute(other, ('tm', 'space'), [(i * 4 + s, (i ^ 1) * 4 + (s ^ 2))...]
  transfers between devices with their start and end apart: 15 -> 16, of which waited for: 10 -> 9; matrix products, arithmetic and copies ran while one was open for 8% -> 8% of each run, Pallas kernels for 5% -> 7%
where the time goes in v5:
time: 77.8 us; the launch traced here: 77.6 us
  starting transfers between devices  36.2 us (47%)
  waiting for transfers between devices  18.3 us (24%)
  Pallas kernels  9.44 us (12%)
  other arithmetic  5.22 us (7%)
  between operations  4.72 us (6%)
  local copies, waits for them, and re-layouts  3.66 us (5%)
    ppermute x15, starting transfers between devices, swap(): lax.ppermute(value, axis, [(i, i ^ bits) for i in range(lax.axis_size(axi...  34.7 us
    ppermute x15, waiting for transfers between devices, swap(): lax.ppermute(value, axis, [(i, i ^ bits) for i in range(lax.axis_size(axi...  17 us
    pallas_call x1, Pallas kernels, early(): pl.pallas_call(functools.partial(early_kernel, rows), name='early', in_sp...  3.33 us
    pallas_call x1, Pallas kernels, late(): pl.pallas_call(late_kernel, name='late', in_specs=[smem] * 6 + [vmem] * 5...  2.37 us
    unnamed x6, local copies, waits for them, and re-layouts  2.26 us
    mul x1, other arithmetic, spectral_table(): window[None, :] * jnp.cos(angles)  1.95 us
    pallas_call x2, Pallas kernels, unpack(): pl.pallas_call(functools.partial(unpack_kernel, factor), name='unpack', i...  1.74 us
    pallas_call x1, Pallas kernels, rest(): pl.pallas_call(rest_kernel, name='rest', in_specs=[smem] * 3 + [vmem] * 2...  1.62 us
  transfers between devices with their start and end apart: 16, of which 9 were waited for; matrix products, arithmetic and copies ran while one was open for 8% of the time, Pallas kernels for 7%

profile of v5, /device:TPU:0, one launch (start us, length us, event | category | flops | bytes accessed | tf_op | source)
XLA Modules:
  0.0 77.6 jit_solution(13640889428783867098)
XLA Ops:
  0.6 0.0 copy-start
  0.6 1.6 %copy-done = f32[528,1024]{1,0:T(8,128)S(1)} copy-done((f32[528,1024]{1,0:T(8,128)S(1)}, f32[528,1024]{1,0:T(8,128)}, u32[]{:S(2)}) %copy-start) | copy-done | bytes 2162712
  2.2 0.0 copy-start.2
  2.2 0.4 cut.1
  2.6 4.1 %collective-permute-start = (f32[528,128]{1,0:T(8,128)S(1)}, f32[528,128]{1,0:T(8,128)S(1)}, u32[]{:S(2)}, u32[]{:S(2)}) collective-permute-start(f32[528,128]{1,0:T(8,128)S(1)} %get-tuple-element.26), channel_id=1, source_target_pairs={{0,16},{4,20},{8,24},{12,28},{16,0},{20,4},{24,8},{28,12},{1,17},{... | collective-permute-start | bytes 811016 | tf_op jit(solution)/shard_map/ppermute | solution.py:327
  6.7 1.6 %collective-permute-start.1 = (f32[528,128]{1,0:T(8,128)S(1)}, f32[528,128]{1,0:T(8,128)S(1)}, u32[]{:S(2)}, u32[]{:S(2)}) collective-permute-start(f32[528,128]{1,0:T(8,128)S(1)} %get-tuple-element.27), channel_id=1, source_target_pairs={{0,8},{4,12},{8,0},{12,4},{16,24},{20,28},{24,16},{28,20},{1,9},{5... | collective-permute-start | bytes 811016 | tf_op jit(solution)/shard_map/ppermute | solution.py:327
  8.3 1.5 %collective-permute-start.2 = (f32[528,128]{1,0:T(8,128)S(1)}, f32[528,128]{1,0:T(8,128)S(1)}, u32[]{:S(2)}, u32[]{:S(2)}) collective-permute-start(f32[528,128]{1,0:T(8,128)S(1)} %get-tuple-element.28), channel_id=1, source_target_pairs={{0,4},{4,0},{8,12},{12,8},{16,20},{20,16},{24,28},{28,24},{1,5},{5... | collective-permute-start | bytes 811016 | tf_op jit(solution)/shard_map/ppermute | solution.py:327
  9.8 0.3 collective-permute-start.3
  10.1 1.4 %collective-permute-start.4 = (f32[528,128]{1,0:T(8,128)S(1)}, f32[528,128]{1,0:T(8,128)S(1)}, u32[]{:S(2)}, u32[]{:S(2)}) collective-permute-start(f32[528,128]{1,0:T(8,128)S(1)} %get-tuple-element.30), channel_id=1, source_target_pairs={{0,12},{4,8},{8,4},{12,0},{16,28},{20,24},{24,20},{28,16},{1,13},{... | collective-permute-start | bytes 811016 | tf_op jit(solution)/shard_map/ppermute | solution.py:327
  11.5 0.6 multiply_reduce_fusion
  12.9 1.9 %cosine_multiply_fusion = (f32[128,256]{1,0:T(8,128)}, f32[128,256]{1,0:T(8,128)}) fusion(s32[128]{0:T(128)} %param.5, f32[256]{0:T(256)S(1)} %get-tuple-element.59, f32[256]{0:T(256)S(1)} %get-tuple-element.60), kind=kLoop, calls=%fused_computation.8 | loop fusion | flops 524288 | bytes 264704 | tf_op jit(solution)/shard_map/mul | solution.py:33
  14.8 1.4 %fusion.7 = s32[]{:T(128)} fusion(s32[32]{0:T(128)} %starts_ref.3, s32[]{:T(128)S(6)} %mul.83), kind=kLoop, calls=%fused_computation.29 | loop fusion | flops 127 | bytes 136 | tf_op jit(solution)/shard_map/reduce_sum | solution.py:341
  16.2 4.6 %collective-permute-done.refs_0_ = f32[528,128]{1,0:T(8,128)S(1)} collective-permute-done((f32[528,128]{1,0:T(8,128)S(1)}, f32[528,128]{1,0:T(8,128)S(1)}, u32[]{:S(2)}, u32[]{:S(2)}) %collective-permute-start) | collective-permute-done | bytes 270368 | tf_op jit(solution)/shard_map/ppermute | solution.py:327
  20.8 3.1 %collective-permute-start.5 = (f32[528,128]{1,0:T(8,128)S(1)}, f32[528,128]{1,0:T(8,128)S(1)}, u32[]{:S(2)}, u32[]{:S(2)}) collective-permute-start(f32[528,128]{1,0:T(8,128)S(1)} %get-tuple-element.31), channel_id=1, source_target_pairs={{0,24},{4,28},{8,16},{12,20},{16,8},{20,12},{24,0},{28,4},{1,25},{... | collective-permute-start | bytes 811016 | tf_op jit(solution)/shard_map/ppermute | solution.py:327
  23.9 0.1 pad_add_fusion.firsts_ref
  23.9 0.0 collective-permute-done.1.refs_1_
  23.9 5.9 %collective-permute-start.6 = (f32[528,128]{1,0:T(8,128)S(1)}, f32[528,128]{1,0:T(8,128)S(1)}, u32[]{:S(2)}, u32[]{:S(2)}) collective-permute-start(f32[528,128]{1,0:T(8,128)S(1)} %get-tuple-element.37), channel_id=1, source_target_pairs={{0,28},{4,24},{8,20},{12,16},{16,12},{20,8},{24,4},{28,0},{1,29},{... | collective-permute-start | bytes 811016 | tf_op jit(solution)/shard_map/ppermute | solution.py:327
  29.8 0.1 pad_add_fusion.1.firsts_ref
  30.6 1.3 %dynamic_slice.3 = s32[1]{0:T(128)} dynamic-slice(s32[32]{0:T(128)} %starts_ref.3, s32[]{:T(128)S(6)} %select_n.42), dynamic_slice_sizes={1} | dynamic-slice | bytes 12 | tf_op jit(solution)/shard_map/dynamic_slice | solution.py:343
  34.5 0.1 stack.51.where_ref
  34.6 1.0 %pad_maximum_fusion.table_ref = f32[256,256]{1,0:T(8,128)S(1)} fusion(f32[128,256]{1,0:T(8,128)} %get-tuple-element.58, f32[128,256]{1,0:T(8,128)} %get-tuple-element.57), kind=kLoop, calls=%fused_computation | loop fusion | flops 65536 | bytes 524288 | tf_op jit(solution)/shard_map/concatenate | solution.py:32
  35.6 0.0 collective-permute-done.2.refs_2_
  35.6 0.0 collective-permute-done.3.refs_3_
  35.6 0.0 collective-permute-done.4.refs_4_
  35.6 4.2 %collective-permute-done.5.refs_5_ = f32[528,128]{1,0:T(8,128)S(1)} collective-permute-done((f32[528,128]{1,0:T(8,128)S(1)}, f32[528,128]{1,0:T(8,128)S(1)}, u32[]{:S(2)}, u32[]{:S(2)}) %collective-permute-start.5) | collective-permute-done | bytes 270368 | tf_op jit(solution)/shard_map/ppermute | solution.py:327
  39.8 0.0 copy-start.1
  39.8 0.7 copy-done.1
  40.4 3.3 %early.1 = (f32[1288,128]{1,0:T(8,128)S(1)}, f32[10240,128]{1,0:T(8,128)S(1)}, f32[128,128]{1,0:T(8,128)S(1)}, bf16[512,256]{1,0:T(8,128)(2,1)S(1)}) custom-call(s32[1]{0:T(128)} %bitcast.1.base_ref, s32[1]{0:T(128)} %bitcast.3.corner_ref, s32[7]{0:T(128)S(1)} %stack.51.where_ref, s32[32]{0:T(128)S(1)} %copy-done.1, ...), custom_call_target="tpu_custom_call" | custom-call | flops 1207959552 | bytes 4194304 | tf_op jit(solution)/shard_map/early/pallas_call | solution.py:146
  43.8 1.6 %collective-permute-done.6.piece_ref = f32[528,128]{1,0:T(8,128)S(1)} collective-permute-done((f32[528,128]{1,0:T(8,128)S(1)}, f32[528,128]{1,0:T(8,128)S(1)}, u32[]{:S(2)}, u32[]{:S(2)}) %collective-permute-start.6) | collective-permute-done | bytes 270368 | tf_op jit(solution)/shard_map/ppermute | solution.py:327
  45.4 0.0 copy-done.2
  45.4 2.4 %late.1 = (f32[128,128]{1,0:T(8,128)S(1)}, f32[10240,128]{1,0:T(8,128)S(1)}, f32[8,32,128]{2,1,0:T(8,128)S(1)}, f32[4,32,128]{2,1,0:T(8,128)S(1)}, f32[4,32,128]{2,1,0:T(8,128)S(1)}) custom-call(s32[1]{0:T(128)} %bitcast.1.base_ref, s32[1]{0:T(128)} %bitcast.3.corner_ref, s32[1]{0:T(128)} %bitcast.4.where_ref, s32[1]{0:T(128)} %bitcast.5.core_ref.order_ref, ...), custom_call_target="tpu_custom_call" | custom-call | flops 3221225472 | bytes 8388608 | tf_op jit(solution)/shard_map/late/pallas_call | solution.py:212
  47.8 0.1 collective-permute-start.7
  47.8 1.6 %rest.1 = (f32[8,32,128]{2,1,0:T(8,128)S(1)}, f32[4,32,128]{2,1,0:T(8,128)S(1)}, f32[4,32,128]{2,1,0:T(8,128)S(1)}) custom-call(s32[1]{0:T(128)} %bitcast.1.base_ref, s32[1]{0:T(128)} %bitcast.5.core_ref.order_ref, s32[2]{0:T(128)S(1)} %pad_add_fusion.1.firsts_ref, f32[10240,128]{1,0:T(8,128)S(1)} %get-tuple-element.35.spec_ref, ...), custom_call_target="tpu_custom_call" | custom-call | flops 2147483648 | bytes 4194304 | tf_op jit(solution)/shard_map/rest/pallas_call | solution.py:228
  49.5 0.6 collective-permute-start.10
  50.0 0.0 collective-permute-done.7
  50.1 1.5 %collective-permute-start.8 = (f32[4,32,128]{2,1,0:T(8,128)S(1)}, f32[4,32,128]{2,1,0:T(8,128)S(1)}, u32[]{:S(2)}, u32[]{:S(2)}) collective-permute-start(f32[4,32,128]{2,1,0:T(8,128)S(1)} %get-tuple-element.53), channel_id=1, source_target_pairs={{0,24},{4,28},{8,16},{12,20},{16,8},{20,12},{24,0},{28,4},{1,25},{... | collective-permute-start | bytes 196616 | tf_op jit(solution)/shard_map/ppermute | solution.py:327
  51.6 12.0 %collective-permute-start.9 = (f32[4,32,128]{2,1,0:T(8,128)S(1)}, f32[4,32,128]{2,1,0:T(8,128)S(1)}, u32[]{:S(2)}, u32[]{:S(2)}) collective-permute-start(f32[4,32,128]{2,1,0:T(8,128)S(1)} %get-tuple-element.54), channel_id=1, source_target_pairs={{0,16},{4,20},{8,24},{12,28},{16,0},{20,4},{24,8},{28,12},{1,17},{... | collective-permute-start | bytes 196616 | tf_op jit(solution)/shard_map/ppermute | solution.py:327
  63.6 0.0 collective-permute-done.10
  63.6 0.6 collective-permute-start.11
  64.2 0.0 collective-permute-done.8
  64.2 3.8 %collective-permute-done.9 = f32[4,32,128]{2,1,0:T(8,128)S(1)} collective-permute-done((f32[4,32,128]{2,1,0:T(8,128)S(1)}, f32[4,32,128]{2,1,0:T(8,128)S(1)}, u32[]{:S(2)}, u32[]{:S(2)}) %collective-permute-start.9) | collective-permute-done | bytes 65568 | tf_op jit(solution)/shard_map/ppermute | solution.py:327
  68.0 0.4 collective-permute-done.11
  68.5 1.5 %collective-permute-start.14 = (f32[2,32,128]{2,1,0:T(8,128)S(1)}, f32[2,32,128]{2,1,0:T(8,128)S(1)}, u32[]{:S(2)}, u32[]{:S(2)}) collective-permute-start(f32[2,32,128]{2,1,0:T(8,128)S(1)} %broadcast_select_fusion), channel_id=1, source_target_pairs={{0,6},{1,7},{2,4},{3,5},{4,2},{5,3},{6,0},{7,1},{8,14},{9,15},{10,... | collective-permute-start | bytes 98312 | tf_op jit(solution)/shard_map/ppermute | solution.py:365
  70.0 1.5 %collective-permute-start.13 = (f32[2,32,128]{2,1,0:T(8,128)S(1)}, f32[2,32,128]{2,1,0:T(8,128)S(1)}, u32[]{:S(2)}, u32[]{:S(2)}) collective-permute-start(f32[2,32,128]{2,1,0:T(8,128)S(1)} %broadcast_select_fusion), channel_id=1, source_target_pairs={{0,4},{4,0},{8,12},{12,8},{16,20},{20,16},{24,28},{28,24},{1,5},{5... | collective-permute-start | bytes 98312 | tf_op jit(solution)/shard_map/ppermute | solution.py:327
  71.5 0.5 collective-permute-start.12
  72.0 1.4 %collective-permute-done.14 = f32[2,32,128]{2,1,0:T(8,128)S(1)} collective-permute-done((f32[2,32,128]{2,1,0:T(8,128)S(1)}, f32[2,32,128]{2,1,0:T(8,128)S(1)}, u32[]{:S(2)}, u32[]{:S(2)}) %collective-permute-start.14) | collective-permute-done | bytes 32800 | tf_op jit(solution)/shard_map/ppermute | solution.py:365
  73.4 0.5 collective-permute-done.13
  73.9 1.5 %collective-permute-done.12 = f32[2,32,128]{2,1,0:T(8,128)S(1)} collective-permute-done((f32[2,32,128]{2,1,0:T(8,128)S(1)}, f32[2,32,128]{2,1,0:T(8,128)S(1)}, u32[]{:S(2)}, u32[]{:S(2)}) %collective-permute-start.12) | collective-permute-done | bytes 32800 | tf_op jit(solution)/shard_map/ppermute | solution.py:327
  75.4 0.1 collective-permute-start.15
  75.5 0.9 %unpack.2 = (f32[2,16,32,32]{3,2,1,0:T(8,128)}, f32[128,128]{1,0:T(8,128)}) custom-call(s32[1]{0:T(128)} %bitcast.5.core_ref.order_ref, f32[2,32,128]{2,1,0:T(8,128)S(1)} %add_add_fusion.packed_ref, f32[128,128]{1,0:T(8,128)S(1)} %get-tuple-element.45.power_ref), custom_call_target="tpu_custom_call" | custom-call | tf_op jit(solution)/shard_map/unpack/pallas_call | solution.py:308
  76.4 0.3 collective-permute-done.15.packed_ref
  76.7 0.9 %unpack.3 = (f32[2,16,32,32]{3,2,1,0:T(8,128)}, f32[128,128]{1,0:T(8,128)}) custom-call(s32[1]{0:T(128)} %bitcast.order_ref, f32[2,32,128]{2,1,0:T(8,128)S(1)} %collective-permute-done.15.packed_ref, f32[128,128]{1,0:T(8,128)} %get-tuple-element.46.power_ref, f32[2,16,32,32]{3,2,1,0:T(8,128)} %get-tuple-element.47.refs_0_), custom_call_target="tpu_custom_call", output_to_operand_aliasing={{0}: (3, {}), {1}: (2, {})} | custom-call | tf_op jit(solution)/shard_map/unpack/pallas_call | solution.py:308
  (6 shorter events, 0.1 us)
Async XLA Ops:
  0.6 1.6 %copy-start = (f32[528,1024]{1,0:T(8,128)S(1)}, f32[528,1024]{1,0:T(8,128)}, u32[]{:S(2)}) copy-start(f32[528,1024]{1,0:T(8,128)} %snapshots_ref.1) | copy-start | bytes 6488068
  2.2 43.2 %copy-start.2 = (s32[32]{0:T(128)S(1)}, s32[32]{0:T(128)}, u32[]{:S(2)}) copy-start(s32[32]{0:T(128)} %starts_ref.3) | copy-start | bytes 388
  2.6 18.1 %collective-permute-start = (f32[528,128]{1,0:T(8,128)S(1)}, f32[528,128]{1,0:T(8,128)S(1)}, u32[]{:S(2)}, u32[]{:S(2)}) collective-permute-start(f32[528,128]{1,0:T(8,128)S(1)} %get-tuple-element.26), channel_id=1, source_target_pairs={{0,16},{4,20},{8,24},{12,28},{16,0},{20,4},{24,8},{28,12},{1,17},{... | collective-permute-start | bytes 811016 | tf_op jit(solution)/shard_map/ppermute | solution.py:327
  6.7 17.2 %collective-permute-start.1 = (f32[528,128]{1,0:T(8,128)S(1)}, f32[528,128]{1,0:T(8,128)S(1)}, u32[]{:S(2)}, u32[]{:S(2)}) collective-permute-start(f32[528,128]{1,0:T(8,128)S(1)} %get-tuple-element.27), channel_id=1, source_target_pairs={{0,8},{4,12},{8,0},{12,4},{16,24},{20,28},{24,16},{28,20},{1,9},{5... | collective-permute-start | bytes 811016 | tf_op jit(solution)/shard_map/ppermute | solution.py:327
  8.3 27.2 %collective-permute-start.2 = (f32[528,128]{1,0:T(8,128)S(1)}, f32[528,128]{1,0:T(8,128)S(1)}, u32[]{:S(2)}, u32[]{:S(2)}) collective-permute-start(f32[528,128]{1,0:T(8,128)S(1)} %get-tuple-element.28), channel_id=1, source_target_pairs={{0,4},{4,0},{8,12},{12,8},{16,20},{20,16},{24,28},{28,24},{1,5},{5... | collective-permute-start | bytes 811016 | tf_op jit(solution)/shard_map/ppermute | solution.py:327
  9.8 25.8 %collective-permute-start.3 = (f32[528,128]{1,0:T(8,128)S(1)}, f32[528,128]{1,0:T(8,128)S(1)}, u32[]{:S(2)}, u32[]{:S(2)}) collective-permute-start(f32[528,128]{1,0:T(8,128)S(1)} %get-tuple-element.29), channel_id=1, source_target_pairs={{0,20},{4,16},{8,28},{12,24},{16,4},{20,0},{24,12},{28,8},{1,21},{... | collective-permute-start | bytes 811016 | tf_op jit(solution)/shard_map/ppermute | solution.py:327
  10.1 25.5 %collective-permute-start.4 = (f32[528,128]{1,0:T(8,128)S(1)}, f32[528,128]{1,0:T(8,128)S(1)}, u32[]{:S(2)}, u32[]{:S(2)}) collective-permute-start(f32[528,128]{1,0:T(8,128)S(1)} %get-tuple-element.30), channel_id=1, source_target_pairs={{0,12},{4,8},{8,4},{12,0},{16,28},{20,24},{24,20},{28,16},{1,13},{... | collective-permute-start | bytes 811016 | tf_op jit(solution)/shard_map/ppermute | solution.py:327
  20.8 19.0 %collective-permute-start.5 = (f32[528,128]{1,0:T(8,128)S(1)}, f32[528,128]{1,0:T(8,128)S(1)}, u32[]{:S(2)}, u32[]{:S(2)}) collective-permute-start(f32[528,128]{1,0:T(8,128)S(1)} %get-tuple-element.31), channel_id=1, source_target_pairs={{0,24},{4,28},{8,16},{12,20},{16,8},{20,12},{24,0},{28,4},{1,25},{... | collective-permute-start | bytes 811016 | tf_op jit(solution)/shard_map/ppermute | solution.py:327
  23.9 21.5 %collective-permute-start.6 = (f32[528,128]{1,0:T(8,128)S(1)}, f32[528,128]{1,0:T(8,128)S(1)}, u32[]{:S(2)}, u32[]{:S(2)}) collective-permute-start(f32[528,128]{1,0:T(8,128)S(1)} %get-tuple-element.37), channel_id=1, source_target_pairs={{0,28},{4,24},{8,20},{12,16},{16,12},{20,8},{24,4},{28,0},{1,29},{... | collective-permute-start | bytes 811016 | tf_op jit(solution)/shard_map/ppermute | solution.py:327
  39.8 0.7 copy-start.1
  47.8 2.3 %collective-permute-start.7 = (f32[8,32,128]{2,1,0:T(8,128)S(1)}, f32[8,32,128]{2,1,0:T(8,128)S(1)}, u32[]{:S(2)}, u32[]{:S(2)}) collective-permute-start(f32[8,32,128]{2,1,0:T(8,128)S(1)} %get-tuple-element.39), channel_id=1, source_target_pairs={{0,1},{1,0},{2,3},{3,2},{4,5},{5,4},{6,7},{7,6},{8,9},{9,8},{10,11... | collective-permute-start | bytes 393224 | tf_op jit(solution)/shard_map/ppermute | solution.py:327
  49.5 14.1 %collective-permute-start.10 = (f32[8,32,128]{2,1,0:T(8,128)S(1)}, f32[8,32,128]{2,1,0:T(8,128)S(1)}, u32[]{:S(2)}, u32[]{:S(2)}) collective-permute-start(f32[8,32,128]{2,1,0:T(8,128)S(1)} %get-tuple-element.43), channel_id=1, source_target_pairs={{0,1},{1,0},{2,3},{3,2},{4,5},{5,4},{6,7},{7,6},{8,9},{9,8},{10,11... | collective-permute-start | bytes 393224 | tf_op jit(solution)/shard_map/ppermute | solution.py:327
  50.1 14.1 %collective-permute-start.8 = (f32[4,32,128]{2,1,0:T(8,128)S(1)}, f32[4,32,128]{2,1,0:T(8,128)S(1)}, u32[]{:S(2)}, u32[]{:S(2)}) collective-permute-start(f32[4,32,128]{2,1,0:T(8,128)S(1)} %get-tuple-element.53), channel_id=1, source_target_pairs={{0,24},{4,28},{8,16},{12,20},{16,8},{20,12},{24,0},{28,4},{1,25},{... | collective-permute-start | bytes 196616 | tf_op jit(solution)/shard_map/ppermute | solution.py:327
  51.6 16.4 %collective-permute-start.9 = (f32[4,32,128]{2,1,0:T(8,128)S(1)}, f32[4,32,128]{2,1,0:T(8,128)S(1)}, u32[]{:S(2)}, u32[]{:S(2)}) collective-permute-start(f32[4,32,128]{2,1,0:T(8,128)S(1)} %get-tuple-element.54), channel_id=1, source_target_pairs={{0,16},{4,20},{8,24},{12,28},{16,0},{20,4},{24,8},{28,12},{1,17},{... | collective-permute-start | bytes 196616 | tf_op jit(solution)/shard_map/ppermute | solution.py:327
  63.6 4.8 %collective-permute-start.11 = (f32[4,32,128]{2,1,0:T(8,128)S(1)}, f32[4,32,128]{2,1,0:T(8,128)S(1)}, u32[]{:S(2)}, u32[]{:S(2)}) collective-permute-start(f32[4,32,128]{2,1,0:T(8,128)S(1)} %get-tuple-element.55), channel_id=1, source_target_pairs={{0,8},{4,12},{8,0},{12,4},{16,24},{20,28},{24,16},{28,20},{1,9},{5... | collective-permute-start | bytes 196616 | tf_op jit(solution)/shard_map/ppermute | solution.py:327
  68.5 4.9 %collective-permute-start.14 = (f32[2,32,128]{2,1,0:T(8,128)S(1)}, f32[2,32,128]{2,1,0:T(8,128)S(1)}, u32[]{:S(2)}, u32[]{:S(2)}) collective-permute-start(f32[2,32,128]{2,1,0:T(8,128)S(1)} %broadcast_select_fusion), channel_id=1, source_target_pairs={{0,6},{1,7},{2,4},{3,5},{4,2},{5,3},{6,0},{7,1},{8,14},{9,15},{10,... | collective-permute-start | bytes 98312 | tf_op jit(solution)/shard_map/ppermute | solution.py:365
  70.0 3.9 %collective-permute-start.13 = (f32[2,32,128]{2,1,0:T(8,128)S(1)}, f32[2,32,128]{2,1,0:T(8,128)S(1)}, u32[]{:S(2)}, u32[]{:S(2)}) collective-permute-start(f32[2,32,128]{2,1,0:T(8,128)S(1)} %broadcast_select_fusion), channel_id=1, source_target_pairs={{0,4},{4,0},{8,12},{12,8},{16,20},{20,16},{24,28},{28,24},{1,5},{5... | collective-permute-start | bytes 98312 | tf_op jit(solution)/shard_map/ppermute | solution.py:327
  71.5 3.9 %collective-permute-start.12 = (f32[2,32,128]{2,1,0:T(8,128)S(1)}, f32[2,32,128]{2,1,0:T(8,128)S(1)}, u32[]{:S(2)}, u32[]{:S(2)}) collective-permute-start(f32[2,32,128]{2,1,0:T(8,128)S(1)} %get-tuple-element.50), channel_id=1, source_target_pairs={{0,2},{1,3},{2,0},{3,1},{4,6},{5,7},{6,4},{7,5},{8,10},{9,11},{10,... | collective-permute-start | bytes 98312 | tf_op jit(solution)/shard_map/ppermute | solution.py:327
  75.4 1.3 %collective-permute-start.15 = (f32[2,32,128]{2,1,0:T(8,128)S(1)}, f32[2,32,128]{2,1,0:T(8,128)S(1)}, u32[]{:S(2)}, u32[]{:S(2)}) collective-permute-start(f32[2,32,128]{2,1,0:T(8,128)S(1)} %add_add_fusion.packed_ref), channel_id=1, source_target_pairs={{0,1},{1,0},{2,3},{3,2},{4,5},{5,4},{6,7},{7,6},{8,9},{9,8},{10,11... | collective-permute-start | bytes 98312 | tf_op jit(solution)/shard_map/ppermute | solution.py:327

commit v6 on v5

--- a/solution.py
+++ b/solution.py
@@ -111,6 +111,7 @@
 
 def cut(order, snapshots):
     rows = snapshots.shape[0]
+    grant = 52 if len(order) == 1 else 50
     return pl.pallas_call(
         functools.partial(cut_kernel, order),
         name="cut",
@@ -118,7 +119,10 @@
         out_specs=[pl.BlockSpec(memory_space=VMEM)] * len(order),
         out_shape=[jax.ShapeDtypeStruct((rows, LANES), F32)] * len(order),
         scratch_shapes=[pltpu.SemaphoreType.DMA((len(order),))],
-        compiler_params=pltpu.CompilerParams(vmem_limit_bytes=8 << 20),
+        compiler_params=pltpu.CompilerParams(vmem_limit_bytes=grant << 20),
+        cost_estimate=pl.CostEstimate(
+            flops=len(order) << 30, bytes_accessed=len(order) << 20, transcendentals=0
+        ),
     )(snapshots)
 
 
@@ -333,8 +337,10 @@
     z, x = me // 2, me % 2
     order = (4, 2, 1, 5, 3, 6, 7)
     rows = snapshots.shape[0]
-    *pieces, own = cut((*order, 0), snapshots)
-    pieces = [swap(p, "tm", k) for p, k in zip(pieces, order)]
+    (first,) = cut(order[:1], snapshots)
+    first = swap(first, "tm", order[0])
+    *pieces, own = cut((*order[1:], 0), snapshots)
+    pieces = [first] + [swap(p, "tm", k) for p, k in zip(pieces, order[1:])]
     pieces, last = pieces[:-1] + [own], pieces[-1]
     where = jnp.stack([me ^ k for k in (*order[:-1], 0)])
     late_part = me ^ order[-1]

time: 77.8 us -> 75.4 us (0.969)
  starting transfers between devices: 36.2 us -> 31.4 us
  waiting for transfers between devices: 18.3 us -> 22.4 us
  other arithmetic: 5.22 us -> 3.9 us
  local copies, waits for them, and re-layouts: 3.66 us -> 2.36 us
  Pallas kernels: 9.44 us -> 10.3 us
    ppermute x15, starting transfers between devices: 34.7 us -> 29.8 us  [swap(): lax.ppermute(value, axis, [(i, i ^ bits) for i in range(lax.axis_size(axi...]
    ppermute x15, waiting for transfers between devices: 17 us -> 21.1 us  [swap(): lax.ppermute(value, axis, [(i, i ^ bits) for i in range(lax.axis_size(axi...]
    pallas_call x1 -> x2, Pallas kernels: 0.39 us -> 1.32 us  [cut(): pl.pallas_call(functools.partial(cut_kernel, order), name='cut', in_specs...]
  transfers between devices with their start and end apart: 16 -> 16, of which waited for: 9 -> 8; matrix products, arithmetic and copies ran while one was open for 8% -> 6% of each run, Pallas kernels for 7% -> 8%
where the time goes in v6:
time: 75.4 us; the launch traced here: 75.2 us
  starting transfers between devices  31.4 us (42%)
  waiting for transfers between devices  22.4 us (30%)
  Pallas kernels  10.3 us (14%)
  between operations  4.73 us (6%)
  other arithmetic  3.9 us (5%)
  local copies, waits for them, and re-layouts  2.36 us (3%)
    ppermute x15, starting transfers between devices, swap(): lax.ppermute(value, axis, [(i, i ^ bits) for i in range(lax.axis_size(axi...  29.8 us
    ppermute x15, waiting for transfers between devices, swap(): lax.ppermute(value, axis, [(i, i ^ bits) for i in range(lax.axis_size(axi...  21.1 us
    pallas_call x1, Pallas kernels, early(): pl.pallas_call(functools.partial(early_kernel, rows), name='early', in_sp...  3.3 us
    pallas_call x1, Pallas kernels, late(): pl.pallas_call(late_kernel, name='late', in_specs=[smem] * 6 + [vmem] * 5...  2.37 us
    pallas_call x2, Pallas kernels, unpack(): pl.pallas_call(functools.partial(unpack_kernel, factor), name='unpack', i...  1.74 us
    unnamed x6, local copies, waits for them, and re-layouts  1.62 us
    pallas_call x1, Pallas kernels, rest(): pl.pallas_call(rest_kernel, name='rest', in_specs=[smem] * 3 + [vmem] * 2...  1.61 us
    ppermute x1, starting transfers between devices, spread_small(): lax.ppermute(other, ('tm', 'space'), [(i * 4 + s, (i ^ 1) * 4 + (s ^ 2))...  1.57 us
  transfers between devices with their start and end apart: 16, of which 8 were waited for; matrix products, arithmetic and copies ran while one was open for 6% of the time, Pallas kernels for 8%

profile of v6, /device:TPU:0, one launch (start us, length us, event | category | flops | bytes accessed | tf_op | source)
XLA Modules:
  0.0 75.2 jit_solution(3340969535881229015)
XLA Ops:
  0.6 1.0 %cut.2 = f32[528,128]{1,0:T(8,128)S(1)} custom-call(f32[528,1024]{1,0:T(8,128)} %snapshots_ref.3), custom_call_target="tpu_custom_call" | custom-call | flops 1073741824 | bytes 1048576 | tf_op jit(solution)/shard_map/cut/pallas_call | solution.py:115
  1.6 4.1 %collective-permute-start = (f32[528,128]{1,0:T(8,128)S(1)}, f32[528,128]{1,0:T(8,128)S(1)}, u32[]{:S(2)}, u32[]{:S(2)}) collective-permute-start(f32[528,128]{1,0:T(8,128)S(1)} %cut.2), channel_id=1, source_target_pairs={{0,16},{4,20},{8,24},{12,28},{16,0},{20,4},{24,8},{28,12},{1,17},{... | collective-permute-start | bytes 811016 | tf_op jit(solution)/shard_map/ppermute | solution.py:331
  5.7 0.0 copy-start
  5.7 1.6 %copy-done = f32[528,1024]{1,0:T(8,128)S(1)} copy-done((f32[528,1024]{1,0:T(8,128)S(1)}, f32[528,1024]{1,0:T(8,128)}, u32[]{:S(2)}) %copy-start) | copy-done | bytes 2162712
  7.3 0.0 copy-start.2
  7.3 0.0 copy-start.1
  7.3 0.3 cut.3
  7.7 1.6 %collective-permute-start.1 = (f32[528,128]{1,0:T(8,128)S(1)}, f32[528,128]{1,0:T(8,128)S(1)}, u32[]{:S(2)}, u32[]{:S(2)}) collective-permute-start(f32[528,128]{1,0:T(8,128)S(1)} %get-tuple-element.25), channel_id=1, source_target_pairs={{0,8},{4,12},{8,0},{12,4},{16,24},{20,28},{24,16},{28,20},{1,9},{5... | collective-permute-start | bytes 811016 | tf_op jit(solution)/shard_map/ppermute | solution.py:331
  9.3 1.5 %collective-permute-start.2 = (f32[528,128]{1,0:T(8,128)S(1)}, f32[528,128]{1,0:T(8,128)S(1)}, u32[]{:S(2)}, u32[]{:S(2)}) collective-permute-start(f32[528,128]{1,0:T(8,128)S(1)} %get-tuple-element.26), channel_id=1, source_target_pairs={{0,4},{4,0},{8,12},{12,8},{16,20},{20,16},{24,28},{28,24},{1,5},{5... | collective-permute-start | bytes 811016 | tf_op jit(solution)/shard_map/ppermute | solution.py:331
  10.8 0.3 collective-permute-start.3
  11.1 1.4 %collective-permute-start.4 = (f32[528,128]{1,0:T(8,128)S(1)}, f32[528,128]{1,0:T(8,128)S(1)}, u32[]{:S(2)}, u32[]{:S(2)}) collective-permute-start(f32[528,128]{1,0:T(8,128)S(1)} %get-tuple-element.28), channel_id=1, source_target_pairs={{0,12},{4,8},{8,4},{12,0},{16,28},{20,24},{24,20},{28,16},{1,13},{... | collective-permute-start | bytes 811016 | tf_op jit(solution)/shard_map/ppermute | solution.py:331
  12.5 0.6 multiply_reduce_fusion
  13.9 0.0 copy-done.2
  13.9 1.3 %cosine_multiply_fusion = (f32[128,256]{1,0:T(8,128)}, f32[128,256]{1,0:T(8,128)}) fusion(s32[128]{0:T(128)S(1)} %copy-done.2, f32[256]{0:T(256)S(1)} %get-tuple-element.57, f32[256]{0:T(256)S(1)} %get-tuple-element.58), kind=kLoop, calls=%fused_computation.8 | loop fusion | flops 524288 | bytes 264704 | tf_op jit(solution)/shard_map/mul | solution.py:33
  15.2 0.0 copy-done.1
  15.2 0.7 fusion.7
  15.9 3.8 %collective-permute-done.refs_0_ = f32[528,128]{1,0:T(8,128)S(1)} collective-permute-done((f32[528,128]{1,0:T(8,128)S(1)}, f32[528,128]{1,0:T(8,128)S(1)}, u32[]{:S(2)}, u32[]{:S(2)}) %collective-permute-start) | collective-permute-done | bytes 270368 | tf_op jit(solution)/shard_map/ppermute | solution.py:331
  19.7 3.1 %collective-permute-start.5 = (f32[528,128]{1,0:T(8,128)S(1)}, f32[528,128]{1,0:T(8,128)S(1)}, u32[]{:S(2)}, u32[]{:S(2)}) collective-permute-start(f32[528,128]{1,0:T(8,128)S(1)} %get-tuple-element.29), channel_id=1, source_target_pairs={{0,24},{4,28},{8,16},{12,20},{16,8},{20,12},{24,0},{28,4},{1,25},{... | collective-permute-start | bytes 811016 | tf_op jit(solution)/shard_map/ppermute | solution.py:331
  22.8 0.1 pad_add_fusion.firsts_ref
  22.9 0.0 collective-permute-done.1.refs_1_
  22.9 5.8 %collective-permute-start.6 = (f32[528,128]{1,0:T(8,128)S(1)}, f32[528,128]{1,0:T(8,128)S(1)}, u32[]{:S(2)}, u32[]{:S(2)}) collective-permute-start(f32[528,128]{1,0:T(8,128)S(1)} %get-tuple-element.35), channel_id=1, source_target_pairs={{0,28},{4,24},{8,20},{12,16},{16,12},{20,8},{24,4},{28,0},{1,29},{... | collective-permute-start | bytes 811016 | tf_op jit(solution)/shard_map/ppermute | solution.py:331
  28.8 0.1 pad_add_fusion.1.firsts_ref
  29.6 0.7 dynamic_slice.3
  32.8 0.1 stack.51.where_ref
  32.9 1.0 %pad_maximum_fusion.table_ref = f32[256,256]{1,0:T(8,128)S(1)} fusion(f32[128,256]{1,0:T(8,128)} %get-tuple-element.56, f32[128,256]{1,0:T(8,128)} %get-tuple-element.55), kind=kLoop, calls=%fused_computation | loop fusion | flops 65536 | bytes 524288 | tf_op jit(solution)/shard_map/concatenate | solution.py:32
  33.9 0.0 collective-permute-done.2.refs_2_
  33.9 0.0 collective-permute-done.3.refs_3_
  33.9 10.6 %collective-permute-done.4.refs_4_ = f32[528,128]{1,0:T(8,128)S(1)} collective-permute-done((f32[528,128]{1,0:T(8,128)S(1)}, f32[528,128]{1,0:T(8,128)S(1)}, u32[]{:S(2)}, u32[]{:S(2)}) %collective-permute-start.4) | collective-permute-done | bytes 270368 | tf_op jit(solution)/shard_map/ppermute | solution.py:331
  44.5 0.0 collective-permute-done.5.refs_5_
  44.5 3.3 %early.1 = (f32[1288,128]{1,0:T(8,128)S(1)}, f32[10240,128]{1,0:T(8,128)S(1)}, f32[128,128]{1,0:T(8,128)S(1)}, bf16[512,256]{1,0:T(8,128)(2,1)S(1)}) custom-call(s32[1]{0:T(128)} %bitcast.1.base_ref, s32[1]{0:T(128)} %bitcast.3.corner_ref, s32[7]{0:T(128)S(1)} %stack.51.where_ref, s32[32]{0:T(128)S(1)} %copy-done.1, ...), custom_call_target="tpu_custom_call" | custom-call | flops 1207959552 | bytes 4194304 | tf_op jit(solution)/shard_map/early/pallas_call | solution.py:150
  47.8 0.0 collective-permute-done.6.piece_ref
  47.8 2.4 %late.1 = (f32[128,128]{1,0:T(8,128)S(1)}, f32[10240,128]{1,0:T(8,128)S(1)}, f32[8,32,128]{2,1,0:T(8,128)S(1)}, f32[4,32,128]{2,1,0:T(8,128)S(1)}, f32[4,32,128]{2,1,0:T(8,128)S(1)}) custom-call(s32[1]{0:T(128)} %bitcast.1.base_ref, s32[1]{0:T(128)} %bitcast.3.corner_ref, s32[1]{0:T(128)} %bitcast.4.where_ref, s32[1]{0:T(128)} %bitcast.5.core_ref.order_ref, ...), custom_call_target="tpu_custom_call" | custom-call | flops 3221225472 | bytes 8388608 | tf_op jit(solution)/shard_map/late/pallas_call | solution.py:216
  50.2 0.1 collective-permute-start.7
  50.2 1.6 %rest.1 = (f32[8,32,128]{2,1,0:T(8,128)S(1)}, f32[4,32,128]{2,1,0:T(8,128)S(1)}, f32[4,32,128]{2,1,0:T(8,128)S(1)}) custom-call(s32[1]{0:T(128)} %bitcast.1.base_ref, s32[1]{0:T(128)} %bitcast.5.core_ref.order_ref, s32[2]{0:T(128)S(1)} %pad_add_fusion.1.firsts_ref, f32[10240,128]{1,0:T(8,128)S(1)} %get-tuple-element.33.spec_ref, ...), custom_call_target="tpu_custom_call" | custom-call | flops 2147483648 | bytes 4194304 | tf_op jit(solution)/shard_map/rest/pallas_call | solution.py:232
  51.9 0.6 collective-permute-start.10
  52.4 0.0 collective-permute-done.7
  52.5 2.4 %collective-permute-start.8 = (f32[4,32,128]{2,1,0:T(8,128)S(1)}, f32[4,32,128]{2,1,0:T(8,128)S(1)}, u32[]{:S(2)}, u32[]{:S(2)}) collective-permute-start(f32[4,32,128]{2,1,0:T(8,128)S(1)} %get-tuple-element.51), channel_id=1, source_target_pairs={{0,24},{4,28},{8,16},{12,20},{16,8},{20,12},{24,0},{28,4},{1,25},{... | collective-permute-start | bytes 196616 | tf_op jit(solution)/shard_map/ppermute | solution.py:331
  54.9 6.3 %collective-permute-start.9 = (f32[4,32,128]{2,1,0:T(8,128)S(1)}, f32[4,32,128]{2,1,0:T(8,128)S(1)}, u32[]{:S(2)}, u32[]{:S(2)}) collective-permute-start(f32[4,32,128]{2,1,0:T(8,128)S(1)} %get-tuple-element.52), channel_id=1, source_target_pairs={{0,16},{4,20},{8,24},{12,28},{16,0},{20,4},{24,8},{28,12},{1,17},{... | collective-permute-start | bytes 196616 | tf_op jit(solution)/shard_map/ppermute | solution.py:331
  61.2 0.0 collective-permute-done.10
  61.2 0.6 collective-permute-start.11
  61.8 0.0 collective-permute-done.8
  61.8 3.8 %collective-permute-done.9 = f32[4,32,128]{2,1,0:T(8,128)S(1)} collective-permute-done((f32[4,32,128]{2,1,0:T(8,128)S(1)}, f32[4,32,128]{2,1,0:T(8,128)S(1)}, u32[]{:S(2)}, u32[]{:S(2)}) %collective-permute-start.9) | collective-permute-done | bytes 65568 | tf_op jit(solution)/shard_map/ppermute | solution.py:331
  65.6 0.4 collective-permute-done.11
  66.1 1.6 %collective-permute-start.14 = (f32[2,32,128]{2,1,0:T(8,128)S(1)}, f32[2,32,128]{2,1,0:T(8,128)S(1)}, u32[]{:S(2)}, u32[]{:S(2)}) collective-permute-start(f32[2,32,128]{2,1,0:T(8,128)S(1)} %broadcast_select_fusion), channel_id=1, source_target_pairs={{0,6},{1,7},{2,4},{3,5},{4,2},{5,3},{6,0},{7,1},{8,14},{9,15},{10,... | collective-permute-start | bytes 98312 | tf_op jit(solution)/shard_map/ppermute | solution.py:371
  67.6 1.5 %collective-permute-start.13 = (f32[2,32,128]{2,1,0:T(8,128)S(1)}, f32[2,32,128]{2,1,0:T(8,128)S(1)}, u32[]{:S(2)}, u32[]{:S(2)}) collective-permute-start(f32[2,32,128]{2,1,0:T(8,128)S(1)} %broadcast_select_fusion), channel_id=1, source_target_pairs={{0,4},{4,0},{8,12},{12,8},{16,20},{20,16},{24,28},{28,24},{1,5},{5... | collective-permute-start | bytes 98312 | tf_op jit(solution)/shard_map/ppermute | solution.py:331
  69.1 0.5 collective-permute-start.12
  69.6 1.4 %collective-permute-done.14 = f32[2,32,128]{2,1,0:T(8,128)S(1)} collective-permute-done((f32[2,32,128]{2,1,0:T(8,128)S(1)}, f32[2,32,128]{2,1,0:T(8,128)S(1)}, u32[]{:S(2)}, u32[]{:S(2)}) %collective-permute-start.14) | collective-permute-done | bytes 32800 | tf_op jit(solution)/shard_map/ppermute | solution.py:371
  71.0 0.5 collective-permute-done.13
  71.5 1.5 %collective-permute-done.12 = f32[2,32,128]{2,1,0:T(8,128)S(1)} collective-permute-done((f32[2,32,128]{2,1,0:T(8,128)S(1)}, f32[2,32,128]{2,1,0:T(8,128)S(1)}, u32[]{:S(2)}, u32[]{:S(2)}) %collective-permute-start.12) | collective-permute-done | bytes 32800 | tf_op jit(solution)/shard_map/ppermute | solution.py:331
  73.0 0.1 collective-permute-start.15
  73.1 0.9 %unpack.2 = (f32[2,16,32,32]{3,2,1,0:T(8,128)}, f32[128,128]{1,0:T(8,128)}) custom-call(s32[1]{0:T(128)} %bitcast.5.core_ref.order_ref, f32[2,32,128]{2,1,0:T(8,128)S(1)} %add_add_fusion.packed_ref, f32[128,128]{1,0:T(8,128)S(1)} %get-tuple-element.43.power_ref), custom_call_target="tpu_custom_call" | custom-call | tf_op jit(solution)/shard_map/unpack/pallas_call | solution.py:312
  74.0 0.3 collective-permute-done.15.packed_ref
  74.3 0.9 %unpack.3 = (f32[2,16,32,32]{3,2,1,0:T(8,128)}, f32[128,128]{1,0:T(8,128)}) custom-call(s32[1]{0:T(128)} %bitcast.order_ref, f32[2,32,128]{2,1,0:T(8,128)S(1)} %collective-permute-done.15.packed_ref, f32[128,128]{1,0:T(8,128)} %get-tuple-element.44.power_ref, f32[2,16,32,32]{3,2,1,0:T(8,128)} %get-tuple-element.45.refs_0_), custom_call_target="tpu_custom_call", output_to_operand_aliasing={{0}: (3, {}), {1}: (2, {})} | custom-call | tf_op jit(solution)/shard_map/unpack/pallas_call | solution.py:312
  (6 shorter events, 0.1 us)
Async XLA Ops:
  1.6 18.1 %collective-permute-start = (f32[528,128]{1,0:T(8,128)S(1)}, f32[528,128]{1,0:T(8,128)S(1)}, u32[]{:S(2)}, u32[]{:S(2)}) collective-permute-start(f32[528,128]{1,0:T(8,128)S(1)} %cut.2), channel_id=1, source_target_pairs={{0,16},{4,20},{8,24},{12,28},{16,0},{20,4},{24,8},{28,12},{1,17},{... | collective-permute-start | bytes 811016 | tf_op jit(solution)/shard_map/ppermute | solution.py:331
  5.7 1.6 %copy-start = (f32[528,1024]{1,0:T(8,128)S(1)}, f32[528,1024]{1,0:T(8,128)}, u32[]{:S(2)}) copy-start(f32[528,1024]{1,0:T(8,128)} %snapshots_ref.3) | copy-start | bytes 6488068
  7.3 6.6 %copy-start.2 = (s32[128]{0:T(128)S(1)}, s32[128]{0:T(128)}, u32[]{:S(2)}) copy-start(s32[128]{0:T(128)} %param.5) | copy-start | bytes 1540
  7.3 7.9 %copy-start.1 = (s32[32]{0:T(128)S(1)}, s32[32]{0:T(128)}, u32[]{:S(2)}) copy-start(s32[32]{0:T(128)} %starts_ref.3) | copy-start | bytes 388
  7.7 15.3 %collective-permute-start.1 = (f32[528,128]{1,0:T(8,128)S(1)}, f32[528,128]{1,0:T(8,128)S(1)}, u32[]{:S(2)}, u32[]{:S(2)}) collective-permute-start(f32[528,128]{1,0:T(8,128)S(1)} %get-tuple-element.25), channel_id=1, source_target_pairs={{0,8},{4,12},{8,0},{12,4},{16,24},{20,28},{24,16},{28,20},{1,9},{5... | collective-permute-start | bytes 811016 | tf_op jit(solution)/shard_map/ppermute | solution.py:331
  9.3 24.6 %collective-permute-start.2 = (f32[528,128]{1,0:T(8,128)S(1)}, f32[528,128]{1,0:T(8,128)S(1)}, u32[]{:S(2)}, u32[]{:S(2)}) collective-permute-start(f32[528,128]{1,0:T(8,128)S(1)} %get-tuple-element.26), channel_id=1, source_target_pairs={{0,4},{4,0},{8,12},{12,8},{16,20},{20,16},{24,28},{28,24},{1,5},{5... | collective-permute-start | bytes 811016 | tf_op jit(solution)/shard_map/ppermute | solution.py:331
  10.8 23.1 %collective-permute-start.3 = (f32[528,128]{1,0:T(8,128)S(1)}, f32[528,128]{1,0:T(8,128)S(1)}, u32[]{:S(2)}, u32[]{:S(2)}) collective-permute-start(f32[528,128]{1,0:T(8,128)S(1)} %get-tuple-element.27), channel_id=1, source_target_pairs={{0,20},{4,16},{8,28},{12,24},{16,4},{20,0},{24,12},{28,8},{1,21},{... | collective-permute-start | bytes 811016 | tf_op jit(solution)/shard_map/ppermute | solution.py:331
  11.1 33.3 %collective-permute-start.4 = (f32[528,128]{1,0:T(8,128)S(1)}, f32[528,128]{1,0:T(8,128)S(1)}, u32[]{:S(2)}, u32[]{:S(2)}) collective-permute-start(f32[528,128]{1,0:T(8,128)S(1)} %get-tuple-element.28), channel_id=1, source_target_pairs={{0,12},{4,8},{8,4},{12,0},{16,28},{20,24},{24,20},{28,16},{1,13},{... | collective-permute-start | bytes 811016 | tf_op jit(solution)/shard_map/ppermute | solution.py:331
  19.7 24.7 %collective-permute-start.5 = (f32[528,128]{1,0:T(8,128)S(1)}, f32[528,128]{1,0:T(8,128)S(1)}, u32[]{:S(2)}, u32[]{:S(2)}) collective-permute-start(f32[528,128]{1,0:T(8,128)S(1)} %get-tuple-element.29), channel_id=1, source_target_pairs={{0,24},{4,28},{8,16},{12,20},{16,8},{20,12},{24,0},{28,4},{1,25},{... | collective-permute-start | bytes 811016 | tf_op jit(solution)/shard_map/ppermute | solution.py:331
  22.9 24.8 %collective-permute-start.6 = (f32[528,128]{1,0:T(8,128)S(1)}, f32[528,128]{1,0:T(8,128)S(1)}, u32[]{:S(2)}, u32[]{:S(2)}) collective-permute-start(f32[528,128]{1,0:T(8,128)S(1)} %get-tuple-element.35), channel_id=1, source_target_pairs={{0,28},{4,24},{8,20},{12,16},{16,12},{20,8},{24,4},{28,0},{1,29},{... | collective-permute-start | bytes 811016 | tf_op jit(solution)/shard_map/ppermute | solution.py:331
  50.2 2.3 %collective-permute-start.7 = (f32[8,32,128]{2,1,0:T(8,128)S(1)}, f32[8,32,128]{2,1,0:T(8,128)S(1)}, u32[]{:S(2)}, u32[]{:S(2)}) collective-permute-start(f32[8,32,128]{2,1,0:T(8,128)S(1)} %get-tuple-element.37), channel_id=1, source_target_pairs={{0,1},{1,0},{2,3},{3,2},{4,5},{5,4},{6,7},{7,6},{8,9},{9,8},{10,11... | collective-permute-start | bytes 393224 | tf_op jit(solution)/shard_map/ppermute | solution.py:331
  51.9 9.3 %collective-permute-start.10 = (f32[8,32,128]{2,1,0:T(8,128)S(1)}, f32[8,32,128]{2,1,0:T(8,128)S(1)}, u32[]{:S(2)}, u32[]{:S(2)}) collective-permute-start(f32[8,32,128]{2,1,0:T(8,128)S(1)} %get-tuple-element.41), channel_id=1, source_target_pairs={{0,1},{1,0},{2,3},{3,2},{4,5},{5,4},{6,7},{7,6},{8,9},{9,8},{10,11... | collective-permute-start | bytes 393224 | tf_op jit(solution)/shard_map/ppermute | solution.py:331
  52.5 9.3 %collective-permute-start.8 = (f32[4,32,128]{2,1,0:T(8,128)S(1)}, f32[4,32,128]{2,1,0:T(8,128)S(1)}, u32[]{:S(2)}, u32[]{:S(2)}) collective-permute-start(f32[4,32,128]{2,1,0:T(8,128)S(1)} %get-tuple-element.51), channel_id=1, source_target_pairs={{0,24},{4,28},{8,16},{12,20},{16,8},{20,12},{24,0},{28,4},{1,25},{... | collective-permute-start | bytes 196616 | tf_op jit(solution)/shard_map/ppermute | solution.py:331
  54.9 10.7 %collective-permute-start.9 = (f32[4,32,128]{2,1,0:T(8,128)S(1)}, f32[4,32,128]{2,1,0:T(8,128)S(1)}, u32[]{:S(2)}, u32[]{:S(2)}) collective-permute-start(f32[4,32,128]{2,1,0:T(8,128)S(1)} %get-tuple-element.52), channel_id=1, source_target_pairs={{0,16},{4,20},{8,24},{12,28},{16,0},{20,4},{24,8},{28,12},{1,17},{... | collective-permute-start | bytes 196616 | tf_op jit(solution)/shard_map/ppermute | solution.py:331
  61.2 4.8 %collective-permute-start.11 = (f32[4,32,128]{2,1,0:T(8,128)S(1)}, f32[4,32,128]{2,1,0:T(8,128)S(1)}, u32[]{:S(2)}, u32[]{:S(2)}) collective-permute-start(f32[4,32,128]{2,1,0:T(8,128)S(1)} %get-tuple-element.53), channel_id=1, source_target_pairs={{0,8},{4,12},{8,0},{12,4},{16,24},{20,28},{24,16},{28,20},{1,9},{5... | collective-permute-start | bytes 196616 | tf_op jit(solution)/shard_map/ppermute | solution.py:331
  66.1 4.9 %collective-permute-start.14 = (f32[2,32,128]{2,1,0:T(8,128)S(1)}, f32[2,32,128]{2,1,0:T(8,128)S(1)}, u32[]{:S(2)}, u32[]{:S(2)}) collective-permute-start(f32[2,32,128]{2,1,0:T(8,128)S(1)} %broadcast_select_fusion), channel_id=1, source_target_pairs={{0,6},{1,7},{2,4},{3,5},{4,2},{5,3},{6,0},{7,1},{8,14},{9,15},{10,... | collective-permute-start | bytes 98312 | tf_op jit(solution)/shard_map/ppermute | solution.py:371
  67.6 3.9 %collective-permute-start.13 = (f32[2,32,128]{2,1,0:T(8,128)S(1)}, f32[2,32,128]{2,1,0:T(8,128)S(1)}, u32[]{:S(2)}, u32[]{:S(2)}) collective-permute-start(f32[2,32,128]{2,1,0:T(8,128)S(1)} %broadcast_select_fusion), channel_id=1, source_target_pairs={{0,4},{4,0},{8,12},{12,8},{16,20},{20,16},{24,28},{28,24},{1,5},{5... | collective-permute-start | bytes 98312 | tf_op jit(solution)/shard_map/ppermute | solution.py:331
  69.1 3.9 %collective-permute-start.12 = (f32[2,32,128]{2,1,0:T(8,128)S(1)}, f32[2,32,128]{2,1,0:T(8,128)S(1)}, u32[]{:S(2)}, u32[]{:S(2)}) collective-permute-start(f32[2,32,128]{2,1,0:T(8,128)S(1)} %get-tuple-element.48), channel_id=1, source_target_pairs={{0,2},{1,3},{2,0},{3,1},{4,6},{5,7},{6,4},{7,5},{8,10},{9,11},{10,... | collective-permute-start | bytes 98312 | tf_op jit(solution)/shard_map/ppermute | solution.py:331
  73.0 1.3 %collective-permute-start.15 = (f32[2,32,128]{2,1,0:T(8,128)S(1)}, f32[2,32,128]{2,1,0:T(8,128)S(1)}, u32[]{:S(2)}, u32[]{:S(2)}) collective-permute-start(f32[2,32,128]{2,1,0:T(8,128)S(1)} %add_add_fusion.packed_ref), channel_id=1, source_target_pairs={{0,1},{1,0},{2,3},{3,2},{4,5},{5,4},{6,7},{7,6},{8,9},{9,8},{10,11... | collective-permute-start | bytes 98312 | tf_op jit(solution)/shard_map/ppermute | solution.py:331

commit v7 on v6

--- a/solution.py
+++ b/solution.py
@@ -16,6 +16,7 @@
 PITCH = NB + 8
 LATE = 8
 WINDOW = (LATE - 1) * NFFT // 2 + NFFT // 2 + NFFT + 8
+SPEC_ROWS = (2 * NF + 1) * PITCH
 CORE_STEP = 2
 F32 = jnp.float32
 BF16 = jnp.bfloat16
@@ -154,7 +155,7 @@
         out_specs=[vmem] * 4,
         out_shape=[
             jax.ShapeDtypeStruct((WINDOW, LANES), F32),
-            jax.ShapeDtypeStruct((2 * NF * PITCH, LANES), F32),
+            jax.ShapeDtypeStruct((SPEC_ROWS, LANES), F32),
             jax.ShapeDtypeStruct((NF, LANES), F32),
             jax.ShapeDtypeStruct((2 * NFFT, NFFT), BF16),
         ],
@@ -270,7 +271,7 @@
             jax.ShapeDtypeStruct((NF, LANES), F32),
             jax.ShapeDtypeStruct((NF // PACK, NB, LANES), F32),
         ],
-        scratch_shapes=[VMEM((2 * NFFT, NFFT), BF16), VMEM((2 * NF * PITCH, LANES), F32)],
+        scratch_shapes=[VMEM((2 * NFFT, NFFT), BF16), VMEM((SPEC_ROWS, LANES), F32)],
         compiler_params=pltpu.CompilerParams(vmem_limit_bytes=28 << 20),
     )(starts, table, series)
 
@@ -278,8 +279,8 @@
 def unpack_kernel(factor, order_ref, packed_ref, power_ref, *refs):
     out_ref, power_out, matrices, sems = refs[-4:]
     first = len(refs) == 4
-    power_copy = pltpu.make_async_copy(power_ref, power_out, sems.at[1])
     if first:
+        power_copy = pltpu.make_async_copy(power_ref, power_out, sems.at[1])
         power_copy.start()
     row = lax.broadcasted_iota(jnp.int32, (NB, NB), 0)
     column = lax.broadcasted_iota(jnp.int32, (NB, NB), 1)

time: 75.4 us -> 75.5 us (level)
  no operation moved by 1% of the time
where the time goes in v7:
time: 75.5 us; the launch traced here: 75.2 us
  starting transfers between devices  31.4 us (42%)
  waiting for transfers between devices  22.4 us (30%)
  Pallas kernels  10.4 us (14%)
  between operations  4.73 us (6%)
  other arithmetic  3.9 us (5%)
  local copies, waits for them, and re-layouts  2.36 us (3%)
    ppermute x15, starting transfers between devices, swap(): lax.ppermute(value, axis, [(i, i ^ bits) for i in range(lax.axis_size(axi...  29.9 us
    ppermute x15, waiting for transfers between devices, swap(): lax.ppermute(value, axis, [(i, i ^ bits) for i in range(lax.axis_size(axi...  21.1 us
    pallas_call x1, Pallas kernels, early(): pl.pallas_call(functools.partial(early_kernel, rows), name='early', in_sp...  3.3 us
    pallas_call x1, Pallas kernels, late(): pl.pallas_call(late_kernel, name='late', in_specs=[smem] * 6 + [vmem] * 5...  2.38 us
    pallas_call x2, Pallas kernels, unpack(): pl.pallas_call(functools.partial(unpack_kernel, factor), name='unpack', i...  1.74 us
    pallas_call x1, Pallas kernels, rest(): pl.pallas_call(rest_kernel, name='rest', in_specs=[smem] * 3 + [vmem] * 2...  1.63 us
    unnamed x6, local copies, waits for them, and re-layouts  1.62 us
    ppermute x1, starting transfers between devices, spread_small(): lax.ppermute(other, ('tm', 'space'), [(i * 4 + s, (i ^ 1) * 4 + (s ^ 2))...  1.54 us
  transfers between devices with their start and end apart: 16, of which 8 were waited for; matrix products, arithmetic and copies ran while one was open for 6% of the time, Pallas kernels for 8%

profile of v7, /device:TPU:0, one launch (start us, length us, event | category | flops | bytes accessed | tf_op | source)
XLA Modules:
  0.0 75.2 jit_solution(17084927884331053429)
XLA Ops:
  0.6 1.0 %cut.2 = f32[528,128]{1,0:T(8,128)S(1)} custom-call(f32[528,1024]{1,0:T(8,128)} %snapshots_ref.3), custom_call_target="tpu_custom_call" | custom-call | flops 1073741824 | bytes 1048576 | tf_op jit(solution)/shard_map/cut/pallas_call | solution.py:116
  1.6 4.1 %collective-permute-start = (f32[528,128]{1,0:T(8,128)S(1)}, f32[528,128]{1,0:T(8,128)S(1)}, u32[]{:S(2)}, u32[]{:S(2)}) collective-permute-start(f32[528,128]{1,0:T(8,128)S(1)} %cut.2), channel_id=1, source_target_pairs={{0,16},{4,20},{8,24},{12,28},{16,0},{20,4},{24,8},{28,12},{1,17},{... | collective-permute-start | bytes 811016 | tf_op jit(solution)/shard_map/ppermute | solution.py:332
  5.7 0.0 copy-start
  5.7 1.6 %copy-done = f32[528,1024]{1,0:T(8,128)S(1)} copy-done((f32[528,1024]{1,0:T(8,128)S(1)}, f32[528,1024]{1,0:T(8,128)}, u32[]{:S(2)}) %copy-start) | copy-done | bytes 2162712
  7.3 0.0 copy-start.2
  7.3 0.0 copy-start.1
  7.3 0.3 cut.3
  7.7 1.6 %collective-permute-start.1 = (f32[528,128]{1,0:T(8,128)S(1)}, f32[528,128]{1,0:T(8,128)S(1)}, u32[]{:S(2)}, u32[]{:S(2)}) collective-permute-start(f32[528,128]{1,0:T(8,128)S(1)} %get-tuple-element.25), channel_id=1, source_target_pairs={{0,8},{4,12},{8,0},{12,4},{16,24},{20,28},{24,16},{28,20},{1,9},{5... | collective-permute-start | bytes 811016 | tf_op jit(solution)/shard_map/ppermute | solution.py:332
  9.3 1.5 %collective-permute-start.2 = (f32[528,128]{1,0:T(8,128)S(1)}, f32[528,128]{1,0:T(8,128)S(1)}, u32[]{:S(2)}, u32[]{:S(2)}) collective-permute-start(f32[528,128]{1,0:T(8,128)S(1)} %get-tuple-element.26), channel_id=1, source_target_pairs={{0,4},{4,0},{8,12},{12,8},{16,20},{20,16},{24,28},{28,24},{1,5},{5... | collective-permute-start | bytes 811016 | tf_op jit(solution)/shard_map/ppermute | solution.py:332
  10.8 0.3 collective-permute-start.3
  11.1 1.4 %collective-permute-start.4 = (f32[528,128]{1,0:T(8,128)S(1)}, f32[528,128]{1,0:T(8,128)S(1)}, u32[]{:S(2)}, u32[]{:S(2)}) collective-permute-start(f32[528,128]{1,0:T(8,128)S(1)} %get-tuple-element.28), channel_id=1, source_target_pairs={{0,12},{4,8},{8,4},{12,0},{16,28},{20,24},{24,20},{28,16},{1,13},{... | collective-permute-start | bytes 811016 | tf_op jit(solution)/shard_map/ppermute | solution.py:332
  12.5 0.6 multiply_reduce_fusion
  13.9 0.0 copy-done.2
  13.9 1.3 %cosine_multiply_fusion = (f32[128,256]{1,0:T(8,128)}, f32[128,256]{1,0:T(8,128)}) fusion(s32[128]{0:T(128)S(1)} %copy-done.2, f32[256]{0:T(256)S(1)} %get-tuple-element.57, f32[256]{0:T(256)S(1)} %get-tuple-element.58), kind=kLoop, calls=%fused_computation.8 | loop fusion | flops 524288 | bytes 264704 | tf_op jit(solution)/shard_map/mul | solution.py:34
  15.2 0.0 copy-done.1
  15.2 0.7 fusion.7
  15.9 3.8 %collective-permute-done.refs_0_ = f32[528,128]{1,0:T(8,128)S(1)} collective-permute-done((f32[528,128]{1,0:T(8,128)S(1)}, f32[528,128]{1,0:T(8,128)S(1)}, u32[]{:S(2)}, u32[]{:S(2)}) %collective-permute-start) | collective-permute-done | bytes 270368 | tf_op jit(solution)/shard_map/ppermute | solution.py:332
  19.7 3.1 %collective-permute-start.5 = (f32[528,128]{1,0:T(8,128)S(1)}, f32[528,128]{1,0:T(8,128)S(1)}, u32[]{:S(2)}, u32[]{:S(2)}) collective-permute-start(f32[528,128]{1,0:T(8,128)S(1)} %get-tuple-element.29), channel_id=1, source_target_pairs={{0,24},{4,28},{8,16},{12,20},{16,8},{20,12},{24,0},{28,4},{1,25},{... | collective-permute-start | bytes 811016 | tf_op jit(solution)/shard_map/ppermute | solution.py:332
  22.8 0.1 pad_add_fusion.firsts_ref
  22.9 0.0 collective-permute-done.1.refs_1_
  22.9 5.8 %collective-permute-start.6 = (f32[528,128]{1,0:T(8,128)S(1)}, f32[528,128]{1,0:T(8,128)S(1)}, u32[]{:S(2)}, u32[]{:S(2)}) collective-permute-start(f32[528,128]{1,0:T(8,128)S(1)} %get-tuple-element.35), channel_id=1, source_target_pairs={{0,28},{4,24},{8,20},{12,16},{16,12},{20,8},{24,4},{28,0},{1,29},{... | collective-permute-start | bytes 811016 | tf_op jit(solution)/shard_map/ppermute | solution.py:332
  28.8 0.1 pad_add_fusion.1.firsts_ref
  29.6 0.7 dynamic_slice.3
  32.8 0.1 stack.51.where_ref
  32.9 1.0 %pad_maximum_fusion.table_ref = f32[256,256]{1,0:T(8,128)S(1)} fusion(f32[128,256]{1,0:T(8,128)} %get-tuple-element.56, f32[128,256]{1,0:T(8,128)} %get-tuple-element.55), kind=kLoop, calls=%fused_computation | loop fusion | flops 65536 | bytes 524288 | tf_op jit(solution)/shard_map/concatenate | solution.py:33
  33.9 0.0 collective-permute-done.2.refs_2_
  33.9 0.0 collective-permute-done.3.refs_3_
  33.9 10.6 %collective-permute-done.4.refs_4_ = f32[528,128]{1,0:T(8,128)S(1)} collective-permute-done((f32[528,128]{1,0:T(8,128)S(1)}, f32[528,128]{1,0:T(8,128)S(1)}, u32[]{:S(2)}, u32[]{:S(2)}) %collective-permute-start.4) | collective-permute-done | bytes 270368 | tf_op jit(solution)/shard_map/ppermute | solution.py:332
  44.5 0.0 collective-permute-done.5.refs_5_
  44.5 3.3 %early.1 = (f32[1288,128]{1,0:T(8,128)S(1)}, f32[10280,128]{1,0:T(8,128)S(1)}, f32[128,128]{1,0:T(8,128)S(1)}, bf16[512,256]{1,0:T(8,128)(2,1)S(1)}) custom-call(s32[1]{0:T(128)} %bitcast.1.base_ref, s32[1]{0:T(128)} %bitcast.3.corner_ref, s32[7]{0:T(128)S(1)} %stack.51.where_ref, s32[32]{0:T(128)S(1)} %copy-done.1, ...), custom_call_target="tpu_custom_call" | custom-call | flops 1207959552 | bytes 4194304 | tf_op jit(solution)/shard_map/early/pallas_call | solution.py:151
  47.8 0.0 collective-permute-done.6.piece_ref
  47.8 2.4 %late.1 = (f32[128,128]{1,0:T(8,128)S(1)}, f32[10280,128]{1,0:T(8,128)S(1)}, f32[8,32,128]{2,1,0:T(8,128)S(1)}, f32[4,32,128]{2,1,0:T(8,128)S(1)}, f32[4,32,128]{2,1,0:T(8,128)S(1)}) custom-call(s32[1]{0:T(128)} %bitcast.1.base_ref, s32[1]{0:T(128)} %bitcast.3.corner_ref, s32[1]{0:T(128)} %bitcast.4.where_ref, s32[1]{0:T(128)} %bitcast.5.core_ref.order_ref, ...), custom_call_target="tpu_custom_call" | custom-call | flops 3221225472 | bytes 8388608 | tf_op jit(solution)/shard_map/late/pallas_call | solution.py:217
  50.2 0.1 collective-permute-start.7
  50.2 1.6 %rest.1 = (f32[8,32,128]{2,1,0:T(8,128)S(1)}, f32[4,32,128]{2,1,0:T(8,128)S(1)}, f32[4,32,128]{2,1,0:T(8,128)S(1)}) custom-call(s32[1]{0:T(128)} %bitcast.1.base_ref, s32[1]{0:T(128)} %bitcast.5.core_ref.order_ref, s32[2]{0:T(128)S(1)} %pad_add_fusion.1.firsts_ref, f32[10280,128]{1,0:T(8,128)S(1)} %get-tuple-element.33.spec_ref, ...), custom_call_target="tpu_custom_call" | custom-call | flops 2147483648 | bytes 4194304 | tf_op jit(solution)/shard_map/rest/pallas_call | solution.py:233
  51.9 0.6 collective-permute-start.10
  52.4 0.0 collective-permute-done.7
  52.5 2.4 %collective-permute-start.8 = (f32[4,32,128]{2,1,0:T(8,128)S(1)}, f32[4,32,128]{2,1,0:T(8,128)S(1)}, u32[]{:S(2)}, u32[]{:S(2)}) collective-permute-start(f32[4,32,128]{2,1,0:T(8,128)S(1)} %get-tuple-element.51), channel_id=1, source_target_pairs={{0,24},{4,28},{8,16},{12,20},{16,8},{20,12},{24,0},{28,4},{1,25},{... | collective-permute-start | bytes 196616 | tf_op jit(solution)/shard_map/ppermute | solution.py:332
  54.9 6.4 %collective-permute-start.9 = (f32[4,32,128]{2,1,0:T(8,128)S(1)}, f32[4,32,128]{2,1,0:T(8,128)S(1)}, u32[]{:S(2)}, u32[]{:S(2)}) collective-permute-start(f32[4,32,128]{2,1,0:T(8,128)S(1)} %get-tuple-element.52), channel_id=1, source_target_pairs={{0,16},{4,20},{8,24},{12,28},{16,0},{20,4},{24,8},{28,12},{1,17},{... | collective-permute-start | bytes 196616 | tf_op jit(solution)/shard_map/ppermute | solution.py:332
  61.2 0.0 collective-permute-done.10
  61.3 0.6 collective-permute-start.11
  61.8 0.0 collective-permute-done.8
  61.8 3.8 %collective-permute-done.9 = f32[4,32,128]{2,1,0:T(8,128)S(1)} collective-permute-done((f32[4,32,128]{2,1,0:T(8,128)S(1)}, f32[4,32,128]{2,1,0:T(8,128)S(1)}, u32[]{:S(2)}, u32[]{:S(2)}) %collective-permute-start.9) | collective-permute-done | bytes 65568 | tf_op jit(solution)/shard_map/ppermute | solution.py:332
  65.7 0.4 collective-permute-done.11
  66.1 1.5 %collective-permute-start.14 = (f32[2,32,128]{2,1,0:T(8,128)S(1)}, f32[2,32,128]{2,1,0:T(8,128)S(1)}, u32[]{:S(2)}, u32[]{:S(2)}) collective-permute-start(f32[2,32,128]{2,1,0:T(8,128)S(1)} %broadcast_select_fusion), channel_id=1, source_target_pairs={{0,6},{1,7},{2,4},{3,5},{4,2},{5,3},{6,0},{7,1},{8,14},{9,15},{10,... | collective-permute-start | bytes 98312 | tf_op jit(solution)/shard_map/ppermute | solution.py:372
  67.6 1.5 %collective-permute-start.13 = (f32[2,32,128]{2,1,0:T(8,128)S(1)}, f32[2,32,128]{2,1,0:T(8,128)S(1)}, u32[]{:S(2)}, u32[]{:S(2)}) collective-permute-start(f32[2,32,128]{2,1,0:T(8,128)S(1)} %broadcast_select_fusion), channel_id=1, source_target_pairs={{0,4},{4,0},{8,12},{12,8},{16,20},{20,16},{24,28},{28,24},{1,5},{5... | collective-permute-start | bytes 98312 | tf_op jit(solution)/shard_map/ppermute | solution.py:332
  69.1 0.5 collective-permute-start.12
  69.7 1.4 %collective-permute-done.14 = f32[2,32,128]{2,1,0:T(8,128)S(1)} collective-permute-done((f32[2,32,128]{2,1,0:T(8,128)S(1)}, f32[2,32,128]{2,1,0:T(8,128)S(1)}, u32[]{:S(2)}, u32[]{:S(2)}) %collective-permute-start.14) | collective-permute-done | bytes 32800 | tf_op jit(solution)/shard_map/ppermute | solution.py:372
  71.0 0.5 collective-permute-done.13
  71.6 1.5 %collective-permute-done.12 = f32[2,32,128]{2,1,0:T(8,128)S(1)} collective-permute-done((f32[2,32,128]{2,1,0:T(8,128)S(1)}, f32[2,32,128]{2,1,0:T(8,128)S(1)}, u32[]{:S(2)}, u32[]{:S(2)}) %collective-permute-start.12) | collective-permute-done | bytes 32800 | tf_op jit(solution)/shard_map/ppermute | solution.py:332
  73.1 0.1 collective-permute-start.15
  73.2 0.9 %unpack.2 = (f32[2,16,32,32]{3,2,1,0:T(8,128)}, f32[128,128]{1,0:T(8,128)}) custom-call(s32[1]{0:T(128)} %bitcast.5.core_ref.order_ref, f32[2,32,128]{2,1,0:T(8,128)S(1)} %add_add_fusion.packed_ref, f32[128,128]{1,0:T(8,128)S(1)} %get-tuple-element.43.power_ref), custom_call_target="tpu_custom_call" | custom-call | tf_op jit(solution)/shard_map/unpack/pallas_call | solution.py:313
  74.0 0.3 collective-permute-done.15.packed_ref
  74.4 0.9 %unpack.3 = (f32[2,16,32,32]{3,2,1,0:T(8,128)}, f32[128,128]{1,0:T(8,128)}) custom-call(s32[1]{0:T(128)} %bitcast.order_ref, f32[2,32,128]{2,1,0:T(8,128)S(1)} %collective-permute-done.15.packed_ref, f32[128,128]{1,0:T(8,128)} %get-tuple-element.44.power_ref, f32[2,16,32,32]{3,2,1,0:T(8,128)} %get-tuple-element.45.refs_0_), custom_call_target="tpu_custom_call", output_to_operand_aliasing={{0}: (3, {}), {1}: (2, {})} | custom-call | tf_op jit(solution)/shard_map/unpack/pallas_call | solution.py:313
  (6 shorter events, 0.1 us)
Async XLA Ops:
  1.6 18.1 %collective-permute-start = (f32[528,128]{1,0:T(8,128)S(1)}, f32[528,128]{1,0:T(8,128)S(1)}, u32[]{:S(2)}, u32[]{:S(2)}) collective-permute-start(f32[528,128]{1,0:T(8,128)S(1)} %cut.2), channel_id=1, source_target_pairs={{0,16},{4,20},{8,24},{12,28},{16,0},{20,4},{24,8},{28,12},{1,17},{... | collective-permute-start | bytes 811016 | tf_op jit(solution)/shard_map/ppermute | solution.py:332
  5.7 1.6 %copy-start = (f32[528,1024]{1,0:T(8,128)S(1)}, f32[528,1024]{1,0:T(8,128)}, u32[]{:S(2)}) copy-start(f32[528,1024]{1,0:T(8,128)} %snapshots_ref.3) | copy-start | bytes 6488068
  7.3 6.6 %copy-start.2 = (s32[128]{0:T(128)S(1)}, s32[128]{0:T(128)}, u32[]{:S(2)}) copy-start(s32[128]{0:T(128)} %param.5) | copy-start | bytes 1540
  7.3 7.9 %copy-start.1 = (s32[32]{0:T(128)S(1)}, s32[32]{0:T(128)}, u32[]{:S(2)}) copy-start(s32[32]{0:T(128)} %starts_ref.3) | copy-start | bytes 388
  7.7 15.3 %collective-permute-start.1 = (f32[528,128]{1,0:T(8,128)S(1)}, f32[528,128]{1,0:T(8,128)S(1)}, u32[]{:S(2)}, u32[]{:S(2)}) collective-permute-start(f32[528,128]{1,0:T(8,128)S(1)} %get-tuple-element.25), channel_id=1, source_target_pairs={{0,8},{4,12},{8,0},{12,4},{16,24},{20,28},{24,16},{28,20},{1,9},{5... | collective-permute-start | bytes 811016 | tf_op jit(solution)/shard_map/ppermute | solution.py:332
  9.3 24.6 %collective-permute-start.2 = (f32[528,128]{1,0:T(8,128)S(1)}, f32[528,128]{1,0:T(8,128)S(1)}, u32[]{:S(2)}, u32[]{:S(2)}) collective-permute-start(f32[528,128]{1,0:T(8,128)S(1)} %get-tuple-element.26), channel_id=1, source_target_pairs={{0,4},{4,0},{8,12},{12,8},{16,20},{20,16},{24,28},{28,24},{1,5},{5... | collective-permute-start | bytes 811016 | tf_op jit(solution)/shard_map/ppermute | solution.py:332
  10.8 23.1 %collective-permute-start.3 = (f32[528,128]{1,0:T(8,128)S(1)}, f32[528,128]{1,0:T(8,128)S(1)}, u32[]{:S(2)}, u32[]{:S(2)}) collective-permute-start(f32[528,128]{1,0:T(8,128)S(1)} %get-tuple-element.27), channel_id=1, source_target_pairs={{0,20},{4,16},{8,28},{12,24},{16,4},{20,0},{24,12},{28,8},{1,21},{... | collective-permute-start | bytes 811016 | tf_op jit(solution)/shard_map/ppermute | solution.py:332
  11.1 33.3 %collective-permute-start.4 = (f32[528,128]{1,0:T(8,128)S(1)}, f32[528,128]{1,0:T(8,128)S(1)}, u32[]{:S(2)}, u32[]{:S(2)}) collective-permute-start(f32[528,128]{1,0:T(8,128)S(1)} %get-tuple-element.28), channel_id=1, source_target_pairs={{0,12},{4,8},{8,4},{12,0},{16,28},{20,24},{24,20},{28,16},{1,13},{... | collective-permute-start | bytes 811016 | tf_op jit(solution)/shard_map/ppermute | solution.py:332
  19.7 24.7 %collective-permute-start.5 = (f32[528,128]{1,0:T(8,128)S(1)}, f32[528,128]{1,0:T(8,128)S(1)}, u32[]{:S(2)}, u32[]{:S(2)}) collective-permute-start(f32[528,128]{1,0:T(8,128)S(1)} %get-tuple-element.29), channel_id=1, source_target_pairs={{0,24},{4,28},{8,16},{12,20},{16,8},{20,12},{24,0},{28,4},{1,25},{... | collective-permute-start | bytes 811016 | tf_op jit(solution)/shard_map/ppermute | solution.py:332
  22.9 24.8 %collective-permute-start.6 = (f32[528,128]{1,0:T(8,128)S(1)}, f32[528,128]{1,0:T(8,128)S(1)}, u32[]{:S(2)}, u32[]{:S(2)}) collective-permute-start(f32[528,128]{1,0:T(8,128)S(1)} %get-tuple-element.35), channel_id=1, source_target_pairs={{0,28},{4,24},{8,20},{12,16},{16,12},{20,8},{24,4},{28,0},{1,29},{... | collective-permute-start | bytes 811016 | tf_op jit(solution)/shard_map/ppermute | solution.py:332
  50.2 2.3 %collective-permute-start.7 = (f32[8,32,128]{2,1,0:T(8,128)S(1)}, f32[8,32,128]{2,1,0:T(8,128)S(1)}, u32[]{:S(2)}, u32[]{:S(2)}) collective-permute-start(f32[8,32,128]{2,1,0:T(8,128)S(1)} %get-tuple-element.37), channel_id=1, source_target_pairs={{0,1},{1,0},{2,3},{3,2},{4,5},{5,4},{6,7},{7,6},{8,9},{9,8},{10,11... | collective-permute-start | bytes 393224 | tf_op jit(solution)/shard_map/ppermute | solution.py:332
  51.9 9.4 %collective-permute-start.10 = (f32[8,32,128]{2,1,0:T(8,128)S(1)}, f32[8,32,128]{2,1,0:T(8,128)S(1)}, u32[]{:S(2)}, u32[]{:S(2)}) collective-permute-start(f32[8,32,128]{2,1,0:T(8,128)S(1)} %get-tuple-element.41), channel_id=1, source_target_pairs={{0,1},{1,0},{2,3},{3,2},{4,5},{5,4},{6,7},{7,6},{8,9},{9,8},{10,11... | collective-permute-start | bytes 393224 | tf_op jit(solution)/shard_map/ppermute | solution.py:332
  52.5 9.4 %collective-permute-start.8 = (f32[4,32,128]{2,1,0:T(8,128)S(1)}, f32[4,32,128]{2,1,0:T(8,128)S(1)}, u32[]{:S(2)}, u32[]{:S(2)}) collective-permute-start(f32[4,32,128]{2,1,0:T(8,128)S(1)} %get-tuple-element.51), channel_id=1, source_target_pairs={{0,24},{4,28},{8,16},{12,20},{16,8},{20,12},{24,0},{28,4},{1,25},{... | collective-permute-start | bytes 196616 | tf_op jit(solution)/shard_map/ppermute | solution.py:332
  54.9 10.8 %collective-permute-start.9 = (f32[4,32,128]{2,1,0:T(8,128)S(1)}, f32[4,32,128]{2,1,0:T(8,128)S(1)}, u32[]{:S(2)}, u32[]{:S(2)}) collective-permute-start(f32[4,32,128]{2,1,0:T(8,128)S(1)} %get-tuple-element.52), channel_id=1, source_target_pairs={{0,16},{4,20},{8,24},{12,28},{16,0},{20,4},{24,8},{28,12},{1,17},{... | collective-permute-start | bytes 196616 | tf_op jit(solution)/shard_map/ppermute | solution.py:332
  61.3 4.8 %collective-permute-start.11 = (f32[4,32,128]{2,1,0:T(8,128)S(1)}, f32[4,32,128]{2,1,0:T(8,128)S(1)}, u32[]{:S(2)}, u32[]{:S(2)}) collective-permute-start(f32[4,32,128]{2,1,0:T(8,128)S(1)} %get-tuple-element.53), channel_id=1, source_target_pairs={{0,8},{4,12},{8,0},{12,4},{16,24},{20,28},{24,16},{28,20},{1,9},{5... | collective-permute-start | bytes 196616 | tf_op jit(solution)/shard_map/ppermute | solution.py:332
  66.1 4.9 %collective-permute-start.14 = (f32[2,32,128]{2,1,0:T(8,128)S(1)}, f32[2,32,128]{2,1,0:T(8,128)S(1)}, u32[]{:S(2)}, u32[]{:S(2)}) collective-permute-start(f32[2,32,128]{2,1,0:T(8,128)S(1)} %broadcast_select_fusion), channel_id=1, source_target_pairs={{0,6},{1,7},{2,4},{3,5},{4,2},{5,3},{6,0},{7,1},{8,14},{9,15},{10,... | collective-permute-start | bytes 98312 | tf_op jit(solution)/shard_map/ppermute | solution.py:372
  67.6 3.9 %collective-permute-start.13 = (f32[2,32,128]{2,1,0:T(8,128)S(1)}, f32[2,32,128]{2,1,0:T(8,128)S(1)}, u32[]{:S(2)}, u32[]{:S(2)}) collective-permute-start(f32[2,32,128]{2,1,0:T(8,128)S(1)} %broadcast_select_fusion), channel_id=1, source_target_pairs={{0,4},{4,0},{8,12},{12,8},{16,20},{20,16},{24,28},{28,24},{1,5},{5... | collective-permute-start | bytes 98312 | tf_op jit(solution)/shard_map/ppermute | solution.py:332
  69.1 3.9 %collective-permute-start.12 = (f32[2,32,128]{2,1,0:T(8,128)S(1)}, f32[2,32,128]{2,1,0:T(8,128)S(1)}, u32[]{:S(2)}, u32[]{:S(2)}) collective-permute-start(f32[2,32,128]{2,1,0:T(8,128)S(1)} %get-tuple-element.48), channel_id=1, source_target_pairs={{0,2},{1,3},{2,0},{3,1},{4,6},{5,7},{6,4},{7,5},{8,10},{9,11},{10,... | collective-permute-start | bytes 98312 | tf_op jit(solution)/shard_map/ppermute | solution.py:332
  73.1 1.3 %collective-permute-start.15 = (f32[2,32,128]{2,1,0:T(8,128)S(1)}, f32[2,32,128]{2,1,0:T(8,128)S(1)}, u32[]{:S(2)}, u32[]{:S(2)}) collective-permute-start(f32[2,32,128]{2,1,0:T(8,128)S(1)} %add_add_fusion.packed_ref), channel_id=1, source_target_pairs={{0,1},{1,0},{2,3},{3,2},{4,5},{5,4},{6,7},{7,6},{8,9},{9,8},{10,11... | collective-permute-start | bytes 98312 | tf_op jit(solution)/shard_map/ppermute | solution.py:332

commit v8 on v7

--- a/solution.py
+++ b/solution.py
@@ -167,7 +167,7 @@
     )(base, corner, where, starts, table, *pieces)
 
 
-def packed_quarters(base, core, firsts_ref, spec_ref, late_spec, sent_ref, kept_refs):
+def packed_quarters(base, core, firsts_ref, spec_ref, late_spec, place):
     block = lax.broadcasted_iota(jnp.int32, (NB, LANES), 0)
     is_late = (block >= base) & (block < base + LATE)
 
@@ -176,19 +176,17 @@
             is_late, line_rows(late_spec, part, line), line_rows(spec_ref, part, line)
         )
 
-    half = kept_refs[0].shape[0]
-    for n, kept_ref in enumerate(kept_refs):
-        for i in range(half):
+    quarters = firsts_ref.shape[0]
+    for n in range(quarters):
+        for i in range(NF // PACK // quarters // 2):
             group = firsts_ref[n] + (i // CORE_STEP) * 2 * CORE_STEP + i % CORE_STEP
-            kept_ref[i] = gram(rows_of, (group + core * CORE_STEP) * PACK)
-            sent_ref[n * half + i] = gram(rows_of, (group + (1 - core) * CORE_STEP) * PACK)
+            place(n, i, gram(rows_of, (group + core * CORE_STEP) * PACK))
 
 
 def late_kernel(
     base_ref, corner_ref, where_ref, core_ref, firsts_ref, starts_ref,
-    halves, window_ref, spec_ref, early_power_ref, piece_ref, power_ref, late_spec, sent_ref, *refs,
+    halves, window_ref, spec_ref, early_power_ref, piece_ref, power_ref, late_spec, sent_ref, series,
 ):
-    kept_refs, series = refs[:-1], refs[-1]
     rows, base = piece_ref.shape[0], base_ref[0]
     origin = corner_ref[0] - rows
     series[pl.ds(rows, WINDOW), :] = window_ref[...]
@@ -199,28 +197,30 @@
         blocks = [series[pl.ds(starts_ref[b] - origin, NFFT), :] for b in numbers]
         power = power + transform(halves, blocks, numbers, late_spec)
     power_ref[...] = power
-    packed_quarters(base, core_ref[0], firsts_ref, spec_ref, late_spec, sent_ref, kept_refs)
-
-
-def rest_kernel(base_ref, core_ref, firsts_ref, spec_ref, late_spec, sent_ref, *kept_refs):
-    packed_quarters(base_ref[0], core_ref[0], firsts_ref, spec_ref, late_spec, sent_ref, kept_refs)
-
-
-def quarter_shapes(quarters):
-    half = NF // PACK // 4 // 2
-    return [jax.ShapeDtypeStruct((n * half, NB, LANES), F32) for n in (quarters, *[1] * quarters)]
+    half = sent_ref.shape[0] // firsts_ref.shape[0]
+
+    def place(n, i, matrices):
+        sent_ref[n * half + i] = matrices
+
+    packed_quarters(base, 1 - core_ref[0], firsts_ref, spec_ref, late_spec, place)
+
+
+def rest_kernel(base_ref, core_ref, firsts_ref, spec_ref, late_spec, *kept_refs):
+    def place(n, i, matrices):
+        kept_refs[n][i] = matrices
+
+    packed_quarters(base_ref[0], core_ref[0], firsts_ref, spec_ref, late_spec, place)
 
 
 def late(base, corner, where, core, firsts, starts, halves, window, spec, power, piece):
-    quarters = firsts.shape[0]
     smem, vmem = pl.BlockSpec(memory_space=SMEM), pl.BlockSpec(memory_space=VMEM)
     return pl.pallas_call(
         late_kernel,
         name="late",
         in_specs=[smem] * 6 + [vmem] * 5,
-        out_specs=[vmem] * (3 + quarters),
+        out_specs=[vmem] * 3,
         out_shape=[jax.ShapeDtypeStruct(a.shape, F32) for a in (power, spec)]
-        + quarter_shapes(quarters),
+        + [jax.ShapeDtypeStruct((NF // PACK // 2, NB, LANES), F32)],
         scratch_shapes=[VMEM((2 * piece.shape[0] + WINDOW, LANES), F32)],
         compiler_params=pltpu.CompilerParams(vmem_limit_bytes=20 << 20),
         cost_estimate=pl.CostEstimate(flops=3 << 30, bytes_accessed=8 << 20, transcendentals=0),
@@ -234,8 +234,8 @@
         rest_kernel,
         name="rest",
         in_specs=[smem] * 3 + [vmem] * 2,
-        out_specs=[vmem] * (1 + quarters),
-        out_shape=quarter_shapes(quarters),
+        out_specs=[vmem] * quarters,
+        out_shape=[jax.ShapeDtypeStruct((NF // PACK // quarters // 2, NB, LANES), F32)] * quarters,
         compiler_params=pltpu.CompilerParams(vmem_limit_bytes=20 << 20),
         cost_estimate=pl.CostEstimate(flops=2 << 30, bytes_accessed=4 << 20, transcendentals=0),
     )(base, core, firsts, spec, late_spec)
@@ -354,16 +354,14 @@
     away = (3, 2, 1)
     firsts = jnp.stack([(z ^ j) * groups for j in (*away, 0)])
     core_number = core.reshape(1)
-    power, late_spec, sent, *kept = late(
-        base, corner, late_part.reshape(1), core_number, firsts[:2], starts,
+    power, late_spec, sent = late(
+        base, corner, late_part.reshape(1), core_number, firsts, starts,
         halves, window, spec, power, last,
     )
-    sent_rest, *kept_rest = rest(base, core_number, firsts[2:], spec, late_spec)
+    kept = rest(base, core_number, firsts, spec, late_spec)
     half = groups // 2
-    terms = []
-    for sent, kept in ((sent, kept), (sent_rest, kept_rest)):
-        theirs = swap(sent, "space", 1)
-        terms += [k + theirs[n * half : (n + 1) * half] for n, k in enumerate(kept)]
+    theirs = swap(sent, "space", 1)
+    terms = [k + theirs[n * half : (n + 1) * half] for n, k in enumerate(kept)]
     terms = [swap(t, "tm", 2 * j) for j, t in zip(away, terms)] + terms[-1:]
     lower, upper = (sum(t[i * half // 2 : (i + 1) * half // 2] for t in terms) for i in range(2))
     mine, other = jnp.where(x == 0, lower, upper), jnp.where(x == 0, upper, lower)

time: 75.5 us -> 76.7 us (1.016)
  waiting for transfers between devices: 22.4 us -> 24.2 us
    ppermute x15 -> x14, waiting for transfers between devices: 21.1 us -> 22.9 us  [swap(): lax.ppermute(value, axis, [(i, i ^ bits) for i in range(lax.axis_size(axi...]
    ppermute x15 -> x14, starting transfers between devices: 29.9 us -> 29.3 us  [swap(): lax.ppermute(value, axis, [(i, i ^ bits) for i in range(lax.axis_size(axi...]
  transfers between devices with their start and end apart: 16 -> 15, of which waited for: 8 -> 8; matrix products, arithmetic and copies ran while one was open for 6% -> 6% of each run, Pallas kernels for 8% -> 8%
where the time goes in v8:
time: 76.7 us; the launch traced here: 76.4 us
  starting transfers between devices  30.8 us (40%)
  waiting for transfers between devices  24.2 us (32%)
  Pallas kernels  10.4 us (14%)
  between operations  4.85 us (6%)
  other arithmetic  3.76 us (5%)
  local copies, waits for them, and re-layouts  2.37 us (3%)
    ppermute x14, starting transfers between devices, swap(): lax.ppermute(value, axis, [(i, i ^ bits) for i in range(lax.axis_size(axi...  29.3 us
    ppermute x14, waiting for transfers between devices, swap(): lax.ppermute(value, axis, [(i, i ^ bits) for i in range(lax.axis_size(axi...  22.9 us
    pallas_call x1, Pallas kernels, early(): pl.pallas_call(functools.partial(early_kernel, rows), name='early', in_sp...  3.33 us
    pallas_call x1, Pallas kernels, late(): pl.pallas_call(late_kernel, name='late', in_specs=[smem] * 6 + [vmem] * 5...  2.38 us
    pallas_call x2, Pallas kernels, unpack(): pl.pallas_call(functools.partial(unpack_kernel, factor), name='unpack', i...  1.74 us
    pallas_call x1, Pallas kernels, rest(): pl.pallas_call(rest_kernel, name='rest', in_specs=[smem] * 3 + [vmem] * 2...  1.62 us
    unnamed x6, local copies, waits for them, and re-layouts  1.62 us
    ppermute x1, starting transfers between devices, spread_small(): lax.ppermute(other, ('tm', 'space'), [(i * 4 + s, (i ^ 1) * 4 + (s ^ 2))...  1.55 us
  transfers between devices with their start and end apart: 15, of which 8 were waited for; matrix products, arithmetic and copies ran while one was open for 6% of the time, Pallas kernels for 8%

profile of v8, /device:TPU:0, one launch (start us, length us, event | category | flops | bytes accessed | tf_op | source)
XLA Modules:
  0.0 76.4 jit_solution(17848590192556851736)
XLA Ops:
  0.6 1.0 %cut.2 = f32[528,128]{1,0:T(8,128)S(1)} custom-call(f32[528,1024]{1,0:T(8,128)} %snapshots_ref.3), custom_call_target="tpu_custom_call" | custom-call | flops 1073741824 | bytes 1048576 | tf_op jit(solution)/shard_map/cut/pallas_call | solution.py:116
  1.6 4.1 %collective-permute-start = (f32[528,128]{1,0:T(8,128)S(1)}, f32[528,128]{1,0:T(8,128)S(1)}, u32[]{:S(2)}, u32[]{:S(2)}) collective-permute-start(f32[528,128]{1,0:T(8,128)S(1)} %cut.2), channel_id=1, source_target_pairs={{0,16},{4,20},{8,24},{12,28},{16,0},{20,4},{24,8},{28,12},{1,17},{... | collective-permute-start | bytes 811016 | tf_op jit(solution)/shard_map/ppermute | solution.py:332
  5.7 0.0 copy-start
  5.7 1.6 %copy-done = f32[528,1024]{1,0:T(8,128)S(1)} copy-done((f32[528,1024]{1,0:T(8,128)S(1)}, f32[528,1024]{1,0:T(8,128)}, u32[]{:S(2)}) %copy-start) | copy-done | bytes 2162712
  7.3 0.0 copy-start.2
  7.3 0.0 copy-start.1
  7.3 0.3 cut.3
  7.7 1.6 %collective-permute-start.1 = (f32[528,128]{1,0:T(8,128)S(1)}, f32[528,128]{1,0:T(8,128)S(1)}, u32[]{:S(2)}, u32[]{:S(2)}) collective-permute-start(f32[528,128]{1,0:T(8,128)S(1)} %get-tuple-element.24), channel_id=1, source_target_pairs={{0,8},{4,12},{8,0},{12,4},{16,24},{20,28},{24,16},{28,20},{1,9},{5... | collective-permute-start | bytes 811016 | tf_op jit(solution)/shard_map/ppermute | solution.py:332
  9.3 1.5 %collective-permute-start.2 = (f32[528,128]{1,0:T(8,128)S(1)}, f32[528,128]{1,0:T(8,128)S(1)}, u32[]{:S(2)}, u32[]{:S(2)}) collective-permute-start(f32[528,128]{1,0:T(8,128)S(1)} %get-tuple-element.25), channel_id=1, source_target_pairs={{0,4},{4,0},{8,12},{12,8},{16,20},{20,16},{24,28},{28,24},{1,5},{5... | collective-permute-start | bytes 811016 | tf_op jit(solution)/shard_map/ppermute | solution.py:332
  10.8 0.3 collective-permute-start.3
  11.1 1.4 %collective-permute-start.4 = (f32[528,128]{1,0:T(8,128)S(1)}, f32[528,128]{1,0:T(8,128)S(1)}, u32[]{:S(2)}, u32[]{:S(2)}) collective-permute-start(f32[528,128]{1,0:T(8,128)S(1)} %get-tuple-element.27), channel_id=1, source_target_pairs={{0,12},{4,8},{8,4},{12,0},{16,28},{20,24},{24,20},{28,16},{1,13},{... | collective-permute-start | bytes 811016 | tf_op jit(solution)/shard_map/ppermute | solution.py:332
  12.5 0.6 multiply_reduce_fusion
  13.9 0.0 copy-done.2
  13.9 1.3 %cosine_multiply_fusion = (f32[128,256]{1,0:T(8,128)}, f32[128,256]{1,0:T(8,128)}) fusion(s32[128]{0:T(128)S(1)} %copy-done.2, f32[256]{0:T(256)S(1)} %get-tuple-element.55, f32[256]{0:T(256)S(1)} %get-tuple-element.56), kind=kLoop, calls=%fused_computation.8 | loop fusion | flops 524288 | bytes 264704 | tf_op jit(solution)/shard_map/mul | solution.py:34
  15.2 4.5 %collective-permute-done.refs_0_ = f32[528,128]{1,0:T(8,128)S(1)} collective-permute-done((f32[528,128]{1,0:T(8,128)S(1)}, f32[528,128]{1,0:T(8,128)S(1)}, u32[]{:S(2)}, u32[]{:S(2)}) %collective-permute-start) | collective-permute-done | bytes 270368 | tf_op jit(solution)/shard_map/ppermute | solution.py:332
  19.7 3.1 %collective-permute-start.5 = (f32[528,128]{1,0:T(8,128)S(1)}, f32[528,128]{1,0:T(8,128)S(1)}, u32[]{:S(2)}, u32[]{:S(2)}) collective-permute-start(f32[528,128]{1,0:T(8,128)S(1)} %get-tuple-element.28), channel_id=1, source_target_pairs={{0,24},{4,28},{8,16},{12,20},{16,8},{20,12},{24,0},{28,4},{1,25},{... | collective-permute-start | bytes 811016 | tf_op jit(solution)/shard_map/ppermute | solution.py:332
  22.8 0.0 copy-done.1
  22.8 0.6 fusion.7
  23.4 0.0 collective-permute-done.1.refs_1_
  23.5 5.9 %collective-permute-start.6 = (f32[528,128]{1,0:T(8,128)S(1)}, f32[528,128]{1,0:T(8,128)S(1)}, u32[]{:S(2)}, u32[]{:S(2)}) collective-permute-start(f32[528,128]{1,0:T(8,128)S(1)} %get-tuple-element.34), channel_id=1, source_target_pairs={{0,28},{4,24},{8,20},{12,16},{16,12},{20,8},{24,4},{28,0},{1,29},{... | collective-permute-start | bytes 811016 | tf_op jit(solution)/shard_map/ppermute | solution.py:332
  29.3 0.1 pad_add_fusion.firsts_ref
  30.0 0.7 dynamic_slice.3
  33.5 0.1 stack.51.where_ref
  33.6 1.0 %pad_maximum_fusion.table_ref = f32[256,256]{1,0:T(8,128)S(1)} fusion(f32[128,256]{1,0:T(8,128)} %get-tuple-element.54, f32[128,256]{1,0:T(8,128)} %get-tuple-element.53), kind=kLoop, calls=%fused_computation | loop fusion | flops 65536 | bytes 524288 | tf_op jit(solution)/shard_map/concatenate | solution.py:33
  34.5 0.0 collective-permute-done.2.refs_2_
  34.6 0.0 collective-permute-done.3.refs_3_
  34.6 9.9 %collective-permute-done.4.refs_4_ = f32[528,128]{1,0:T(8,128)S(1)} collective-permute-done((f32[528,128]{1,0:T(8,128)S(1)}, f32[528,128]{1,0:T(8,128)S(1)}, u32[]{:S(2)}, u32[]{:S(2)}) %collective-permute-start.4) | collective-permute-done | bytes 270368 | tf_op jit(solution)/shard_map/ppermute | solution.py:332
  44.5 0.0 collective-permute-done.5.refs_5_
  44.5 3.3 %early.1 = (f32[1288,128]{1,0:T(8,128)S(1)}, f32[10280,128]{1,0:T(8,128)S(1)}, f32[128,128]{1,0:T(8,128)S(1)}, bf16[512,256]{1,0:T(8,128)(2,1)S(1)}) custom-call(s32[1]{0:T(128)} %bitcast.1.base_ref, s32[1]{0:T(128)} %bitcast.8.corner_ref, s32[7]{0:T(128)S(1)} %stack.51.where_ref, s32[32]{0:T(128)S(1)} %copy-done.1, ...), custom_call_target="tpu_custom_call" | custom-call | flops 1207959552 | bytes 4194304 | tf_op jit(solution)/shard_map/early/pallas_call | solution.py:151
  47.8 0.0 collective-permute-done.6.piece_ref
  47.8 2.4 %late.1 = (f32[128,128]{1,0:T(8,128)S(1)}, f32[10280,128]{1,0:T(8,128)S(1)}, f32[16,32,128]{2,1,0:T(8,128)S(1)}) custom-call(s32[1]{0:T(128)} %bitcast.1.base_ref, s32[1]{0:T(128)} %bitcast.8.corner_ref, s32[1]{0:T(128)} %bitcast.16.where_ref, s32[1]{0:T(128)} %bitcast.2.core_ref.order_ref, s32[4]{0:T(128)S(1)} %pad_add_fusion.firsts_ref, s32[32]{0:T(128)S(1)} %copy-done.1, ...), custom_call_target="tpu_custom_call" | custom-call | flops 3221225472 | bytes 8388608 | tf_op jit(solution)/shard_map/late/pallas_call | solution.py:217
  50.2 0.1 collective-permute-start.7
  50.3 1.6 %rest.1 = (f32[4,32,128]{2,1,0:T(8,128)S(1)}, f32[4,32,128]{2,1,0:T(8,128)S(1)}, f32[4,32,128]{2,1,0:T(8,128)S(1)}, f32[4,32,128]{2,1,0:T(8,128)S(1)}) custom-call(s32[1]{0:T(128)} %bitcast.1.base_ref, s32[1]{0:T(128)} %bitcast.2.core_ref.order_ref, s32[4]{0:T(128)S(1)} %pad_add_fusion.firsts_ref, f32[10280,128]{1,0:T(8,128)S(1)} %get-tuple-element.30.spec_ref, ...), custom_call_target="tpu_custom_call" | custom-call | flops 2147483648 | bytes 4194304 | tf_op jit(solution)/shard_map/rest/pallas_call | solution.py:233
  51.9 0.0 collective-permute-done.7
  52.0 2.4 %collective-permute-start.8 = (f32[4,32,128]{2,1,0:T(8,128)S(1)}, f32[4,32,128]{2,1,0:T(8,128)S(1)}, u32[]{:S(2)}, u32[]{:S(2)}) collective-permute-start(f32[4,32,128]{2,1,0:T(8,128)S(1)} %get-tuple-element.49), channel_id=1, source_target_pairs={{0,24},{4,28},{8,16},{12,20},{16,8},{20,12},{24,0},{28,4},{1,25},{... | collective-permute-start | bytes 196616 | tf_op jit(solution)/shard_map/ppermute | solution.py:332
  54.4 6.8 %collective-permute-start.10 = (f32[4,32,128]{2,1,0:T(8,128)S(1)}, f32[4,32,128]{2,1,0:T(8,128)S(1)}, u32[]{:S(2)}, u32[]{:S(2)}) collective-permute-start(f32[4,32,128]{2,1,0:T(8,128)S(1)} %get-tuple-element.51), channel_id=1, source_target_pairs={{0,8},{4,12},{8,0},{12,4},{16,24},{20,28},{24,16},{28,20},{1,9},{5... | collective-permute-start | bytes 196616 | tf_op jit(solution)/shard_map/ppermute | solution.py:332
  61.2 0.0 collective-permute-start.9
  61.2 0.0 collective-permute-done.8
  61.2 2.5 %collective-permute-done.10 = f32[4,32,128]{2,1,0:T(8,128)S(1)} collective-permute-done((f32[4,32,128]{2,1,0:T(8,128)S(1)}, f32[4,32,128]{2,1,0:T(8,128)S(1)}, u32[]{:S(2)}, u32[]{:S(2)}) %collective-permute-start.10) | collective-permute-done | bytes 65568 | tf_op jit(solution)/shard_map/ppermute | solution.py:332
  63.7 3.6 %collective-permute-done.9 = f32[4,32,128]{2,1,0:T(8,128)S(1)} collective-permute-done((f32[4,32,128]{2,1,0:T(8,128)S(1)}, f32[4,32,128]{2,1,0:T(8,128)S(1)}, u32[]{:S(2)}, u32[]{:S(2)}) %collective-permute-start.9) | collective-permute-done | bytes 65568 | tf_op jit(solution)/shard_map/ppermute | solution.py:332
  67.3 1.5 %collective-permute-start.13 = (f32[2,32,128]{2,1,0:T(8,128)S(1)}, f32[2,32,128]{2,1,0:T(8,128)S(1)}, u32[]{:S(2)}, u32[]{:S(2)}) collective-permute-start(f32[2,32,128]{2,1,0:T(8,128)S(1)} %broadcast_select_fusion), channel_id=1, source_target_pairs={{0,6},{1,7},{2,4},{3,5},{4,2},{5,3},{6,0},{7,1},{8,14},{9,15},{10,... | collective-permute-start | bytes 98312 | tf_op jit(solution)/shard_map/ppermute | solution.py:370
  68.8 1.5 %collective-permute-start.12 = (f32[2,32,128]{2,1,0:T(8,128)S(1)}, f32[2,32,128]{2,1,0:T(8,128)S(1)}, u32[]{:S(2)}, u32[]{:S(2)}) collective-permute-start(f32[2,32,128]{2,1,0:T(8,128)S(1)} %broadcast_select_fusion), channel_id=1, source_target_pairs={{0,4},{4,0},{8,12},{12,8},{16,20},{20,16},{24,28},{28,24},{1,5},{5... | collective-permute-start | bytes 98312 | tf_op jit(solution)/shard_map/ppermute | solution.py:332
  70.3 0.5 collective-permute-start.11
  70.8 1.3 %collective-permute-done.13 = f32[2,32,128]{2,1,0:T(8,128)S(1)} collective-permute-done((f32[2,32,128]{2,1,0:T(8,128)S(1)}, f32[2,32,128]{2,1,0:T(8,128)S(1)}, u32[]{:S(2)}, u32[]{:S(2)}) %collective-permute-start.13) | collective-permute-done | bytes 32800 | tf_op jit(solution)/shard_map/ppermute | solution.py:370
  72.2 0.6 collective-permute-done.12
  72.8 1.5 %collective-permute-done.11 = f32[2,32,128]{2,1,0:T(8,128)S(1)} collective-permute-done((f32[2,32,128]{2,1,0:T(8,128)S(1)}, f32[2,32,128]{2,1,0:T(8,128)S(1)}, u32[]{:S(2)}, u32[]{:S(2)}) %collective-permute-start.11) | collective-permute-done | bytes 32800 | tf_op jit(solution)/shard_map/ppermute | solution.py:332
  74.3 0.1 collective-permute-start.14
  74.3 0.9 %unpack.2 = (f32[2,16,32,32]{3,2,1,0:T(8,128)}, f32[128,128]{1,0:T(8,128)}) custom-call(s32[1]{0:T(128)} %bitcast.2.core_ref.order_ref, f32[2,32,128]{2,1,0:T(8,128)S(1)} %add_add_fusion.packed_ref, f32[128,128]{1,0:T(8,128)S(1)} %get-tuple-element.41.power_ref), custom_call_target="tpu_custom_call" | custom-call | tf_op jit(solution)/shard_map/unpack/pallas_call | solution.py:313
  75.2 0.3 collective-permute-done.14.packed_ref
  75.5 0.9 %unpack.3 = (f32[2,16,32,32]{3,2,1,0:T(8,128)}, f32[128,128]{1,0:T(8,128)}) custom-call(s32[1]{0:T(128)} %bitcast.order_ref, f32[2,32,128]{2,1,0:T(8,128)S(1)} %collective-permute-done.14.packed_ref, f32[128,128]{1,0:T(8,128)} %get-tuple-element.42.power_ref, f32[2,16,32,32]{3,2,1,0:T(8,128)} %get-tuple-element.43.refs_0_), custom_call_target="tpu_custom_call", output_to_operand_aliasing={{0}: (3, {}), {1}: (2, {})} | custom-call | tf_op jit(solution)/shard_map/unpack/pallas_call | solution.py:313
  (5 shorter events, 0.1 us)
Async XLA Ops:
  1.6 18.1 %collective-permute-start = (f32[528,128]{1,0:T(8,128)S(1)}, f32[528,128]{1,0:T(8,128)S(1)}, u32[]{:S(2)}, u32[]{:S(2)}) collective-permute-start(f32[528,128]{1,0:T(8,128)S(1)} %cut.2), channel_id=1, source_target_pairs={{0,16},{4,20},{8,24},{12,28},{16,0},{20,4},{24,8},{28,12},{1,17},{... | collective-permute-start | bytes 811016 | tf_op jit(solution)/shard_map/ppermute | solution.py:332
  5.7 1.6 %copy-start = (f32[528,1024]{1,0:T(8,128)S(1)}, f32[528,1024]{1,0:T(8,128)}, u32[]{:S(2)}) copy-start(f32[528,1024]{1,0:T(8,128)} %snapshots_ref.3) | copy-start | bytes 6488068
  7.3 6.6 %copy-start.2 = (s32[128]{0:T(128)S(1)}, s32[128]{0:T(128)}, u32[]{:S(2)}) copy-start(s32[128]{0:T(128)} %param.5) | copy-start | bytes 1540
  7.3 15.5 %copy-start.1 = (s32[32]{0:T(128)S(1)}, s32[32]{0:T(128)}, u32[]{:S(2)}) copy-start(s32[32]{0:T(128)} %starts_ref.3) | copy-start | bytes 388
  7.7 15.8 %collective-permute-start.1 = (f32[528,128]{1,0:T(8,128)S(1)}, f32[528,128]{1,0:T(8,128)S(1)}, u32[]{:S(2)}, u32[]{:S(2)}) collective-permute-start(f32[528,128]{1,0:T(8,128)S(1)} %get-tuple-element.24), channel_id=1, source_target_pairs={{0,8},{4,12},{8,0},{12,4},{16,24},{20,28},{24,16},{28,20},{1,9},{5... | collective-permute-start | bytes 811016 | tf_op jit(solution)/shard_map/ppermute | solution.py:332
  9.3 25.2 %collective-permute-start.2 = (f32[528,128]{1,0:T(8,128)S(1)}, f32[528,128]{1,0:T(8,128)S(1)}, u32[]{:S(2)}, u32[]{:S(2)}) collective-permute-start(f32[528,128]{1,0:T(8,128)S(1)} %get-tuple-element.25), channel_id=1, source_target_pairs={{0,4},{4,0},{8,12},{12,8},{16,20},{20,16},{24,28},{28,24},{1,5},{5... | collective-permute-start | bytes 811016 | tf_op jit(solution)/shard_map/ppermute | solution.py:332
  10.8 23.7 %collective-permute-start.3 = (f32[528,128]{1,0:T(8,128)S(1)}, f32[528,128]{1,0:T(8,128)S(1)}, u32[]{:S(2)}, u32[]{:S(2)}) collective-permute-start(f32[528,128]{1,0:T(8,128)S(1)} %get-tuple-element.26), channel_id=1, source_target_pairs={{0,20},{4,16},{8,28},{12,24},{16,4},{20,0},{24,12},{28,8},{1,21},{... | collective-permute-start | bytes 811016 | tf_op jit(solution)/shard_map/ppermute | solution.py:332
  11.1 33.3 %collective-permute-start.4 = (f32[528,128]{1,0:T(8,128)S(1)}, f32[528,128]{1,0:T(8,128)S(1)}, u32[]{:S(2)}, u32[]{:S(2)}) collective-permute-start(f32[528,128]{1,0:T(8,128)S(1)} %get-tuple-element.27), channel_id=1, source_target_pairs={{0,12},{4,8},{8,4},{12,0},{16,28},{20,24},{24,20},{28,16},{1,13},{... | collective-permute-start | bytes 811016 | tf_op jit(solution)/shard_map/ppermute | solution.py:332
  19.7 24.7 %collective-permute-start.5 = (f32[528,128]{1,0:T(8,128)S(1)}, f32[528,128]{1,0:T(8,128)S(1)}, u32[]{:S(2)}, u32[]{:S(2)}) collective-permute-start(f32[528,128]{1,0:T(8,128)S(1)} %get-tuple-element.28), channel_id=1, source_target_pairs={{0,24},{4,28},{8,16},{12,20},{16,8},{20,12},{24,0},{28,4},{1,25},{... | collective-permute-start | bytes 811016 | tf_op jit(solution)/shard_map/ppermute | solution.py:332
  23.5 24.4 %collective-permute-start.6 = (f32[528,128]{1,0:T(8,128)S(1)}, f32[528,128]{1,0:T(8,128)S(1)}, u32[]{:S(2)}, u32[]{:S(2)}) collective-permute-start(f32[528,128]{1,0:T(8,128)S(1)} %get-tuple-element.34), channel_id=1, source_target_pairs={{0,28},{4,24},{8,20},{12,16},{16,12},{20,8},{24,4},{28,0},{1,29},{... | collective-permute-start | bytes 811016 | tf_op jit(solution)/shard_map/ppermute | solution.py:332
  50.2 1.7 %collective-permute-start.7 = (f32[16,32,128]{2,1,0:T(8,128)S(1)}, f32[16,32,128]{2,1,0:T(8,128)S(1)}, u32[]{:S(2)}, u32[]{:S(2)}) collective-permute-start(f32[16,32,128]{2,1,0:T(8,128)S(1)} %get-tuple-element.37), channel_id=1, source_target_pairs={{0,1},{1,0},{2,3},{3,2},{4,5},{5,4},{6,7},{7,6},{8,9},{9,8},{10,11... | collective-permute-start | bytes 786440 | tf_op jit(solution)/shard_map/ppermute | solution.py:332
  52.0 9.2 %collective-permute-start.8 = (f32[4,32,128]{2,1,0:T(8,128)S(1)}, f32[4,32,128]{2,1,0:T(8,128)S(1)}, u32[]{:S(2)}, u32[]{:S(2)}) collective-permute-start(f32[4,32,128]{2,1,0:T(8,128)S(1)} %get-tuple-element.49), channel_id=1, source_target_pairs={{0,24},{4,28},{8,16},{12,20},{16,8},{20,12},{24,0},{28,4},{1,25},{... | collective-permute-start | bytes 196616 | tf_op jit(solution)/shard_map/ppermute | solution.py:332
  54.4 9.3 %collective-permute-start.10 = (f32[4,32,128]{2,1,0:T(8,128)S(1)}, f32[4,32,128]{2,1,0:T(8,128)S(1)}, u32[]{:S(2)}, u32[]{:S(2)}) collective-permute-start(f32[4,32,128]{2,1,0:T(8,128)S(1)} %get-tuple-element.51), channel_id=1, source_target_pairs={{0,8},{4,12},{8,0},{12,4},{16,24},{20,28},{24,16},{28,20},{1,9},{5... | collective-permute-start | bytes 196616 | tf_op jit(solution)/shard_map/ppermute | solution.py:332
  61.2 6.1 %collective-permute-start.9 = (f32[4,32,128]{2,1,0:T(8,128)S(1)}, f32[4,32,128]{2,1,0:T(8,128)S(1)}, u32[]{:S(2)}, u32[]{:S(2)}) collective-permute-start(f32[4,32,128]{2,1,0:T(8,128)S(1)} %get-tuple-element.52), channel_id=1, source_target_pairs={{0,16},{4,20},{8,24},{12,28},{16,0},{20,4},{24,8},{28,12},{1,17},{... | collective-permute-start | bytes 196616 | tf_op jit(solution)/shard_map/ppermute | solution.py:332
  67.3 4.9 %collective-permute-start.13 = (f32[2,32,128]{2,1,0:T(8,128)S(1)}, f32[2,32,128]{2,1,0:T(8,128)S(1)}, u32[]{:S(2)}, u32[]{:S(2)}) collective-permute-start(f32[2,32,128]{2,1,0:T(8,128)S(1)} %broadcast_select_fusion), channel_id=1, source_target_pairs={{0,6},{1,7},{2,4},{3,5},{4,2},{5,3},{6,0},{7,1},{8,14},{9,15},{10,... | collective-permute-start | bytes 98312 | tf_op jit(solution)/shard_map/ppermute | solution.py:370
  68.8 3.9 %collective-permute-start.12 = (f32[2,32,128]{2,1,0:T(8,128)S(1)}, f32[2,32,128]{2,1,0:T(8,128)S(1)}, u32[]{:S(2)}, u32[]{:S(2)}) collective-permute-start(f32[2,32,128]{2,1,0:T(8,128)S(1)} %broadcast_select_fusion), channel_id=1, source_target_pairs={{0,4},{4,0},{8,12},{12,8},{16,20},{20,16},{24,28},{28,24},{1,5},{5... | collective-permute-start | bytes 98312 | tf_op jit(solution)/shard_map/ppermute | solution.py:332
  70.3 3.9 %collective-permute-start.11 = (f32[2,32,128]{2,1,0:T(8,128)S(1)}, f32[2,32,128]{2,1,0:T(8,128)S(1)}, u32[]{:S(2)}, u32[]{:S(2)}) collective-permute-start(f32[2,32,128]{2,1,0:T(8,128)S(1)} %get-tuple-element.46), channel_id=1, source_target_pairs={{0,2},{1,3},{2,0},{3,1},{4,6},{5,7},{6,4},{7,5},{8,10},{9,11},{10,... | collective-permute-start | bytes 98312 | tf_op jit(solution)/shard_map/ppermute | solution.py:332
  74.3 1.3 %collective-permute-start.14 = (f32[2,32,128]{2,1,0:T(8,128)S(1)}, f32[2,32,128]{2,1,0:T(8,128)S(1)}, u32[]{:S(2)}, u32[]{:S(2)}) collective-permute-start(f32[2,32,128]{2,1,0:T(8,128)S(1)} %add_add_fusion.packed_ref), channel_id=1, source_target_pairs={{0,1},{1,0},{2,3},{3,2},{4,5},{5,4},{6,7},{7,6},{8,9},{9,8},{10,11... | collective-permute-start | bytes 98312 | tf_op jit(solution)/shard_map/ppermute | solution.py:332

commit v9 on v8

--- a/solution.py
+++ b/solution.py
@@ -351,7 +351,7 @@
     base = base.reshape(1)
     window, spec, power, halves = early(base, corner, where, starts, table, pieces)
     groups = NF // PACK // 4
-    away = (3, 2, 1)
+    away = (3, 1, 2)
     firsts = jnp.stack([(z ^ j) * groups for j in (*away, 0)])
     core_number = core.reshape(1)
     power, late_spec, sent = late(

time: 76.7 us -> 75.6 us (0.986)
  waiting for transfers between devices: 24.2 us -> 23.1 us
    ppermute x14, waiting for transfers between devices: 22.9 us -> 21.8 us  [swap(): lax.ppermute(value, axis, [(i, i ^ bits) for i in range(lax.axis_size(axi...]
where the time goes in v9:
time: 75.6 us; the launch traced here: 75.3 us
  starting transfers between devices  30.8 us (41%)
  waiting for transfers between devices  23.1 us (31%)
  Pallas kernels  10.4 us (14%)
  between operations  4.85 us (6%)
  other arithmetic  3.76 us (5%)
  local copies, waits for them, and re-layouts  2.37 us (3%)
    ppermute x14, starting transfers between devices, swap(): lax.ppermute(value, axis, [(i, i ^ bits) for i in range(lax.axis_size(axi...  29.2 us
    ppermute x14, waiting for transfers between devices, swap(): lax.ppermute(value, axis, [(i, i ^ bits) for i in range(lax.axis_size(axi...  21.8 us
    pallas_call x1, Pallas kernels, early(): pl.pallas_call(functools.partial(early_kernel, rows), name='early', in_sp...  3.32 us
    pallas_call x1, Pallas kernels, late(): pl.pallas_call(late_kernel, name='late', in_specs=[smem] * 6 + [vmem] * 5...  2.37 us
    pallas_call x2, Pallas kernels, unpack(): pl.pallas_call(functools.partial(unpack_kernel, factor), name='unpack', i...  1.74 us
    pallas_call x1, Pallas kernels, rest(): pl.pallas_call(rest_kernel, name='rest', in_specs=[smem] * 3 + [vmem] * 2...  1.63 us
    unnamed x6, local copies, waits for them, and re-layouts  1.62 us
    ppermute x1, starting transfers between devices, spread_small(): lax.ppermute(other, ('tm', 'space'), [(i * 4 + s, (i ^ 1) * 4 + (s ^ 2))...  1.57 us
  transfers between devices with their start and end apart: 15, of which 8 were waited for; matrix products, arithmetic and copies ran while one was open for 6% of the time, Pallas kernels for 8%

profile of v9, /device:TPU:0, one launch (start us, length us, event | category | flops | bytes accessed | tf_op | source)
XLA Modules:
  0.0 75.3 jit_solution(7760738026744082252)
XLA Ops:
  0.6 1.0 %cut.2 = f32[528,128]{1,0:T(8,128)S(1)} custom-call(f32[528,1024]{1,0:T(8,128)} %snapshots_ref.3), custom_call_target="tpu_custom_call" | custom-call | flops 1073741824 | bytes 1048576 | tf_op jit(solution)/shard_map/cut/pallas_call | solution.py:116
  1.6 4.1 %collective-permute-start = (f32[528,128]{1,0:T(8,128)S(1)}, f32[528,128]{1,0:T(8,128)S(1)}, u32[]{:S(2)}, u32[]{:S(2)}) collective-permute-start(f32[528,128]{1,0:T(8,128)S(1)} %cut.2), channel_id=1, source_target_pairs={{0,16},{4,20},{8,24},{12,28},{16,0},{20,4},{24,8},{28,12},{1,17},{... | collective-permute-start | bytes 811016 | tf_op jit(solution)/shard_map/ppermute | solution.py:332
  5.7 0.0 copy-start
  5.7 1.6 %copy-done = f32[528,1024]{1,0:T(8,128)S(1)} copy-done((f32[528,1024]{1,0:T(8,128)S(1)}, f32[528,1024]{1,0:T(8,128)}, u32[]{:S(2)}) %copy-start) | copy-done | bytes 2162712
  7.3 0.0 copy-start.2
  7.3 0.0 copy-start.1
  7.3 0.3 cut.3
  7.7 1.6 %collective-permute-start.1 = (f32[528,128]{1,0:T(8,128)S(1)}, f32[528,128]{1,0:T(8,128)S(1)}, u32[]{:S(2)}, u32[]{:S(2)}) collective-permute-start(f32[528,128]{1,0:T(8,128)S(1)} %get-tuple-element.24), channel_id=1, source_target_pairs={{0,8},{4,12},{8,0},{12,4},{16,24},{20,28},{24,16},{28,20},{1,9},{5... | collective-permute-start | bytes 811016 | tf_op jit(solution)/shard_map/ppermute | solution.py:332
  9.3 1.5 %collective-permute-start.2 = (f32[528,128]{1,0:T(8,128)S(1)}, f32[528,128]{1,0:T(8,128)S(1)}, u32[]{:S(2)}, u32[]{:S(2)}) collective-permute-start(f32[528,128]{1,0:T(8,128)S(1)} %get-tuple-element.25), channel_id=1, source_target_pairs={{0,4},{4,0},{8,12},{12,8},{16,20},{20,16},{24,28},{28,24},{1,5},{5... | collective-permute-start | bytes 811016 | tf_op jit(solution)/shard_map/ppermute | solution.py:332
  10.8 0.3 collective-permute-start.3
  11.1 1.4 %collective-permute-start.4 = (f32[528,128]{1,0:T(8,128)S(1)}, f32[528,128]{1,0:T(8,128)S(1)}, u32[]{:S(2)}, u32[]{:S(2)}) collective-permute-start(f32[528,128]{1,0:T(8,128)S(1)} %get-tuple-element.27), channel_id=1, source_target_pairs={{0,12},{4,8},{8,4},{12,0},{16,28},{20,24},{24,20},{28,16},{1,13},{... | collective-permute-start | bytes 811016 | tf_op jit(solution)/shard_map/ppermute | solution.py:332
  12.5 0.6 multiply_reduce_fusion
  13.9 0.0 copy-done.2
  13.9 1.3 %cosine_multiply_fusion = (f32[128,256]{1,0:T(8,128)}, f32[128,256]{1,0:T(8,128)}) fusion(s32[128]{0:T(128)S(1)} %copy-done.2, f32[256]{0:T(256)S(1)} %get-tuple-element.55, f32[256]{0:T(256)S(1)} %get-tuple-element.56), kind=kLoop, calls=%fused_computation.8 | loop fusion | flops 524288 | bytes 264704 | tf_op jit(solution)/shard_map/mul | solution.py:34
  15.2 4.5 %collective-permute-done.refs_0_ = f32[528,128]{1,0:T(8,128)S(1)} collective-permute-done((f32[528,128]{1,0:T(8,128)S(1)}, f32[528,128]{1,0:T(8,128)S(1)}, u32[]{:S(2)}, u32[]{:S(2)}) %collective-permute-start) | collective-permute-done | bytes 270368 | tf_op jit(solution)/shard_map/ppermute | solution.py:332
  19.7 3.1 %collective-permute-start.5 = (f32[528,128]{1,0:T(8,128)S(1)}, f32[528,128]{1,0:T(8,128)S(1)}, u32[]{:S(2)}, u32[]{:S(2)}) collective-permute-start(f32[528,128]{1,0:T(8,128)S(1)} %get-tuple-element.28), channel_id=1, source_target_pairs={{0,24},{4,28},{8,16},{12,20},{16,8},{20,12},{24,0},{28,4},{1,25},{... | collective-permute-start | bytes 811016 | tf_op jit(solution)/shard_map/ppermute | solution.py:332
  22.8 0.0 copy-done.1
  22.8 0.6 fusion.7
  23.4 0.0 collective-permute-done.1.refs_1_
  23.5 5.9 %collective-permute-start.6 = (f32[528,128]{1,0:T(8,128)S(1)}, f32[528,128]{1,0:T(8,128)S(1)}, u32[]{:S(2)}, u32[]{:S(2)}) collective-permute-start(f32[528,128]{1,0:T(8,128)S(1)} %get-tuple-element.34), channel_id=1, source_target_pairs={{0,28},{4,24},{8,20},{12,16},{16,12},{20,8},{24,4},{28,0},{1,29},{... | collective-permute-start | bytes 811016 | tf_op jit(solution)/shard_map/ppermute | solution.py:332
  29.3 0.1 pad_add_fusion.firsts_ref
  30.0 0.7 dynamic_slice.3
  33.5 0.1 stack.51.where_ref
  33.6 1.0 %pad_maximum_fusion.table_ref = f32[256,256]{1,0:T(8,128)S(1)} fusion(f32[128,256]{1,0:T(8,128)} %get-tuple-element.54, f32[128,256]{1,0:T(8,128)} %get-tuple-element.53), kind=kLoop, calls=%fused_computation | loop fusion | flops 65536 | bytes 524288 | tf_op jit(solution)/shard_map/concatenate | solution.py:33
  34.5 0.0 collective-permute-done.2.refs_2_
  34.6 0.0 collective-permute-done.3.refs_3_
  34.6 9.9 %collective-permute-done.4.refs_4_ = f32[528,128]{1,0:T(8,128)S(1)} collective-permute-done((f32[528,128]{1,0:T(8,128)S(1)}, f32[528,128]{1,0:T(8,128)S(1)}, u32[]{:S(2)}, u32[]{:S(2)}) %collective-permute-start.4) | collective-permute-done | bytes 270368 | tf_op jit(solution)/shard_map/ppermute | solution.py:332
  44.5 0.0 collective-permute-done.5.refs_5_
  44.5 3.3 %early.1 = (f32[1288,128]{1,0:T(8,128)S(1)}, f32[10280,128]{1,0:T(8,128)S(1)}, f32[128,128]{1,0:T(8,128)S(1)}, bf16[512,256]{1,0:T(8,128)(2,1)S(1)}) custom-call(s32[1]{0:T(128)} %bitcast.1.base_ref, s32[1]{0:T(128)} %bitcast.8.corner_ref, s32[7]{0:T(128)S(1)} %stack.51.where_ref, s32[32]{0:T(128)S(1)} %copy-done.1, ...), custom_call_target="tpu_custom_call" | custom-call | flops 1207959552 | bytes 4194304 | tf_op jit(solution)/shard_map/early/pallas_call | solution.py:151
  47.8 0.0 collective-permute-done.6.piece_ref
  47.8 2.4 %late.1 = (f32[128,128]{1,0:T(8,128)S(1)}, f32[10280,128]{1,0:T(8,128)S(1)}, f32[16,32,128]{2,1,0:T(8,128)S(1)}) custom-call(s32[1]{0:T(128)} %bitcast.1.base_ref, s32[1]{0:T(128)} %bitcast.8.corner_ref, s32[1]{0:T(128)} %bitcast.16.where_ref, s32[1]{0:T(128)} %bitcast.2.core_ref.order_ref, s32[4]{0:T(128)S(1)} %pad_add_fusion.firsts_ref, s32[32]{0:T(128)S(1)} %copy-done.1, ...), custom_call_target="tpu_custom_call" | custom-call | flops 3221225472 | bytes 8388608 | tf_op jit(solution)/shard_map/late/pallas_call | solution.py:217
  50.2 0.1 collective-permute-start.7
  50.3 1.6 %rest.1 = (f32[4,32,128]{2,1,0:T(8,128)S(1)}, f32[4,32,128]{2,1,0:T(8,128)S(1)}, f32[4,32,128]{2,1,0:T(8,128)S(1)}, f32[4,32,128]{2,1,0:T(8,128)S(1)}) custom-call(s32[1]{0:T(128)} %bitcast.1.base_ref, s32[1]{0:T(128)} %bitcast.2.core_ref.order_ref, s32[4]{0:T(128)S(1)} %pad_add_fusion.firsts_ref, f32[10280,128]{1,0:T(8,128)S(1)} %get-tuple-element.30.spec_ref, ...), custom_call_target="tpu_custom_call" | custom-call | flops 2147483648 | bytes 4194304 | tf_op jit(solution)/shard_map/rest/pallas_call | solution.py:233
  51.9 0.0 collective-permute-done.7
  52.0 2.4 %collective-permute-start.8 = (f32[4,32,128]{2,1,0:T(8,128)S(1)}, f32[4,32,128]{2,1,0:T(8,128)S(1)}, u32[]{:S(2)}, u32[]{:S(2)}) collective-permute-start(f32[4,32,128]{2,1,0:T(8,128)S(1)} %get-tuple-element.49), channel_id=1, source_target_pairs={{0,24},{4,28},{8,16},{12,20},{16,8},{20,12},{24,0},{28,4},{1,25},{... | collective-permute-start | bytes 196616 | tf_op jit(solution)/shard_map/ppermute | solution.py:332
  54.4 6.3 %collective-permute-start.10 = (f32[4,32,128]{2,1,0:T(8,128)S(1)}, f32[4,32,128]{2,1,0:T(8,128)S(1)}, u32[]{:S(2)}, u32[]{:S(2)}) collective-permute-start(f32[4,32,128]{2,1,0:T(8,128)S(1)} %get-tuple-element.51), channel_id=1, source_target_pairs={{0,16},{4,20},{8,24},{12,28},{16,0},{20,4},{24,8},{28,12},{1,17},{... | collective-permute-start | bytes 196616 | tf_op jit(solution)/shard_map/ppermute | solution.py:332
  60.7 0.5 collective-permute-start.9
  61.2 0.0 collective-permute-done.8
  61.2 4.7 %collective-permute-done.10 = f32[4,32,128]{2,1,0:T(8,128)S(1)} collective-permute-done((f32[4,32,128]{2,1,0:T(8,128)S(1)}, f32[4,32,128]{2,1,0:T(8,128)S(1)}, u32[]{:S(2)}, u32[]{:S(2)}) %collective-permute-start.10) | collective-permute-done | bytes 65568 | tf_op jit(solution)/shard_map/ppermute | solution.py:332
  65.9 0.2 collective-permute-done.9
  66.2 1.6 %collective-permute-start.13 = (f32[2,32,128]{2,1,0:T(8,128)S(1)}, f32[2,32,128]{2,1,0:T(8,128)S(1)}, u32[]{:S(2)}, u32[]{:S(2)}) collective-permute-start(f32[2,32,128]{2,1,0:T(8,128)S(1)} %broadcast_select_fusion), channel_id=1, source_target_pairs={{0,6},{1,7},{2,4},{3,5},{4,2},{5,3},{6,0},{7,1},{8,14},{9,15},{10,... | collective-permute-start | bytes 98312 | tf_op jit(solution)/shard_map/ppermute | solution.py:370
  67.7 1.5 %collective-permute-start.12 = (f32[2,32,128]{2,1,0:T(8,128)S(1)}, f32[2,32,128]{2,1,0:T(8,128)S(1)}, u32[]{:S(2)}, u32[]{:S(2)}) collective-permute-start(f32[2,32,128]{2,1,0:T(8,128)S(1)} %broadcast_select_fusion), channel_id=1, source_target_pairs={{0,4},{4,0},{8,12},{12,8},{16,20},{20,16},{24,28},{28,24},{1,5},{5... | collective-permute-start | bytes 98312 | tf_op jit(solution)/shard_map/ppermute | solution.py:332
  69.2 0.5 collective-permute-start.11
  69.7 1.3 %collective-permute-done.13 = f32[2,32,128]{2,1,0:T(8,128)S(1)} collective-permute-done((f32[2,32,128]{2,1,0:T(8,128)S(1)}, f32[2,32,128]{2,1,0:T(8,128)S(1)}, u32[]{:S(2)}, u32[]{:S(2)}) %collective-permute-start.13) | collective-permute-done | bytes 32800 | tf_op jit(solution)/shard_map/ppermute | solution.py:370
  71.1 0.6 collective-permute-done.12
  71.7 1.5 %collective-permute-done.11 = f32[2,32,128]{2,1,0:T(8,128)S(1)} collective-permute-done((f32[2,32,128]{2,1,0:T(8,128)S(1)}, f32[2,32,128]{2,1,0:T(8,128)S(1)}, u32[]{:S(2)}, u32[]{:S(2)}) %collective-permute-start.11) | collective-permute-done | bytes 32800 | tf_op jit(solution)/shard_map/ppermute | solution.py:332
  73.1 0.1 collective-permute-start.14
  73.2 0.9 %unpack.2 = (f32[2,16,32,32]{3,2,1,0:T(8,128)}, f32[128,128]{1,0:T(8,128)}) custom-call(s32[1]{0:T(128)} %bitcast.2.core_ref.order_ref, f32[2,32,128]{2,1,0:T(8,128)S(1)} %add_add_fusion.packed_ref, f32[128,128]{1,0:T(8,128)S(1)} %get-tuple-element.41.power_ref), custom_call_target="tpu_custom_call" | custom-call | tf_op jit(solution)/shard_map/unpack/pallas_call | solution.py:313
  74.1 0.3 collective-permute-done.14.packed_ref
  74.4 0.9 %unpack.3 = (f32[2,16,32,32]{3,2,1,0:T(8,128)}, f32[128,128]{1,0:T(8,128)}) custom-call(s32[1]{0:T(128)} %bitcast.order_ref, f32[2,32,128]{2,1,0:T(8,128)S(1)} %collective-permute-done.14.packed_ref, f32[128,128]{1,0:T(8,128)} %get-tuple-element.42.power_ref, f32[2,16,32,32]{3,2,1,0:T(8,128)} %get-tuple-element.43.refs_0_), custom_call_target="tpu_custom_call", output_to_operand_aliasing={{0}: (3, {}), {1}: (2, {})} | custom-call | tf_op jit(solution)/shard_map/unpack/pallas_call | solution.py:313
  (5 shorter events, 0.1 us)
Async XLA Ops:
  1.6 18.1 %collective-permute-start = (f32[528,128]{1,0:T(8,128)S(1)}, f32[528,128]{1,0:T(8,128)S(1)}, u32[]{:S(2)}, u32[]{:S(2)}) collective-permute-start(f32[528,128]{1,0:T(8,128)S(1)} %cut.2), channel_id=1, source_target_pairs={{0,16},{4,20},{8,24},{12,28},{16,0},{20,4},{24,8},{28,12},{1,17},{... | collective-permute-start | bytes 811016 | tf_op jit(solution)/shard_map/ppermute | solution.py:332
  5.7 1.6 %copy-start = (f32[528,1024]{1,0:T(8,128)S(1)}, f32[528,1024]{1,0:T(8,128)}, u32[]{:S(2)}) copy-start(f32[528,1024]{1,0:T(8,128)} %snapshots_ref.3) | copy-start | bytes 6488068
  7.3 6.6 %copy-start.2 = (s32[128]{0:T(128)S(1)}, s32[128]{0:T(128)}, u32[]{:S(2)}) copy-start(s32[128]{0:T(128)} %param.5) | copy-start | bytes 1540
  7.3 15.5 %copy-start.1 = (s32[32]{0:T(128)S(1)}, s32[32]{0:T(128)}, u32[]{:S(2)}) copy-start(s32[32]{0:T(128)} %starts_ref.3) | copy-start | bytes 388
  7.7 15.8 %collective-permute-start.1 = (f32[528,128]{1,0:T(8,128)S(1)}, f32[528,128]{1,0:T(8,128)S(1)}, u32[]{:S(2)}, u32[]{:S(2)}) collective-permute-start(f32[528,128]{1,0:T(8,128)S(1)} %get-tuple-element.24), channel_id=1, source_target_pairs={{0,8},{4,12},{8,0},{12,4},{16,24},{20,28},{24,16},{28,20},{1,9},{5... | collective-permute-start | bytes 811016 | tf_op jit(solution)/shard_map/ppermute | solution.py:332
  9.3 25.2 %collective-permute-start.2 = (f32[528,128]{1,0:T(8,128)S(1)}, f32[528,128]{1,0:T(8,128)S(1)}, u32[]{:S(2)}, u32[]{:S(2)}) collective-permute-start(f32[528,128]{1,0:T(8,128)S(1)} %get-tuple-element.25), channel_id=1, source_target_pairs={{0,4},{4,0},{8,12},{12,8},{16,20},{20,16},{24,28},{28,24},{1,5},{5... | collective-permute-start | bytes 811016 | tf_op jit(solution)/shard_map/ppermute | solution.py:332
  10.8 23.7 %collective-permute-start.3 = (f32[528,128]{1,0:T(8,128)S(1)}, f32[528,128]{1,0:T(8,128)S(1)}, u32[]{:S(2)}, u32[]{:S(2)}) collective-permute-start(f32[528,128]{1,0:T(8,128)S(1)} %get-tuple-element.26), channel_id=1, source_target_pairs={{0,20},{4,16},{8,28},{12,24},{16,4},{20,0},{24,12},{28,8},{1,21},{... | collective-permute-start | bytes 811016 | tf_op jit(solution)/shard_map/ppermute | solution.py:332
  11.1 33.3 %collective-permute-start.4 = (f32[528,128]{1,0:T(8,128)S(1)}, f32[528,128]{1,0:T(8,128)S(1)}, u32[]{:S(2)}, u32[]{:S(2)}) collective-permute-start(f32[528,128]{1,0:T(8,128)S(1)} %get-tuple-element.27), channel_id=1, source_target_pairs={{0,12},{4,8},{8,4},{12,0},{16,28},{20,24},{24,20},{28,16},{1,13},{... | collective-permute-start | bytes 811016 | tf_op jit(solution)/shard_map/ppermute | solution.py:332
  19.7 24.7 %collective-permute-start.5 = (f32[528,128]{1,0:T(8,128)S(1)}, f32[528,128]{1,0:T(8,128)S(1)}, u32[]{:S(2)}, u32[]{:S(2)}) collective-permute-start(f32[528,128]{1,0:T(8,128)S(1)} %get-tuple-element.28), channel_id=1, source_target_pairs={{0,24},{4,28},{8,16},{12,20},{16,8},{20,12},{24,0},{28,4},{1,25},{... | collective-permute-start | bytes 811016 | tf_op jit(solution)/shard_map/ppermute | solution.py:332
  23.5 24.3 %collective-permute-start.6 = (f32[528,128]{1,0:T(8,128)S(1)}, f32[528,128]{1,0:T(8,128)S(1)}, u32[]{:S(2)}, u32[]{:S(2)}) collective-permute-start(f32[528,128]{1,0:T(8,128)S(1)} %get-tuple-element.34), channel_id=1, source_target_pairs={{0,28},{4,24},{8,20},{12,16},{16,12},{20,8},{24,4},{28,0},{1,29},{... | collective-permute-start | bytes 811016 | tf_op jit(solution)/shard_map/ppermute | solution.py:332
  50.2 1.7 %collective-permute-start.7 = (f32[16,32,128]{2,1,0:T(8,128)S(1)}, f32[16,32,128]{2,1,0:T(8,128)S(1)}, u32[]{:S(2)}, u32[]{:S(2)}) collective-permute-start(f32[16,32,128]{2,1,0:T(8,128)S(1)} %get-tuple-element.37), channel_id=1, source_target_pairs={{0,1},{1,0},{2,3},{3,2},{4,5},{5,4},{6,7},{7,6},{8,9},{9,8},{10,11... | collective-permute-start | bytes 786440 | tf_op jit(solution)/shard_map/ppermute | solution.py:332
  52.0 9.2 %collective-permute-start.8 = (f32[4,32,128]{2,1,0:T(8,128)S(1)}, f32[4,32,128]{2,1,0:T(8,128)S(1)}, u32[]{:S(2)}, u32[]{:S(2)}) collective-permute-start(f32[4,32,128]{2,1,0:T(8,128)S(1)} %get-tuple-element.49), channel_id=1, source_target_pairs={{0,24},{4,28},{8,16},{12,20},{16,8},{20,12},{24,0},{28,4},{1,25},{... | collective-permute-start | bytes 196616 | tf_op jit(solution)/shard_map/ppermute | solution.py:332
  54.4 11.5 %collective-permute-start.10 = (f32[4,32,128]{2,1,0:T(8,128)S(1)}, f32[4,32,128]{2,1,0:T(8,128)S(1)}, u32[]{:S(2)}, u32[]{:S(2)}) collective-permute-start(f32[4,32,128]{2,1,0:T(8,128)S(1)} %get-tuple-element.51), channel_id=1, source_target_pairs={{0,16},{4,20},{8,24},{12,28},{16,0},{20,4},{24,8},{28,12},{1,17},{... | collective-permute-start | bytes 196616 | tf_op jit(solution)/shard_map/ppermute | solution.py:332
  60.7 5.5 %collective-permute-start.9 = (f32[4,32,128]{2,1,0:T(8,128)S(1)}, f32[4,32,128]{2,1,0:T(8,128)S(1)}, u32[]{:S(2)}, u32[]{:S(2)}) collective-permute-start(f32[4,32,128]{2,1,0:T(8,128)S(1)} %get-tuple-element.52), channel_id=1, source_target_pairs={{0,8},{4,12},{8,0},{12,4},{16,24},{20,28},{24,16},{28,20},{1,9},{5... | collective-permute-start | bytes 196616 | tf_op jit(solution)/shard_map/ppermute | solution.py:332
  66.2 4.9 %collective-permute-start.13 = (f32[2,32,128]{2,1,0:T(8,128)S(1)}, f32[2,32,128]{2,1,0:T(8,128)S(1)}, u32[]{:S(2)}, u32[]{:S(2)}) collective-permute-start(f32[2,32,128]{2,1,0:T(8,128)S(1)} %broadcast_select_fusion), channel_id=1, source_target_pairs={{0,6},{1,7},{2,4},{3,5},{4,2},{5,3},{6,0},{7,1},{8,14},{9,15},{10,... | collective-permute-start | bytes 98312 | tf_op jit(solution)/shard_map/ppermute | solution.py:370
  67.7 3.9 %collective-permute-start.12 = (f32[2,32,128]{2,1,0:T(8,128)S(1)}, f32[2,32,128]{2,1,0:T(8,128)S(1)}, u32[]{:S(2)}, u32[]{:S(2)}) collective-permute-start(f32[2,32,128]{2,1,0:T(8,128)S(1)} %broadcast_select_fusion), channel_id=1, source_target_pairs={{0,4},{4,0},{8,12},{12,8},{16,20},{20,16},{24,28},{28,24},{1,5},{5... | collective-permute-start | bytes 98312 | tf_op jit(solution)/shard_map/ppermute | solution.py:332
  69.2 3.9 %collective-permute-start.11 = (f32[2,32,128]{2,1,0:T(8,128)S(1)}, f32[2,32,128]{2,1,0:T(8,128)S(1)}, u32[]{:S(2)}, u32[]{:S(2)}) collective-permute-start(f32[2,32,128]{2,1,0:T(8,128)S(1)} %get-tuple-element.46), channel_id=1, source_target_pairs={{0,2},{1,3},{2,0},{3,1},{4,6},{5,7},{6,4},{7,5},{8,10},{9,11},{10,... | collective-permute-start | bytes 98312 | tf_op jit(solution)/shard_map/ppermute | solution.py:332
  73.1 1.3 %collective-permute-start.14 = (f32[2,32,128]{2,1,0:T(8,128)S(1)}, f32[2,32,128]{2,1,0:T(8,128)S(1)}, u32[]{:S(2)}, u32[]{:S(2)}) collective-permute-start(f32[2,32,128]{2,1,0:T(8,128)S(1)} %add_add_fusion.packed_ref), channel_id=1, source_target_pairs={{0,1},{1,0},{2,3},{3,2},{4,5},{5,4},{6,7},{7,6},{8,9},{9,8},{10,11... | collective-permute-start | bytes 98312 | tf_op jit(solution)/shard_map/ppermute | solution.py:332
